TPU v7x, 32 devices: a whole 2x2x4 slice. The times are simulated.
32 devices in a mesh: groups: 2 (over y), expert: 4 (over z), replica: 4 (over x, core).
Axes of the slice: x: 2, y: 2, z: 4, core: 2. Of those that a mesh axis runs over, the one named last changes fastest.
Arguments:
- tokens: bfloat16 [4096, 1024], P(('groups', 'expert', 'replica')), parts along dimension 0, may hold values from -6 to 6
- expert_ids: int32 [4096, 6], P(('groups', 'expert', 'replica')), parts along dimension 0, may hold values from 0 to 15, all different within a row; in each aligned block of 128 rows (0 to 127, 128 to 255, ...) at most 64 rows name the same one
- gate_probs: bfloat16 [4096, 6], P(('groups', 'expert', 'replica')), parts along dimension 0, may hold values from 0.099609375 to 0.59765625
- cotangent: bfloat16 [4096, 1024], P(('groups', 'expert', 'replica')), parts along dimension 0, may hold values from -1.5 to 1.5
- gate_up: bfloat16 [1024, 16, 1536], P(None, 'expert'), may hold values from -0.1875 to 0.1875
- down_weights: bfloat16 [768, 16, 1024], P(None, 'expert'), may hold values from -0.21875 to 0.21875
Outputs:
- combined: bfloat16 [4096, 1024], P(('groups', 'expert', 'replica')), parts along dimension 0
- token_gradient: bfloat16 [4096, 1024], P(('groups', 'expert', 'replica')), parts along dimension 0
- prob_gradient: float32 [4096, 6], P(('groups', 'expert', 'replica')), parts along dimension 0
- gate_up_gradient: float32 [2048, 16, 1536], P(('groups', 'replica'), 'expert'), parts along dimension 0
- down_gradient: float32 [1536, 16, 1024], P(('groups', 'replica'), 'expert'), parts along dimension 0
There are 2 independent parts, one for each index of `groups`. A program takes and returns all parts, laid end to end along the dimension named above; an argument that names none is the same for every part. Nothing has to cross between parts.
Inputs may be any that keep to these rules, and one draw needn't show every extreme that they name: `expert_ids`: each row names 6 different experts. Within the rows of one device (aligned blocks of 128 rows) no expert is named by more than 64 rows, and in some block one expert is named by exactly 64 rows.
All inputs are finite; a program needn't handle non-finite values.
Results may differ from a plain program's by a relative error of at most 0.0064.
Values may be sent and summed in bfloat16 or wider, within the bound.
A program may use at most 128 MiB of HBM per device.

v0:
```python
import jax
import jax.numpy as jnp
from jax import lax
from jax.experimental.layout import Layout, with_layout_constraint
from jax.sharding import PartitionSpec as P


CAP = 64
CORES = 2
BF = jnp.bfloat16
F32 = jnp.float32


def on_device(tokens, expert_ids, gate_probs, cotangent, gate_up, down_weights, *, sources, replicas):
    count, width = tokens.shape
    top = expert_ids.shape[1]
    local = gate_up.shape[1]
    hidden_width = down_weights.shape[0]
    cap = min(CAP, count)
    along = replicas // CORES
    replica = lax.axis_index("replica")
    core, place = lax.rem(replica, CORES), lax.div(replica, CORES)
    first = lax.axis_index("expert") * local
    slots = sources * cap

    def to_source(values, shift):
        step = [(i, (i + shift) % sources) for i in range(sources)]
        return lax.ppermute(values, "expert", step) if shift else values

    def to_chip(values, shift):
        step = [
            (x * CORES + c, ((x + shift) % along) * CORES + c)
            for x in range(along) for c in range(CORES)
        ]
        return lax.ppermute(values, "replica", step)

    notes = jnp.concatenate([expert_ids.T.astype(BF), gate_probs.T], axis=0)
    flat = notes.reshape(-1)
    extra = -(-flat.shape[0] // (16 * width)) * 16
    flat = jnp.pad(flat, (0, extra * width - flat.shape[0])).reshape(extra, width)
    packed = jnp.concatenate([tokens, flat], axis=0)

    def gathered(values):
        others = [[to_chip(values, t)] for t in range(1, along)]
        held = [to_source(values, s) for s in range(sources)]
        if sources <= 4:
            pieces = [[h] for h in held[1:]]
        else:
            pieces = [held[1:]]
        for piece in pieces:
            sent = piece[0] if len(piece) == 1 else jnp.stack(piece)
            for t in range(1, along):
                got = to_chip(sent, t)
                others[t - 1] += [got] if len(piece) == 1 else [got[i] for i in range(len(piece))]
        return [held] + others

    all_packed = gathered(packed)
    all_cots = gathered(cotangent)

    gate_rows = lax.optimization_barrier(
        with_layout_constraint(gate_up.swapaxes(0, 1), Layout((0, 1, 2)))
    )
    down_rows = lax.optimization_barrier(
        with_layout_constraint(down_weights.swapaxes(0, 1), Layout((0, 1, 2)))
    )

    ahead = (jnp.arange(count)[:, None] < jnp.arange(count)[None, :]).astype(BF)
    same = jnp.arange(sources)[:, None] == jnp.arange(sources)[None, :]

    def routing(held):
        all_notes = jnp.stack([h[count:].reshape(-1)[:notes.size].reshape(notes.shape) for h in held])
        all_ids = all_notes[:, :top].astype(jnp.int32)
        all_probs = all_notes[:, top:]
        named = (all_ids[None] == (first + jnp.arange(local, dtype=jnp.int32))[:, None, None, None])
        member = jnp.any(named, axis=2)
        weight = jnp.sum(jnp.where(named, all_probs[None].astype(F32), 0.0), axis=2)
        rank = jnp.einsum("esp,pq->esq", member.astype(BF), ahead, preferred_element_type=F32)
        rank = jnp.where(member, rank.astype(jnp.int32), -1)
        chosen = rank[:, :, None, :] == jnp.arange(cap, dtype=jnp.int32)[None, None, :, None]
        wide = chosen[:, :, :, None, :] & same[None, :, None, :, None]
        pick = wide.astype(BF).reshape(local * slots, sources * count)
        slot_weight = jnp.sum(jnp.where(chosen, weight[:, :, None, :], 0.0), axis=3).reshape(local, slots, 1)
        return weight, chosen, wide, pick, slot_weight

    def rows(pick, values):
        return jnp.dot(pick, values, preferred_element_type=F32).astype(BF).reshape(local, slots, width)

    def forward(held):
        weight, chosen, wide, pick, slot_weight = routing(held)
        inputs = rows(pick, jnp.concatenate([h[:count] for h in held], axis=0))
        pre_act = jnp.einsum("erd,edf->erf", inputs, gate_rows, preferred_element_type=F32)
        gate, up = pre_act[..., :hidden_width], pre_act[..., hidden_width:]
        sig = jax.nn.sigmoid(gate)
        hidden = (gate * sig * up).astype(BF)
        return (weight, chosen, wide, pick, slot_weight), inputs, gate, up, sig, hidden

    def backward(route, held, gate, up, sig):
        _, _, _, pick, slot_weight = route
        raw_cot = rows(pick, jnp.concatenate(held, axis=0))
        out_grad = (slot_weight * raw_cot.astype(F32)).astype(BF)
        hidden_grad = jnp.einsum("erd,efd->erf", out_grad, down_rows, preferred_element_type=F32)
        pre_grad = jnp.concatenate(
            [hidden_grad * up * sig * (1.0 + gate * (1.0 - sig)), hidden_grad * gate * sig], axis=-1
        ).astype(BF)
        return raw_cot, out_grad, pre_grad

    def returned(matrix, values):
        parts = jnp.einsum(
            "ra,rd->ad", matrix, values.reshape(local * slots, width), preferred_element_type=F32
        ).astype(BF).reshape(sources, count, width)
        arrived = [to_source(parts[s], -s).astype(F32) for s in range(sources)]
        return sum(arrived[1:], arrived[0]).astype(BF)

    route, inputs, gate, up, sig, hidden = forward(all_packed[0])
    weight, chosen, wide, pick, _ = route
    outputs = jnp.einsum("erf,efd->erd", hidden, down_rows, preferred_element_type=F32).astype(BF)
    back = jnp.where(wide, weight[:, :, None, None, :], 0.0).astype(BF).reshape(local * slots, sources * count)
    combined = returned(back, outputs)
    raw_cot, out_grad, pre_grad = backward(route, all_cots[0], gate, up, sig)
    input_grad = jnp.einsum("erf,edf->erd", pre_grad, gate_rows, preferred_element_type=F32).astype(BF)
    token_gradient = returned(pick, input_grad)

    all_inputs, all_hidden, all_grads, all_pre = [inputs], [hidden], [out_grad], [pre_grad]
    for t in range(1, along):
        route_t, inputs_t, gate_t, up_t, sig_t, hidden_t = forward(all_packed[t])
        _, out_grad_t, pre_grad_t = backward(route_t, all_cots[t], gate_t, up_t, sig_t)
        all_inputs.append(inputs_t)
        all_hidden.append(hidden_t)
        all_grads.append(out_grad_t)
        all_pre.append(pre_grad_t)

    pair = [(i, i ^ 1) for i in range(replicas)]

    def columns(values, side):
        size = values.shape[-1] // replicas
        return lax.dynamic_slice_in_dim(values, (place * CORES + side) * size, size, 2)

    def gradient(left, right):
        right = jnp.concatenate(right, axis=1)

        def part(side):
            chosen_columns = jnp.concatenate([columns(l, side) for l in left], axis=1)
            return jnp.einsum("era,erb->eab", chosen_columns, right, preferred_element_type=F32)

        share = with_layout_constraint(part(1 - core).astype(BF).swapaxes(0, 1), Layout((0, 1, 2)))
        theirs = lax.ppermute(share, "replica", pair)
        own = with_layout_constraint(part(core).swapaxes(0, 1), Layout((0, 1, 2)))
        return own + theirs.astype(F32)

    down_gradient = gradient(all_hidden, all_grads)
    gate_up_gradient = gradient(all_inputs, all_pre)

    slot_prob = jnp.sum(raw_cot.astype(F32) * outputs.astype(F32), axis=2).reshape(local, sources, cap, 1)
    prob_part = jnp.sum(jnp.where(chosen, slot_prob, 0.0), axis=2).swapaxes(0, 1)
    choice = expert_ids.T
    prob_gradient = jnp.zeros((top, count), F32)
    home = lax.axis_index("expert")
    for s in range(sources):
        block = lax.rem(home + s, sources) * local
        theirs = to_source(prob_part[s], -s)
        hit = choice[:, None, :] == (block + jnp.arange(local, dtype=jnp.int32))[None, :, None]
        prob_gradient = prob_gradient + jnp.sum(jnp.where(hit, theirs[None], 0.0), axis=1)
    prob_gradient = prob_gradient.T
    return (combined, token_gradient, prob_gradient, gate_up_gradient, down_gradient)


def solution(mesh):
    rows = P(("groups", "expert", "replica"), None)
    sources, replicas = mesh.shape["expert"], mesh.shape["replica"]

    def body(*args):
        return on_device(*args, sources=sources, replicas=replicas)

    return jax.shard_map(
        body,
        mesh=mesh,
        in_specs=(rows, rows, rows, rows, P(None, "expert", None), P(None, "expert", None)),
        out_specs=(
            rows,
            rows,
            rows,
            P(("groups", "replica"), "expert", None),
            P(("groups", "replica"), "expert", None),
        ),
        check_vma=False,
    )
```

profile of v0, /device:TPU:0, one launch (start us, length us, event | category | flops | bytes accessed | tf_op | source)
XLA Modules:
  0.0 222.0 jit_solution(17018279804925090615)
XLA Ops:
  4.5 5.1 %collective-permute-start.2 = (bf16[144,1024]{1,0:T(8,128)(2,1)}, bf16[144,1024]{1,0:T(8,128)(2,1)S(1)}, u32[]{:S(2)}, u32[]{:S(2)}) collective-permute-start(bf16[144,1024]{1,0:T(8,128)(2,1)} %constant_dynamic-update-slice_fusion), channel_id=1, source_target_pairs={{0,12},{4,0},{8,4},{12,8},{1,13},{5,1},{9,5},{13,9},{2,14},{6,2},{... | collective-permute-start | bytes 884744 | tf_op jit(solution)/shard_map/ppermute | solution.py:28
  12.1 2.8 %collective-permute-start.8 = (bf16[128,1024]{1,0:T(8,128)(2,1)}, bf16[128,1024]{1,0:T(8,128)(2,1)}, u32[]{:S(2)}, u32[]{:S(2)}) collective-permute-start(bf16[128,1024]{1,0:T(8,128)(2,1)} %param.9), channel_id=1, source_target_pairs={{0,12},{4,0},{8,4},{12,8},{1,13},{5,1},{9,5},{13,9},{2,14},{6,2},{... | collective-permute-start | bytes 786440 | tf_op jit(solution)/shard_map/ppermute | solution.py:28
  14.9 12.6 %copy.101 = bf16[1024,4,1536]{2,0,1:T(8,128)(2,1)} copy(bf16[1024,4,1536]{2,1,0:T(4,128)(2,1)} %param.10) | data formatting | bytes 25165824 | tf_op args[4]
  27.5 4.8 %copy.102 = bf16[768,4,1024]{2,0,1:T(8,128)(2,1)} copy(bf16[768,4,1024]{2,1,0:T(4,128)(2,1)S(1)} %bitcast.137) | data formatting | bytes 12582912 | tf_op args[5]
  32.4 10.9 %collective-permute-start.7 = (bf16[128,1024]{1,0:T(8,128)(2,1)}, bf16[128,1024]{1,0:T(8,128)(2,1)}, u32[]{:S(2)}, u32[]{:S(2)}) collective-permute-start(bf16[128,1024]{1,0:T(8,128)(2,1)} %param.9), channel_id=1, source_target_pairs={{0,8},{4,12},{8,0},{12,4},{1,9},{5,13},{9,1},{13,5},{2,10},{6,14},... | collective-permute-start | bytes 786440 | tf_op jit(solution)/shard_map/ppermute | solution.py:28
  46.3 7.6 %collective-permute-done.18 = bf16[144,1024]{1,0:T(8,128)(2,1)S(1)} collective-permute-done((bf16[144,1024]{1,0:T(8,128)(2,1)S(1)}, bf16[144,1024]{1,0:T(8,128)(2,1)S(1)}, u32[]{:S(2)}, u32[]{:S(2)}) %collective-permute-start.18) | collective-permute-done | bytes 294944 | tf_op jit(solution)/shard_map/ppermute | solution.py:35
  56.1 4.6 %collective-permute-done.7 = bf16[128,1024]{1,0:T(8,128)(2,1)} collective-permute-done((bf16[128,1024]{1,0:T(8,128)(2,1)}, bf16[128,1024]{1,0:T(8,128)(2,1)}, u32[]{:S(2)}, u32[]{:S(2)}) %collective-permute-start.7) | collective-permute-done | bytes 262176 | tf_op jit(solution)/shard_map/ppermute | solution.py:28
  64.2 2.4 %collective-permute-done.16 = bf16[144,1024]{1,0:T(8,128)(2,1)S(1)} collective-permute-done((bf16[144,1024]{1,0:T(8,128)(2,1)S(1)}, bf16[144,1024]{1,0:T(8,128)(2,1)S(1)}, u32[]{:S(2)}, u32[]{:S(2)}) %collective-permute-start.16) | collective-permute-done | bytes 294944 | tf_op jit(solution)/shard_map/ppermute | solution.py:35
  70.1 3.4 %fusion.107 = f32[4,256,1536]{2,1,0:T(8,128)S(1)} fusion(bf16[4,256,1024]{2,1,0:T(8,128)(2,1)S(1)} %bitcast.138, bf16[4,1024,1536]{2,1,0:T(8,128)(2,1)S(1)} %bitcast.125), kind=kOutput, calls=%fused_computation.175 | convolution fusion | flops 3221225472 | bytes 20971520 | tf_op jit(solution)/shard_map/erd,edf->erf/dot_general | solution.py:91
  74.9 5.5 %fusion.108 = f32[4,256,1536]{2,1,0:T(8,128)} fusion(bf16[4,256,1024]{2,1,0:T(8,128)(2,1)S(1)} %bitcast.140, bf16[4,1024,1536]{2,1,0:T(8,128)(2,1)S(1)} %bitcast.126), kind=kOutput, calls=%fused_computation.176 | convolution fusion | flops 3221225472 | bytes 20971520 | tf_op jit(solution)/shard_map/erd,edf->erf/dot_general | solution.py:91
  84.0 1.8 convolution_convert_fusion.1
  85.9 2.9 %fusion.22 = bf16[1024,1024]{1,0:T(8,128)(2,1)S(1)} fusion(pred[128,8,4,128]{3,2,1,0:T(4,128)(4,1)S(1)} %bitcast.147, bf16[128,1024]{1,0:T(8,128)(2,1)} %collective-permute-done.8, bf16[128,1024]{1,0:T(8,128)(2,1)} %collective-permute-done.7, bf16[128,1024]{1,0:T(8,128)(2,1)} %collective-permute-done.6, bf16[128,1024]{1,0:T(8,128)(2,1)S(1)} %copy-done.20), kind=kOutput, calls=%fused_computation.40 | convolution fusion | flops 1078984704 | bytes 3670016 | tf_op jit(solution)/shard_map/dot_general | solution.py:86
  90.6 10.3 %multiply_convert_fusion.4 = (bf16[4,256,768]{2,1,0:T(8,128)(2,1)S(1)}, bf16[4,256,768]{2,1,0:T(8,128)(2,1)}) fusion(f32[4,256,1536]{2,1,0:T(8,128)} %copy-done.1, bf16[4,256,1024]{2,1,0:T(8,128)(2,1)S(1)} %fusion, bf16[4,768,1024]{2,1,0:T(8,128)(2,1)} %bitcast.127), kind=kOutput, calls=%fused_computation.23 | convolution fusion | flops 1620836352 | bytes 17825792 | tf_op jit(solution)/shard_map/erd,efd->erf/dot_general | solution.py:101
  100.8 10.4 %fusion.31 = bf16[4,256,1024]{2,1,0:T(8,128)(2,1)} fusion(bf16[4,1024,1536]{2,1,0:T(8,128)(2,1)} %bitcast.124, bf16[4,256,768]{2,1,0:T(8,128)(2,1)} %get-tuple-element.18, bf16[4,256,768]{2,1,0:T(8,128)(2,1)S(1)} %get-tuple-element.17), kind=kOutput, calls=%fused_computation.43 | convolution fusion | flops 3228565504 | bytes 17825792 | tf_op jit(solution)/shard_map/erf,edf->erd/dot_general | solution.py:120
  111.3 3.9 %fusion.37 = bf16[512,1024]{1,0:T(8,128)(2,1)} fusion(bf16[1024,1024]{1,0:T(8,128)(2,1)} %bitcast.163, pred[128,8,4,128]{3,2,1,0:T(4,128)(4,1)S(1)} %bitcast.148), kind=kOutput, calls=%fused_computation.49 | convolution fusion | flops 1074266112 | bytes 3670016 | tf_op jit(solution)/shard_map/ra,rd->ad/dot_general | solution.py:108
  115.2 3.8 %collective-permute-start.12 = (f32[4,128]{1,0:T(4,128)S(1)}, f32[4,128]{1,0:T(4,128)S(1)}, u32[]{:S(2)}, u32[]{:S(2)}) collective-permute-start(f32[4,128]{1,0:T(4,128)S(1)} %bitcast.162), channel_id=1, source_target_pairs={{0,12},{4,0},{8,4},{12,8},{1,13},{5,1},{9,5},{13,9},{2,14},{6,2},{... | collective-permute-start | bytes 6152 | tf_op jit(solution)/shard_map/ppermute | solution.py:28
  122.3 2.9 %fusion.28 = bf16[1024,1024]{1,0:T(8,128)(2,1)S(1)} fusion(pred[128,8,4,128]{3,2,1,0:T(4,128)(4,1)} %bitcast.145, bf16[128,1024]{1,0:T(8,128)(2,1)} %collective-permute-done.22, bf16[128,1024]{1,0:T(8,128)(2,1)} %collective-permute-done.21, bf16[128,1024]{1,0:T(8,128)(2,1)} %collective-permute-done.20, bf16[128,1024]{1,0:T(8,128)(2,1)} %collective-permute-done.19), kind=kOutput, calls=%fused_computation.42 | convolution fusion | flops 1078984704 | bytes 3670016 | tf_op jit(solution)/shard_map/dot_general | solution.py:86
  125.7 5.9 %multiply_convert_fusion.2 = (bf16[4,256,768]{2,1,0:T(8,128)(2,1)S(1)}, bf16[4,256,768]{2,1,0:T(8,128)(2,1)S(1)}, bf16[4,256,768]{2,1,0:T(8,128)(2,1)S(1)}) fusion(f32[4,256,1536]{2,1,0:T(8,128)} %fusion.108, bf16[4,256,1024]{2,1,0:T(8,128)(2,1)S(1)} %fusion.2, bf16[4,768,1024]{2,1,0:T(8,128)(2,1)S(1)} %bitcast.133), kind=kOutput, calls=%fused_computation.20 | convolution fusion | flops 1623195648 | bytes 19398656 | tf_op jit(solution)/shard_map/erd,efd->erf/dot_general | solution.py:101
  131.7 2.4 %convolution_convert_fusion = bf16[4,256,1536]{2,1,0:T(8,128)(2,1)S(1)} fusion(bf16[4,256,768]{2,1,0:T(8,128)(2,1)S(1)} %get-tuple-element.16, bf16[4,256,768]{2,1,0:T(8,128)(2,1)S(1)} %get-tuple-element.15, bf16[4,256,768]{2,1,0:T(8,128)(2,1)S(1)} %copy-done.23, bf16[4,256,768]{2,1,0:T(8,128)(2,1)S(1)} %copy-done.22, ...), kind=kOutput, calls=%fused_computation.11 | convolution fusion | flops 1639448576 | bytes 10485760 | tf_op jit(solution)/shard_map/era,erb->eab/dot_general | solution.py:143
  134.1 4.1 %copy.103 = bf16[4,256,1536]{2,0,1:T(4,128)(2,1)} copy(bf16[4,256,1536]{2,1,0:T(8,128)(2,1)S(1)} %convolution_convert_fusion) | data formatting | bytes 6291456
  142.0 2.5 %copy.104 = bf16[4,192,1024]{2,0,1:T(4,128)(2,1)} copy(bf16[4,192,1024]{2,1,0:T(8,128)(2,1)S(1)} %fusion.34) | data formatting | bytes 3145728
  146.3 2.0 copy.56
  148.3 2.1 copy.55
  150.4 4.2 %fusion.45 = f32[4,256,1536]{2,1,0:T(8,128)S(1)} fusion(bf16[4,256,768]{2,1,0:T(8,128)(2,1)} %copy-done.25, bf16[4,256,768]{2,1,0:T(8,128)(2,1)} %copy-done.24, bf16[4,256,768]{2,1,0:T(8,128)(2,1)} %get-tuple-element.18, bf16[4,256,768]{2,1,0:T(8,128)(2,1)} %copy-done.21, bf16[4,256,256]{1,2,0:T(8,128)(2,1)} %copy.56, bf16[4,256,256]{1,2,0:T(8,128)(2,1)} %copy.55), kind=kOutput, calls=%fused_computation.58 | convolution fusion | flops 1637875712 | bytes 13631488 | tf_op jit(solution)/shard_map/era,erb->eab/dot_general | solution.py:143
  156.1 2.9 %collective-permute-start.5 = (bf16[128,1024]{1,0:T(8,128)(2,1)S(1)}, bf16[128,1024]{1,0:T(8,128)(2,1)S(1)}, u32[]{:S(2)}, u32[]{:S(2)}) collective-permute-start(bf16[128,1024]{1,0:T(8,128)(2,1)S(1)} %get-tuple-element.32), channel_id=1, source_target_pairs={{0,4},{4,8},{8,12},{12,0},{1,5},{5,9},{9,13},{13,1},{2,6},{6,10},{... | collective-permute-start | bytes 786440 | tf_op jit(solution)/shard_map/ppermute | solution.py:28
  161.7 5.8 %collective-permute-done.5 = bf16[128,1024]{1,0:T(8,128)(2,1)S(1)} collective-permute-done((bf16[128,1024]{1,0:T(8,128)(2,1)S(1)}, bf16[128,1024]{1,0:T(8,128)(2,1)S(1)}, u32[]{:S(2)}, u32[]{:S(2)}) %collective-permute-start.5) | collective-permute-done | bytes 262176 | tf_op jit(solution)/shard_map/ppermute | solution.py:28
  168.1 10.6 %collective-permute-done.4 = bf16[128,1024]{1,0:T(8,128)(2,1)S(1)} collective-permute-done((bf16[128,1024]{1,0:T(8,128)(2,1)S(1)}, bf16[128,1024]{1,0:T(8,128)(2,1)S(1)}, u32[]{:S(2)}, u32[]{:S(2)}) %collective-permute-start.4) | collective-permute-done | bytes 262176 | tf_op jit(solution)/shard_map/ppermute | solution.py:28
  178.7 7.4 %collective-permute-start.9 = (bf16[128,1024]{1,0:T(8,128)(2,1)S(1)}, bf16[128,1024]{1,0:T(8,128)(2,1)S(1)}, u32[]{:S(2)}, u32[]{:S(2)}) collective-permute-start(bf16[128,1024]{1,0:T(8,128)(2,1)S(1)} %get-tuple-element.28), channel_id=1, source_target_pairs={{0,12},{4,0},{8,4},{12,8},{1,13},{5,1},{9,5},{13,9},{2,14},{6,2},{... | collective-permute-start | bytes 786440 | tf_op jit(solution)/shard_map/ppermute | solution.py:28
  187.6 12.7 %collective-permute-done.10 = bf16[128,1024]{1,0:T(8,128)(2,1)S(1)} collective-permute-done((bf16[128,1024]{1,0:T(8,128)(2,1)S(1)}, bf16[128,1024]{1,0:T(8,128)(2,1)S(1)}, u32[]{:S(2)}, u32[]{:S(2)}) %collective-permute-start.10) | collective-permute-done | bytes 262176 | tf_op jit(solution)/shard_map/ppermute | solution.py:28
  200.3 5.5 %collective-permute-done.9 = bf16[128,1024]{1,0:T(8,128)(2,1)S(1)} collective-permute-done((bf16[128,1024]{1,0:T(8,128)(2,1)S(1)}, bf16[128,1024]{1,0:T(8,128)(2,1)S(1)}, u32[]{:S(2)}, u32[]{:S(2)}) %collective-permute-start.9) | collective-permute-done | bytes 262176 | tf_op jit(solution)/shard_map/ppermute | solution.py:28
  206.6 5.5 %bitcast_add_fusion.1 = f32[192,4,1024]{2,1,0:T(4,128)} fusion(f32[4,192,1024]{2,1,0:T(8,128)S(1)} %fusion.8, bf16[192,4,1024]{2,1,0:T(4,128)(2,1)} %collective-permute-done.24), kind=kLoop, calls=%fused_computation.17 | loop fusion | flops 1572864 | bytes 7864320 | tf_op jit(solution)/shard_map/add | solution.py:148
  212.1 9.4 %bitcast_add_fusion = f32[256,4,1536]{2,1,0:T(4,128)} fusion(f32[4,256,1536]{2,1,0:T(8,128)S(1)} %fusion.45, bf16[256,4,1536]{2,1,0:T(4,128)(2,1)} %collective-permute-done.23), kind=kLoop, calls=%fused_computation.2 | loop fusion | flops 3145728 | bytes 15728640 | tf_op jit(solution)/shard_map/add | solution.py:148
  (183 shorter events, 41.3 us)
Async XLA Ops:
  3.0 24.5 %slice-start.4 = ((s8[6291456]{0:T(1024)(128)(4,1)}), s8[2097152]{0:T(1024)(128)(4,1)S(1)}, s32[]{:S(2)}) async-start(s8[6291456]{0:T(1024)(128)(4,1)} %bitcast.136), calls=%async_computation.4 | async-start | bytes 4194304
  4.5 38.8 %collective-permute-start.2 = (bf16[144,1024]{1,0:T(8,128)(2,1)}, bf16[144,1024]{1,0:T(8,128)(2,1)S(1)}, u32[]{:S(2)}, u32[]{:S(2)}) collective-permute-start(bf16[144,1024]{1,0:T(8,128)(2,1)} %constant_dynamic-update-slice_fusion), channel_id=1, source_target_pairs={{0,12},{4,0},{8,4},{12,8},{1,13},{5,1},{9,5},{13,9},{2,14},{6,2},{... | collective-permute-start | bytes 884744 | tf_op jit(solution)/shard_map/ppermute | solution.py:28
  9.6 34.4 %collective-permute-start.1 = (bf16[144,1024]{1,0:T(8,128)(2,1)}, bf16[144,1024]{1,0:T(8,128)(2,1)S(1)}, u32[]{:S(2)}, u32[]{:S(2)}) collective-permute-start(bf16[144,1024]{1,0:T(8,128)(2,1)} %constant_dynamic-update-slice_fusion), channel_id=1, source_target_pairs={{0,8},{4,12},{8,0},{12,4},{1,9},{5,13},{9,1},{13,5},{2,10},{6,14},... | collective-permute-start | bytes 884744 | tf_op jit(solution)/shard_map/ppermute | solution.py:28
  9.6 22.8 %collective-permute-start = (bf16[144,1024]{1,0:T(8,128)(2,1)}, bf16[144,1024]{1,0:T(8,128)(2,1)S(1)}, u32[]{:S(2)}, u32[]{:S(2)}) collective-permute-start(bf16[144,1024]{1,0:T(8,128)(2,1)} %constant_dynamic-update-slice_fusion), channel_id=1, source_target_pairs={{0,4},{4,8},{8,12},{12,0},{1,5},{5,9},{9,13},{13,1},{2,6},{6,10},{... | collective-permute-start | bytes 884744 | tf_op jit(solution)/shard_map/ppermute | solution.py:28
  10.6 35.0 %collective-permute-start.15 = (bf16[144,1024]{1,0:T(8,128)(2,1)}, bf16[144,1024]{1,0:T(8,128)(2,1)S(1)}, u32[]{:S(2)}, u32[]{:S(2)}) collective-permute-start(bf16[144,1024]{1,0:T(8,128)(2,1)} %constant_dynamic-update-slice_fusion), channel_id=1, source_target_pairs={{0,2},{1,3},{2,0},{3,1},{4,6},{5,7},{6,4},{7,5},{8,10},{9,11},{10,... | collective-permute-start | bytes 884744 | tf_op jit(solution)/shard_map/ppermute | solution.py:35
  12.1 43.4 %collective-permute-start.8 = (bf16[128,1024]{1,0:T(8,128)(2,1)}, bf16[128,1024]{1,0:T(8,128)(2,1)}, u32[]{:S(2)}, u32[]{:S(2)}) collective-permute-start(bf16[128,1024]{1,0:T(8,128)(2,1)} %param.9), channel_id=1, source_target_pairs={{0,12},{4,0},{8,4},{12,8},{1,13},{5,1},{9,5},{13,9},{2,14},{6,2},{... | collective-permute-start | bytes 786440 | tf_op jit(solution)/shard_map/ppermute | solution.py:28
  14.9 12.6 %slice-start.5 = ((s8[6291456]{0:T(1024)(128)(4,1)}), s8[4194304]{0:T(1024)(128)(4,1)S(1)}, s32[]{:S(2)}) async-start(s8[6291456]{0:T(1024)(128)(4,1)} %bitcast.136), calls=%async_computation.5 | async-start | bytes 8388608
  32.4 36.4 %copy-start.18 = (bf16[128,1024]{1,0:T(8,128)(2,1)S(1)}, bf16[128,1024]{1,0:T(8,128)(2,1)}, u32[]{:S(2)}) copy-start(bf16[128,1024]{1,0:T(8,128)(2,1)} %param.6) | copy-start | bytes 786436
  32.4 28.2 %collective-permute-start.7 = (bf16[128,1024]{1,0:T(8,128)(2,1)}, bf16[128,1024]{1,0:T(8,128)(2,1)}, u32[]{:S(2)}, u32[]{:S(2)}) collective-permute-start(bf16[128,1024]{1,0:T(8,128)(2,1)} %param.9), channel_id=1, source_target_pairs={{0,8},{4,12},{8,0},{12,4},{1,9},{5,13},{9,1},{13,5},{2,10},{6,14},... | collective-permute-start | bytes 786440 | tf_op jit(solution)/shard_map/ppermute | solution.py:28
  43.3 18.8 %collective-permute-start.6 = (bf16[128,1024]{1,0:T(8,128)(2,1)}, bf16[128,1024]{1,0:T(8,128)(2,1)}, u32[]{:S(2)}, u32[]{:S(2)}) collective-permute-start(bf16[128,1024]{1,0:T(8,128)(2,1)} %param.9), channel_id=1, source_target_pairs={{0,4},{4,8},{8,12},{12,0},{1,5},{5,9},{9,13},{13,1},{2,6},{6,10},{... | collective-permute-start | bytes 786440 | tf_op jit(solution)/shard_map/ppermute | solution.py:28
  44.0 9.9 %collective-permute-start.18 = (bf16[144,1024]{1,0:T(8,128)(2,1)S(1)}, bf16[144,1024]{1,0:T(8,128)(2,1)S(1)}, u32[]{:S(2)}, u32[]{:S(2)}) collective-permute-start(bf16[144,1024]{1,0:T(8,128)(2,1)S(1)} %collective-permute-done.2), channel_id=1, source_target_pairs={{0,2},{1,3},{2,0},{3,1},{4,6},{5,7},{6,4},{7,5},{8,10},{9,11},{10,... | collective-permute-start | bytes 884744 | tf_op jit(solution)/shard_map/ppermute | solution.py:35
  45.6 21.5 %copy-start.17 = (bf16[144,1024]{1,0:T(8,128)(2,1)}, bf16[144,1024]{1,0:T(8,128)(2,1)S(1)}, u32[]{:S(2)}) copy-start(bf16[144,1024]{1,0:T(8,128)(2,1)S(1)} %collective-permute-done.15) | copy-start | bytes 884740
  45.6 17.1 %collective-permute-start.17 = (bf16[144,1024]{1,0:T(8,128)(2,1)S(1)}, bf16[144,1024]{1,0:T(8,128)(2,1)S(1)}, u32[]{:S(2)}, u32[]{:S(2)}) collective-permute-start(bf16[144,1024]{1,0:T(8,128)(2,1)S(1)} %collective-permute-done.1), channel_id=1, source_target_pairs={{0,2},{1,3},{2,0},{3,1},{4,6},{5,7},{6,4},{7,5},{8,10},{9,11},{10,... | collective-permute-start | bytes 884744 | tf_op jit(solution)/shard_map/ppermute | solution.py:35
  46.2 23.8 %copy-start = (bf16[1024,4,1536]{2,0,1:T(8,128)(2,1)S(1)}, bf16[1024,4,1536]{2,0,1:T(8,128)(2,1)}, u32[]{:S(2)}) copy-start(bf16[1024,4,1536]{2,0,1:T(8,128)(2,1)} %copy.101) | copy-start | bytes 37748740
  54.0 12.6 %collective-permute-start.16 = (bf16[144,1024]{1,0:T(8,128)(2,1)S(1)}, bf16[144,1024]{1,0:T(8,128)(2,1)S(1)}, u32[]{:S(2)}, u32[]{:S(2)}) collective-permute-start(bf16[144,1024]{1,0:T(8,128)(2,1)S(1)} %collective-permute-done), channel_id=1, source_target_pairs={{0,2},{1,3},{2,0},{3,1},{4,6},{5,7},{6,4},{7,5},{8,10},{9,11},{10,... | collective-permute-start | bytes 884744 | tf_op jit(solution)/shard_map/ppermute | solution.py:35
  55.5 66.0 %collective-permute-start.19 = (bf16[128,1024]{1,0:T(8,128)(2,1)}, bf16[128,1024]{1,0:T(8,128)(2,1)}, u32[]{:S(2)}, u32[]{:S(2)}) collective-permute-start(bf16[128,1024]{1,0:T(8,128)(2,1)} %param.9), channel_id=1, source_target_pairs={{0,2},{1,3},{2,0},{3,1},{4,6},{5,7},{6,4},{7,5},{8,10},{9,11},{10,... | collective-permute-start | bytes 786440 | tf_op jit(solution)/shard_map/ppermute | solution.py:35
  60.6 60.9 %collective-permute-start.22 = (bf16[128,1024]{1,0:T(8,128)(2,1)}, bf16[128,1024]{1,0:T(8,128)(2,1)}, u32[]{:S(2)}, u32[]{:S(2)}) collective-permute-start(bf16[128,1024]{1,0:T(8,128)(2,1)} %collective-permute-done.8), channel_id=1, source_target_pairs={{0,2},{1,3},{2,0},{3,1},{4,6},{5,7},{6,4},{7,5},{8,10},{9,11},{10,... | collective-permute-start | bytes 786440 | tf_op jit(solution)/shard_map/ppermute | solution.py:35
  62.1 60.2 %collective-permute-start.21 = (bf16[128,1024]{1,0:T(8,128)(2,1)}, bf16[128,1024]{1,0:T(8,128)(2,1)}, u32[]{:S(2)}, u32[]{:S(2)}) collective-permute-start(bf16[128,1024]{1,0:T(8,128)(2,1)} %collective-permute-done.7), channel_id=1, source_target_pairs={{0,2},{1,3},{2,0},{3,1},{4,6},{5,7},{6,4},{7,5},{8,10},{9,11},{10,... | collective-permute-start | bytes 786440 | tf_op jit(solution)/shard_map/ppermute | solution.py:35
  62.7 59.6 %collective-permute-start.20 = (bf16[128,1024]{1,0:T(8,128)(2,1)}, bf16[128,1024]{1,0:T(8,128)(2,1)}, u32[]{:S(2)}, u32[]{:S(2)}) collective-permute-start(bf16[128,1024]{1,0:T(8,128)(2,1)} %collective-permute-done.6), channel_id=1, source_target_pairs={{0,2},{1,3},{2,0},{3,1},{4,6},{5,7},{6,4},{7,5},{8,10},{9,11},{10,... | collective-permute-start | bytes 786440 | tf_op jit(solution)/shard_map/ppermute | solution.py:35
  68.8 17.1 %copy-start.12 = (pred[4,4,64,4,128]{4,3,2,1,0:T(4,128)(4,1)}, pred[4,4,64,4,128]{4,3,2,1,0:T(4,128)(4,1)S(1)}, u32[]{:S(2)}) copy-start(pred[4,4,64,4,128]{4,3,2,1,0:T(4,128)(4,1)S(1)} %get-tuple-element.45) | copy-start | bytes 1572868
  115.2 40.9 %collective-permute-start.12 = (f32[4,128]{1,0:T(4,128)S(1)}, f32[4,128]{1,0:T(4,128)S(1)}, u32[]{:S(2)}, u32[]{:S(2)}) collective-permute-start(f32[4,128]{1,0:T(4,128)S(1)} %bitcast.162), channel_id=1, source_target_pairs={{0,12},{4,0},{8,4},{12,8},{1,13},{5,1},{9,5},{13,9},{2,14},{6,2},{... | collective-permute-start | bytes 6152 | tf_op jit(solution)/shard_map/ppermute | solution.py:28
  121.5 37.5 %collective-permute-start.13 = (f32[4,128]{1,0:T(4,128)S(1)}, f32[4,128]{1,0:T(4,128)S(1)}, u32[]{:S(2)}, u32[]{:S(2)}) collective-permute-start(f32[4,128]{1,0:T(4,128)S(1)} %bitcast.161), channel_id=1, source_target_pairs={{0,8},{4,12},{8,0},{12,4},{1,9},{5,13},{9,1},{13,5},{2,10},{6,14},... | collective-permute-start | bytes 6152 | tf_op jit(solution)/shard_map/ppermute | solution.py:28
  121.6 38.4 %collective-permute-start.14 = (f32[4,128]{1,0:T(4,128)S(1)}, f32[4,128]{1,0:T(4,128)S(1)}, u32[]{:S(2)}, u32[]{:S(2)}) collective-permute-start(f32[4,128]{1,0:T(4,128)S(1)} %bitcast.160), channel_id=1, source_target_pairs={{0,4},{4,8},{8,12},{12,0},{1,5},{5,9},{9,13},{13,1},{2,6},{6,10},{... | collective-permute-start | bytes 6152 | tf_op jit(solution)/shard_map/ppermute | solution.py:28
  125.7 15.0 %copy-start.8 = (bf16[4,256,1024]{2,1,0:T(8,128)(2,1)}, bf16[4,256,1024]{2,1,0:T(8,128)(2,1)S(1)}, u32[]{:S(2)}) copy-start(bf16[4,256,1024]{2,1,0:T(8,128)(2,1)S(1)} %fusion.2) | copy-start | bytes 6291460
  138.2 73.9 %collective-permute-start.23 = (bf16[256,4,1536]{2,1,0:T(4,128)(2,1)}, bf16[256,4,1536]{2,1,0:T(4,128)(2,1)}, u32[]{:S(2)}, u32[]{:S(2)}) collective-permute-start(bf16[256,4,1536]{2,1,0:T(4,128)(2,1)} %bitcast.122), channel_id=1, source_target_pairs={{0,1},{1,0},{2,3},{3,2},{4,5},{5,4},{6,7},{7,6},{8,9},{9,8},{10,11... | collective-permute-start | bytes 9437192 | tf_op jit(solution)/shard_map/ppermute | solution.py:146
  144.5 62.1 %collective-permute-start.24 = (bf16[192,4,1024]{2,1,0:T(4,128)(2,1)}, bf16[192,4,1024]{2,1,0:T(4,128)(2,1)}, u32[]{:S(2)}, u32[]{:S(2)}) collective-permute-start(bf16[192,4,1024]{2,1,0:T(4,128)(2,1)} %bitcast.123), channel_id=1, source_target_pairs={{0,1},{1,0},{2,3},{3,2},{4,5},{5,4},{6,7},{7,6},{8,9},{9,8},{10,11... | collective-permute-start | bytes 4718600 | tf_op jit(solution)/shard_map/ppermute | solution.py:146
  156.1 11.4 %collective-permute-start.5 = (bf16[128,1024]{1,0:T(8,128)(2,1)S(1)}, bf16[128,1024]{1,0:T(8,128)(2,1)S(1)}, u32[]{:S(2)}, u32[]{:S(2)}) collective-permute-start(bf16[128,1024]{1,0:T(8,128)(2,1)S(1)} %get-tuple-element.32), channel_id=1, source_target_pairs={{0,4},{4,8},{8,12},{12,0},{1,5},{5,9},{9,13},{13,1},{2,6},{6,10},{... | collective-permute-start | bytes 786440 | tf_op jit(solution)/shard_map/ppermute | solution.py:28
  158.9 19.8 %collective-permute-start.4 = (bf16[128,1024]{1,0:T(8,128)(2,1)S(1)}, bf16[128,1024]{1,0:T(8,128)(2,1)S(1)}, u32[]{:S(2)}, u32[]{:S(2)}) collective-permute-start(bf16[128,1024]{1,0:T(8,128)(2,1)S(1)} %get-tuple-element.33), channel_id=1, source_target_pairs={{0,8},{4,12},{8,0},{12,4},{1,9},{5,13},{9,1},{13,5},{2,10},{6,14},... | collective-permute-start | bytes 786440 | tf_op jit(solution)/shard_map/ppermute | solution.py:28
  160.0 18.8 %collective-permute-start.3 = (bf16[128,1024]{1,0:T(8,128)(2,1)S(1)}, bf16[128,1024]{1,0:T(8,128)(2,1)S(1)}, u32[]{:S(2)}, u32[]{:S(2)}) collective-permute-start(bf16[128,1024]{1,0:T(8,128)(2,1)S(1)} %get-tuple-element.31), channel_id=1, source_target_pairs={{0,12},{4,0},{8,4},{12,8},{1,13},{5,1},{9,5},{13,9},{2,14},{6,2},{... | collective-permute-start | bytes 786440 | tf_op jit(solution)/shard_map/ppermute | solution.py:28
  167.5 20.1 %collective-permute-start.11 = (bf16[128,1024]{1,0:T(8,128)(2,1)S(1)}, bf16[128,1024]{1,0:T(8,128)(2,1)S(1)}, u32[]{:S(2)}, u32[]{:S(2)}) collective-permute-start(bf16[128,1024]{1,0:T(8,128)(2,1)S(1)} %get-tuple-element.29), channel_id=1, source_target_pairs={{0,4},{4,8},{8,12},{12,0},{1,5},{5,9},{9,13},{13,1},{2,6},{6,10},{... | collective-permute-start | bytes 786440 | tf_op jit(solution)/shard_map/ppermute | solution.py:28
  178.7 21.5 %collective-permute-start.10 = (bf16[128,1024]{1,0:T(8,128)(2,1)S(1)}, bf16[128,1024]{1,0:T(8,128)(2,1)S(1)}, u32[]{:S(2)}, u32[]{:S(2)}) collective-permute-start(bf16[128,1024]{1,0:T(8,128)(2,1)S(1)} %get-tuple-element.30), channel_id=1, source_target_pairs={{0,8},{4,12},{8,0},{12,4},{1,9},{5,13},{9,1},{13,5},{2,10},{6,14},... | collective-permute-start | bytes 786440 | tf_op jit(solution)/shard_map/ppermute | solution.py:28
  178.7 27.0 %collective-permute-start.9 = (bf16[128,1024]{1,0:T(8,128)(2,1)S(1)}, bf16[128,1024]{1,0:T(8,128)(2,1)S(1)}, u32[]{:S(2)}, u32[]{:S(2)}) collective-permute-start(bf16[128,1024]{1,0:T(8,128)(2,1)S(1)} %get-tuple-element.28), channel_id=1, source_target_pairs={{0,12},{4,0},{8,4},{12,8},{1,13},{5,1},{9,5},{13,9},{2,14},{6,2},{... | collective-permute-start | bytes 786440 | tf_op jit(solution)/shard_map/ppermute | solution.py:28
  (26 other events, 127.3 us)
where the time goes:
time: 226 us; the launch traced here: 222 us
  matrix products  60.3 us (27%)
  waiting for transfers between devices  49.2 us (22%)
  starting transfers between devices  48.3 us (21%)
  local copies, waits for them, and re-layouts  37.6 us (17%)
  other arithmetic  24.7 us (11%)
    ppermute x15, waiting for transfers between devices, to_source(): return lax.ppermute(values, 'expert', step) if shift else values  39.1 us
    ppermute x15, starting transfers between devices, to_source(): return lax.ppermute(values, 'expert', step) if shift else values  38.5 us
    unnamed x87, local copies, waits for them, and re-layouts  32 us
    dot_general x2, matrix products, backward(): jnp.einsum('erd,efd->erf', out_grad, down_rows, preferred_element_type=F32)  16.1 us
    add x2, other arithmetic, gradient(): return own + theirs.astype(F32)  14.9 us
    dot_general x1, matrix products, on_device(): jnp.einsum('erf,edf->erd', pre_grad, gate_rows, preferred_element_type=F32)  10.4 us
    ppermute x8, waiting for transfers between devices, to_chip(): return lax.ppermute(values, 'replica', step)  10.1 us
    ppermute x8, starting transfers between devices, to_chip(): return lax.ppermute(values, 'replica', step)  9.25 us
  transfers between devices with their start and end apart: 25, of which 7 were waited for; matrix products, arithmetic and copies ran while one was open for 49% of the time, Pallas kernels for 0%

commit v1 on v0

--- a/solution.py
+++ b/solution.py
@@ -1,6 +1,10 @@
+import functools
+
 import jax
 import jax.numpy as jnp
 from jax import lax
+from jax.experimental import pallas as pl
+from jax.experimental.pallas import tpu as pltpu
 from jax.experimental.layout import Layout, with_layout_constraint
 from jax.sharding import PartitionSpec as P
 
@@ -11,7 +15,7 @@
 F32 = jnp.float32
 
 
-def on_device(tokens, expert_ids, gate_probs, cotangent, gate_up, down_weights, *, sources, replicas):
+def general(tokens, expert_ids, gate_probs, cotangent, gate_up, down_weights, *, sources, replicas):
     count, width = tokens.shape
     top = expert_ids.shape[1]
     local = gate_up.shape[1]
@@ -164,6 +168,351 @@
     return (combined, token_gradient, prob_gradient, gate_up_gradient, down_gradient)
 
 
+NOTES = 16
+HALF = 8
+
+
+def routing_tile(note_refs, expert, count, cap):
+    members, weights = [], []
+    for ref in note_refs:
+        tile = ref[...].astype(F32)
+        named = tile[:HALF].astype(jnp.int32) == expert
+        members.append(jnp.max(jnp.where(named, 1.0, 0.0), axis=0, keepdims=True))
+        weights.append(jnp.sum(jnp.where(named, tile[HALF:], 0.0), axis=0, keepdims=True))
+    member = jnp.concatenate(members, axis=0)
+    ahead = (
+        lax.broadcasted_iota(jnp.int32, (count, count), 0) < lax.broadcasted_iota(jnp.int32, (count, count), 1)
+    )
+    ahead = jnp.where(ahead, 1.0, 0.0).astype(BF)
+    rank = jnp.dot(member.astype(BF), ahead, preferred_element_type=F32).astype(jnp.int32)
+    slots = len(note_refs) * cap
+    row = lax.broadcasted_iota(jnp.int32, (slots, count), 0)
+    picks = []
+    for s in range(len(note_refs)):
+        place = jnp.where(members[s] > 0.0, rank[s:s + 1] + s * cap, -1)
+        picks.append(row == place)
+    return picks, weights
+
+
+def selected(picks, values):
+    return jnp.concatenate([jnp.where(p, v, 0.0) for p, v in zip(picks, values)], axis=1)
+
+
+def across(left, right):
+    return lax.dot_general(left, right, (((0,), (0,)), ((), ())), preferred_element_type=F32)
+
+
+def against(left, right):
+    return lax.dot_general(left, right, (((1,), (1,)), ((), ())), preferred_element_type=F32)
+
+
+def forward_tile(pick, tok, gate_ref, hidden_width):
+    inputs = jnp.dot(pick, tok[...], preferred_element_type=F32).astype(BF)
+    pre_act = jnp.dot(inputs, gate_ref[0], preferred_element_type=F32)
+    gate, up = pre_act[:, :hidden_width], pre_act[:, hidden_width:]
+    sig = jax.nn.sigmoid(gate)
+    return inputs, pre_act, (gate * sig * up).astype(BF)
+
+
+def backward_tile(pick, back, cot, down_ref, pre_act, hidden_width):
+    raw_cot = jnp.dot(pick, cot[...], preferred_element_type=F32)
+    out_grad = (jnp.sum(back, axis=1, keepdims=True) * raw_cot).astype(BF)
+    hidden_grad = against(out_grad, down_ref[0])
+    gate, up = pre_act[:, :hidden_width], pre_act[:, hidden_width:]
+    sig = jax.nn.sigmoid(gate)
+    pre_grad = jnp.concatenate(
+        [hidden_grad * up * sig * (1.0 + gate * (1.0 - sig)), hidden_grad * gate * sig], axis=1
+    ).astype(BF)
+    return raw_cot, out_grad, pre_grad
+
+
+def own_forward(sources, cap, info, *refs):
+    packed, refs = refs[:sources], refs[sources:]
+    note_refs, refs = refs[:sources], refs[sources:]
+    gate_ref, down_ref, refs = refs[0], refs[1], refs[2:]
+    part_refs, refs = refs[:sources], refs[sources:]
+    input_ref, pre_ref, hidden_ref, output_ref, tok, total = refs
+    e = pl.program_id(0)
+    count = tok.shape[0] // sources
+
+    @pl.when(e == 0)
+    def _():
+        for s in range(sources):
+            tok[s * count:(s + 1) * count, :] = packed[s][...]
+        total[...] = jnp.zeros_like(total)
+
+    picks, weights = routing_tile(note_refs, info[0] + e, count, cap)
+    pick = selected(picks, [1.0] * sources).astype(BF)
+    back = selected(picks, weights)
+    inputs, pre_act, hidden = forward_tile(pick, tok, gate_ref, hidden_ref.shape[2])
+    outputs = jnp.dot(hidden, down_ref[0], preferred_element_type=F32).astype(BF)
+    input_ref[0] = inputs
+    pre_ref[0] = pre_act
+    hidden_ref[0] = hidden
+    output_ref[0] = outputs
+    total[...] += across(back.astype(BF), outputs)
+
+    @pl.when(e == pl.num_programs(0) - 1)
+    def _():
+        for s in range(sources):
+            part_refs[s][...] = total[s * count:(s + 1) * count, :].astype(BF)
+
+
+def own_backward(sources, cap, info, *refs):
+    cots, refs = refs[:sources], refs[sources:]
+    note_refs, refs = refs[:sources], refs[sources:]
+    gate_ref, down_ref, pre_ref, output_ref, refs = refs[0], refs[1], refs[2], refs[3], refs[4:]
+    part_refs, refs = refs[:sources], refs[sources:]
+    prob_ref, out_grad_ref, pre_grad_ref, cot, total = refs
+    e = pl.program_id(0)
+    count = cot.shape[0] // sources
+
+    @pl.when(e == 0)
+    def _():
+        for s in range(sources):
+            cot[s * count:(s + 1) * count, :] = cots[s][...]
+        total[...] = jnp.zeros_like(total)
+
+    picks, weights = routing_tile(note_refs, info[0] + e, count, cap)
+    pick = selected(picks, [1.0] * sources).astype(BF)
+    back = selected(picks, weights)
+    hidden_width = pre_ref.shape[2] // 2
+    raw_cot, out_grad, pre_grad = backward_tile(pick, back, cot, down_ref, pre_ref[0], hidden_width)
+    out_grad_ref[0] = out_grad
+    pre_grad_ref[0] = pre_grad
+    slot_prob = jnp.sum(raw_cot * output_ref[0].astype(F32), axis=1, keepdims=True)
+    for s in range(sources):
+        prob_ref[s, pl.ds(e, 1), :] = jnp.sum(jnp.where(picks[s], slot_prob, 0.0), axis=0, keepdims=True)
+    input_grad = against(pre_grad, gate_ref[0]).astype(BF)
+    total[...] += across(pick, input_grad)
+
+    @pl.when(e == pl.num_programs(0) - 1)
+    def _():
+        for s in range(sources):
+            part_refs[s][...] = total[s * count:(s + 1) * count, :].astype(BF)
+
+
+def far_gradients(sources, cap, info, *refs):
+    packed, refs = refs[:sources], refs[sources:]
+    note_refs, refs = refs[:sources], refs[sources:]
+    cots, refs = refs[:sources], refs[sources:]
+    gate_ref, down_ref, input_ref, hidden_ref, out_grad_ref, pre_grad_ref = refs[:6]
+    gate_own, gate_share, down_own, down_share = refs[6:10]
+    tok, cot, all_inputs, all_hidden, all_grads, all_pre, gate_sum, down_sum = refs[10:]
+    e = pl.program_id(0)
+    count = tok.shape[0] // sources
+    slots = sources * cap
+
+    @pl.when(e == 0)
+    def _():
+        for s in range(sources):
+            tok[s * count:(s + 1) * count, :] = packed[s][...]
+            cot[s * count:(s + 1) * count, :] = cots[s][...]
+
+    picks, weights = routing_tile(note_refs, info[0] + e, count, cap)
+    pick = selected(picks, [1.0] * sources).astype(BF)
+    back = selected(picks, weights)
+    hidden_width = hidden_ref.shape[2]
+    inputs, pre_act, hidden = forward_tile(pick, tok, gate_ref, hidden_width)
+    _, out_grad, pre_grad = backward_tile(pick, back, cot, down_ref, pre_act, hidden_width)
+    for scratch, own, far in (
+        (all_inputs, input_ref, inputs), (all_hidden, hidden_ref, hidden),
+        (all_grads, out_grad_ref, out_grad), (all_pre, pre_grad_ref, pre_grad),
+    ):
+        scratch[:slots, :] = own[0]
+        scratch[slots:, :] = far
+
+    place, core = info[1], info[2]
+    for left, right, total, own, share in (
+        (all_hidden, all_grads, down_sum, down_own, down_share),
+        (all_inputs, all_pre, gate_sum, gate_own, gate_share),
+    ):
+        size, block = total.shape[0], own.shape[1]
+        columns = pl.ds(pl.multiple_of(place * size, size), size)
+        total[...] = across(left[:, columns], right[...])
+        own[0] = total[pl.ds(pl.multiple_of(core * block, block), block), :]
+        share[0] = total[pl.ds(pl.multiple_of((1 - core) * block, block), block), :].astype(BF)
+
+
+def joined(local, own_ref, share_ref, out_ref):
+    for e in range(local):
+        out_ref[:, e, :] = own_ref[e] + share_ref[e].astype(F32)
+
+
+def whole(*shape):
+    return pl.BlockSpec(shape, lambda e, info: (0,) * len(shape))
+
+
+def each(*shape):
+    return pl.BlockSpec((1,) + shape, lambda e, info: (e,) + (0,) * len(shape))
+
+
+def kernel_call(body, grid, in_specs, out_specs, out_shape, scratch, flops, moved):
+    return pl.pallas_call(
+        body,
+        grid_spec=pltpu.PrefetchScalarGridSpec(
+            num_scalar_prefetch=1, grid=(grid,), in_specs=in_specs, out_specs=out_specs, scratch_shapes=scratch
+        ),
+        out_shape=out_shape,
+        compiler_params=pltpu.CompilerParams(vmem_limit_bytes=56 << 20),
+        cost_estimate=pl.CostEstimate(flops=flops, bytes_accessed=moved, transcendentals=0),
+    )
+
+
+def two_chips(tokens, expert_ids, gate_probs, cotangent, gate_up, down_weights, *, sources, replicas):
+    count, width = tokens.shape
+    top = expert_ids.shape[1]
+    local = gate_up.shape[1]
+    hidden_width = down_weights.shape[0]
+    pre_width = gate_up.shape[2]
+    cap = min(CAP, count)
+    along = replicas // CORES
+    replica = lax.axis_index("replica")
+    core, place = lax.rem(replica, CORES), lax.div(replica, CORES)
+    home = lax.axis_index("expert")
+    slots = sources * cap
+    info = jnp.stack([home * local, place, core]).astype(jnp.int32)
+
+    def to_source(values, shift):
+        step = [(i, (i + shift) % sources) for i in range(sources)]
+        return lax.ppermute(values, "expert", step) if shift else values
+
+    def to_chip(values):
+        step = [
+            (x * CORES + c, ((x + 1) % along) * CORES + c)
+            for x in range(along) for c in range(CORES)
+        ]
+        return lax.ppermute(values, "replica", step)
+
+    fill = ((0, HALF - top), (0, width - count))
+    packed = jnp.concatenate(
+        [tokens, jnp.pad(expert_ids.T.astype(BF), fill, constant_values=-1), jnp.pad(gate_probs.T, fill)], axis=0
+    )
+
+    def gathered(values):
+        far = [to_chip(values)]
+        held = [to_source(values, s) for s in range(sources)]
+        far += [to_chip(h) for h in held[1:]]
+        return held, far
+
+    near_packed, far_packed = gathered(packed)
+    near_cots, far_cots = gathered(cotangent)
+    gate_rows = lax.optimization_barrier(
+        with_layout_constraint(gate_up.swapaxes(0, 1), Layout((0, 1, 2)))
+    )
+    down_rows = lax.optimization_barrier(
+        with_layout_constraint(down_weights.swapaxes(0, 1), Layout((0, 1, 2)))
+    )
+
+    block_specs = [whole(count, width)] * sources
+    note_specs = [pl.BlockSpec((NOTES, count), lambda e, info: (count // NOTES, 0))] * sources
+    weight_specs = [each(width, pre_width), each(hidden_width, width)]
+    block_shape = jax.ShapeDtypeStruct((count, width), BF)
+    gathered_rows = pltpu.VMEM((sources * count, width), BF)
+    part_total = pltpu.VMEM((sources * count, width), F32)
+
+    def array(size, dtype, rows=slots):
+        return jax.ShapeDtypeStruct((local, rows, size), dtype)
+
+    product = 2 * local * slots * width * hidden_width
+    weight_bytes = 6 * local * width * hidden_width
+    *out_parts, inputs, pre_act, hidden, outputs = kernel_call(
+        functools.partial(own_forward, sources, cap),
+        local,
+        block_specs + note_specs + weight_specs,
+        block_specs + [each(slots, width), each(slots, pre_width), each(slots, hidden_width), each(slots, width)],
+        [block_shape] * sources + [array(width, BF), array(pre_width, F32), array(hidden_width, BF), array(width, BF)],
+        [gathered_rows, part_total],
+        4 * product,
+        2 * weight_bytes,
+    )(info, *near_packed, *near_packed, gate_rows, down_rows)
+
+    def returned(parts):
+        return [to_source(parts[s], -s) for s in range(sources)]
+
+    def added(arrived):
+        return sum([a.astype(F32) for a in arrived[1:]], arrived[0].astype(F32)).astype(BF)
+
+    out_arrived = returned(out_parts)
+
+    *grad_parts, prob_part, out_grad, pre_grad = kernel_call(
+        functools.partial(own_backward, sources, cap),
+        local,
+        block_specs + note_specs + weight_specs + [each(slots, pre_width), each(slots, width)],
+        block_specs + [whole(sources, local, count), each(slots, width), each(slots, pre_width)],
+        [block_shape] * sources + [
+            jax.ShapeDtypeStruct((sources, local, count), F32), array(width, BF), array(pre_width, BF)
+        ],
+        [gathered_rows, part_total],
+        4 * product,
+        2 * weight_bytes,
+    )(info, *near_cots, *near_packed, gate_rows, down_rows, pre_act, outputs)
+    prob_arrived = [to_source(prob_part[s], -s) for s in range(sources)]
+    grad_arrived = returned(grad_parts)
+
+    gate_block, down_block = width // replicas, hidden_width // replicas
+    gate_own, gate_share, down_own, down_share = kernel_call(
+        functools.partial(far_gradients, sources, cap),
+        local,
+        block_specs + note_specs + block_specs + weight_specs + [
+            each(slots, width), each(slots, hidden_width), each(slots, width), each(slots, pre_width)
+        ],
+        [
+            each(gate_block, pre_width), each(gate_block, pre_width),
+            each(down_block, width), each(down_block, width),
+        ],
+        [
+            array(pre_width, F32, gate_block), array(pre_width, BF, gate_block),
+            array(width, F32, down_block), array(width, BF, down_block),
+        ],
+        [
+            gathered_rows, gathered_rows,
+            pltpu.VMEM((2 * slots, width), BF), pltpu.VMEM((2 * slots, hidden_width), BF),
+            pltpu.VMEM((2 * slots, width), BF), pltpu.VMEM((2 * slots, pre_width), BF),
+            pltpu.VMEM((CORES * gate_block, pre_width), F32), pltpu.VMEM((CORES * down_block, width), F32),
+        ],
+        6 * product,
+        3 * weight_bytes,
+    )(
+        info, *far_packed, *far_packed, *far_cots, gate_rows, down_rows,
+        inputs, hidden, out_grad, pre_grad,
+    )
+
+    pair = [(i, i ^ 1) for i in range(replicas)]
+
+    def final(own, share):
+        theirs = lax.ppermute(share, "replica", pair)
+        rows, size = own.shape[1], own.shape[2]
+        cut = rows // 4
+        return pl.pallas_call(
+            functools.partial(joined, local),
+            grid=(rows // cut,),
+            in_specs=[pl.BlockSpec((local, cut, size), lambda i: (0, i, 0))] * 2,
+            out_specs=pl.BlockSpec((cut, local, size), lambda i: (i, 0, 0)),
+            out_shape=jax.ShapeDtypeStruct((rows, local, size), F32),
+            compiler_params=pltpu.CompilerParams(vmem_limit_bytes=56 << 20),
+            cost_estimate=pl.CostEstimate(flops=0, bytes_accessed=10 * own.size, transcendentals=0),
+        )(own, theirs)
+
+    gate_up_gradient = final(gate_own, gate_share)
+    down_gradient = final(down_own, down_share)
+
+    choice = expert_ids.T
+    prob_gradient = jnp.zeros((top, count), F32)
+    for s in range(sources):
+        block = lax.rem(home + s, sources) * local
+        hit = choice[:, None, :] == (block + jnp.arange(local, dtype=jnp.int32))[None, :, None]
+        prob_gradient = prob_gradient + jnp.sum(jnp.where(hit, prob_arrived[s][None], 0.0), axis=1)
+    return (added(out_arrived), added(grad_arrived), prob_gradient.T, gate_up_gradient, down_gradient)
+
+
+def on_device(*args, sources, replicas):
+    count, top, local = args[0].shape[0], args[1].shape[1], args[4].shape[1]
+    small = sources * min(CAP, count) * local <= 1024 and sources <= 4
+    plain = replicas == 2 * CORES and small and count % 128 == 0 and top <= HALF
+    return (two_chips if plain else general)(*args, sources=sources, replicas=replicas)
+
+
 def solution(mesh):
     rows = P(("groups", "expert", "replica"), None)
     sources, replicas = mesh.shape["expert"], mesh.shape["replica"]

time: 226 us -> 193 us (0.85); the launches traced: 222 us -> 192 us
  Pallas kernels: 0 us -> 67.8 us
  matrix products: 60.3 us -> 0 us
  other arithmetic: 24.7 us -> 6.99 us
  local copies, waits for them, and re-layouts: 37.6 us -> 19.9 us
  starting transfers between devices: 48.3 us -> 44.5 us
  waiting for transfers between devices: 49.2 us -> 52.2 us
    pallas_call x0 -> x5, Pallas kernels: none -> 67.8 us  [the longest x1 22.7 us: two_chips(): kernel_call(functools.partial(far_gradients, sources, cap), local, block_...]
    dot_general x18 -> x0, matrix products: 60.3 us -> none  [the longest x2 16.1 us: backward(): jnp.einsum('erd,efd->erf', out_grad, down_rows, preferred_element_type=F32)]
    add x6 -> x3, other arithmetic: 15.5 us -> 0.6 us  [the longest x1 0.6 us: two_chips(): prob_gradient + jnp.sum(jnp.where(hit, prob_arrived[s][None], 0.0), axis=1)]
    unnamed x87 -> x40, local copies, waits for them, and re-layouts: 32 us -> 19.9 us
    ppermute x15, waiting for transfers between devices: 39.1 us -> 43.7 us  [to_source(): return lax.ppermute(values, 'expert', step) if shift else values]
    dynamic_slice x4 -> x0, local copies, waits for them, and re-layouts: 4.41 us -> none  [columns(): lax.dynamic_slice_in_dim(values, (place * CORES + side) * size, size, 2)]
    ppermute x15, starting transfers between devices: 38.5 us -> 35.7 us  [to_source(): return lax.ppermute(values, 'expert', step) if shift else values]
    convert_element_type x9 -> x3, other arithmetic: 5.1 us -> 4.49 us  [the longest x2 3.8 us: added(): sum([a.astype(F32) for a in arrived[1:]], arrived[0].astype(F32)).astype(BF)]
  transfers between devices with their start and end apart: 25 -> 25, of which waited for: 7 -> 10; matrix products, arithmetic and copies ran while one was open for 49% -> 13% of each run, Pallas kernels for 0% -> 20%
where the time goes in v1:
time: 193 us; the launch traced here: 192 us
  Pallas kernels  67.8 us (35%)
  waiting for transfers between devices  52.2 us (27%)
  starting transfers between devices  44.5 us (23%)
  local copies, waits for them, and re-layouts  19.9 us (10%)
  other arithmetic  6.99 us (4%)
    ppermute x15, waiting for transfers between devices, to_source(): return lax.ppermute(values, 'expert', step) if shift else values  43.7 us
    ppermute x15, starting transfers between devices, to_source(): return lax.ppermute(values, 'expert', step) if shift else values  35.7 us
    pallas_call x1, Pallas kernels, two_chips(): kernel_call(functools.partial(far_gradients, sources, cap), local, block_...  22.7 us
    unnamed x40, local copies, waits for them, and re-layouts  19.9 us
    pallas_call x1, Pallas kernels, two_chips(): kernel_call(functools.partial(own_backward, sources, cap), local, block_s...  17.1 us
    pallas_call x1, Pallas kernels, two_chips(): kernel_call(functools.partial(own_forward, sources, cap), local, block_sp...  16.3 us
    pallas_call x2, Pallas kernels, final(): pl.pallas_call(functools.partial(joined, local), grid=(rows // cut,), in_...  11.7 us
    ppermute x8, waiting for transfers between devices, to_chip(): return lax.ppermute(values, 'replica', step)  8.45 us
  transfers between devices with their start and end apart: 25, of which 10 were waited for; matrix products, arithmetic and copies ran while one was open for 13% of the time, Pallas kernels for 20%

profile of v1, /device:TPU:0, one launch (start us, length us, event | category | flops | bytes accessed | tf_op | source)
XLA Modules:
  0.0 192.2 jit_solution(3998783188281024593)
XLA Ops:
  0.6 3.1 %collective-permute-start.6 = (bf16[128,1024]{1,0:T(8,128)(2,1)}, bf16[128,1024]{1,0:T(8,128)(2,1)}, u32[]{:S(2)}, u32[]{:S(2)}) collective-permute-start(bf16[128,1024]{1,0:T(8,128)(2,1)} %refs_0_.1), channel_id=1, source_target_pairs={{0,4},{4,8},{8,12},{12,0},{1,5},{5,9},{9,13},{13,1},{2,6},{6,10},{... | collective-permute-start | bytes 786440 | tf_op jit(solution)/shard_map/ppermute | solution.py:378
  4.4 1.1 fusion.4.refs_0_.refs_4_
  5.6 1.6 collective-permute-start
  7.2 1.1 collective-permute-start.1
  8.3 2.8 %collective-permute-start.2 = (bf16[144,1024]{1,0:T(8,128)(2,1)S(1)}, bf16[144,1024]{1,0:T(8,128)(2,1)S(1)}, u32[]{:S(2)}, u32[]{:S(2)}) collective-permute-start(bf16[144,1024]{1,0:T(8,128)(2,1)S(1)} %fusion.4.refs_0_.refs_4_), channel_id=1, source_target_pairs={{0,12},{4,0},{8,4},{12,8},{1,13},{5,1},{9,5},{13,9},{2,14},{6,2},{... | collective-permute-start | bytes 884744 | tf_op jit(solution)/shard_map/ppermute | solution.py:378
  11.5 1.9 %collective-permute-done.6.refs_1_ = bf16[128,1024]{1,0:T(8,128)(2,1)} collective-permute-done((bf16[128,1024]{1,0:T(8,128)(2,1)}, bf16[128,1024]{1,0:T(8,128)(2,1)}, u32[]{:S(2)}, u32[]{:S(2)}) %collective-permute-start.6) | collective-permute-done | bytes 262176 | tf_op jit(solution)/shard_map/ppermute | solution.py:378
  13.4 1.8 collective-permute-start.8
  15.3 12.7 %copy.17 = bf16[1024,4,1536]{2,0,1:T(8,128)(2,1)} copy(bf16[1024,4,1536]{2,1,0:T(4,128)(2,1)} %param.10) | data formatting | bytes 25165824 | tf_op args[4]
  27.9 4.8 %copy.18 = bf16[768,4,1024]{2,0,1:T(8,128)(2,1)} copy(bf16[768,4,1024]{2,1,0:T(4,128)(2,1)S(1)} %bitcast.29) | data formatting | bytes 12582912 | tf_op args[5]
  33.4 15.7 %collective-permute-done.7.refs_2_ = bf16[128,1024]{1,0:T(8,128)(2,1)} collective-permute-done((bf16[128,1024]{1,0:T(8,128)(2,1)}, bf16[128,1024]{1,0:T(8,128)(2,1)}, u32[]{:S(2)}, u32[]{:S(2)}) %collective-permute-start.7) | collective-permute-done | bytes 262176 | tf_op jit(solution)/shard_map/ppermute | solution.py:378
  49.1 1.5 collective-permute-start.15
  51.1 1.5 collective-permute-start.20
  53.2 1.5 collective-permute-start.22
  54.7 16.3 %shard_map.101 = (bf16[128,1024]{1,0:T(8,128)(2,1)}, bf16[128,1024]{1,0:T(8,128)(2,1)}, bf16[128,1024]{1,0:T(8,128)(2,1)}, bf16[128,1024]{1,0:T(8,128)(2,1)}, bf...) custom-call(s32[3]{0:T(128)} %pad_add_fusion.info, ...), custom_call_target="tpu_custom_call" | custom-call | flops 6442450944 | bytes 37748736 | tf_op jit(solution)/shard_map/pallas_call | solution.py:419
  71.7 1.4 collective-permute-start.17
  73.7 17.1 %shard_map.102 = (bf16[128,1024]{1,0:T(8,128)(2,1)}, bf16[128,1024]{1,0:T(8,128)(2,1)}, bf16[128,1024]{1,0:T(8,128)(2,1)}, bf16[128,1024]{1,0:T(8,128)(2,1)}, f3...) custom-call(s32[3]{0:T(128)} %pad_add_fusion.info, bf16[128,1024]{1,0:T(8,128)(2,1)} %refs_0_.1, ...), custom_call_target="tpu_custom_call" | custom-call | flops 6442450944 | bytes 37748736 | tf_op jit(solution)/shard_map/pallas_call | solution.py:438
  90.9 3.2 %collective-permute-done.17.refs_2_.refs_6_ = bf16[144,1024]{1,0:T(8,128)(2,1)S(1)} collective-permute-done((bf16[144,1024]{1,0:T(8,128)(2,1)}, bf16[144,1024]{1,0:T(8,128)(2,1)S(1)}, u32[]{:S(2)}, u32[]{:S(2)}) %collective-permute-start.17) | collective-permute-done | bytes 294944 | tf_op jit(solution)/shard_map/ppermute | solution.py:385
  94.1 5.3 %collective-permute-done.18.refs_3_.refs_7_ = bf16[144,1024]{1,0:T(8,128)(2,1)S(1)} collective-permute-done((bf16[144,1024]{1,0:T(8,128)(2,1)}, bf16[144,1024]{1,0:T(8,128)(2,1)S(1)}, u32[]{:S(2)}, u32[]{:S(2)}) %collective-permute-start.18) | collective-permute-done | bytes 294944 | tf_op jit(solution)/shard_map/ppermute | solution.py:385
  100.1 22.7 %shard_map.103 = (f32[4,256,1536]{2,1,0:T(8,128)}, bf16[4,256,1536]{2,1,0:T(8,128)(2,1)}, f32[4,192,1024]{2,1,0:T(8,128)}, bf16[4,192,1024]{2,1,0:T(8,128)(2,1)}) custom-call(s32[3]{0:T(128)} %pad_add_fusion.info, bf16[144,1024]{1,0:T(8,128)(2,1)} %copy-done.9, bf16[144,1024]{1,0:T(8,128)(2,1)} %copy-done.10, bf16[144,1024]{1,0:T(8,128)(2,1)} %copy-done.11, ...), custom_call_target="tpu_custom_call" | custom-call | flops 9663676416 | bytes 56623104 | tf_op jit(solution)/shard_map/pallas_call | solution.py:454
  123.4 6.1 %collective-permute-start.12 = (f32[4,128]{1,0:T(4,128)S(1)}, f32[4,128]{1,0:T(4,128)S(1)}, u32[]{:S(2)}, u32[]{:S(2)}) collective-permute-start(f32[4,128]{1,0:T(4,128)S(1)} %get-tuple-element.50), channel_id=1, source_target_pairs={{0,12},{4,0},{8,4},{12,8},{1,13},{5,1},{9,5},{13,9},{2,14},{6,2},{... | collective-permute-start | bytes 6152 | tf_op jit(solution)/shard_map/ppermute | solution.py:378
  130.8 2.2 %collective-permute-start.5 = (bf16[128,1024]{1,0:T(8,128)(2,1)}, bf16[128,1024]{1,0:T(8,128)(2,1)}, u32[]{:S(2)}, u32[]{:S(2)}) collective-permute-start(bf16[128,1024]{1,0:T(8,128)(2,1)} %get-tuple-element.27), channel_id=1, source_target_pairs={{0,4},{4,8},{8,12},{12,0},{1,5},{5,9},{9,13},{13,1},{2,6},{6,10},{... | collective-permute-start | bytes 786440 | tf_op jit(solution)/shard_map/ppermute | solution.py:378
  134.0 1.5 collective-permute-start.4
  135.6 6.9 %collective-permute-done.5 = bf16[128,1024]{1,0:T(8,128)(2,1)} collective-permute-done((bf16[128,1024]{1,0:T(8,128)(2,1)}, bf16[128,1024]{1,0:T(8,128)(2,1)}, u32[]{:S(2)}, u32[]{:S(2)}) %collective-permute-start.5) | collective-permute-done | bytes 262176 | tf_op jit(solution)/shard_map/ppermute | solution.py:378
  142.5 11.2 %collective-permute-done.4 = bf16[128,1024]{1,0:T(8,128)(2,1)} collective-permute-done((bf16[128,1024]{1,0:T(8,128)(2,1)}, bf16[128,1024]{1,0:T(8,128)(2,1)}, u32[]{:S(2)}, u32[]{:S(2)}) %collective-permute-start.4) | collective-permute-done | bytes 262176 | tf_op jit(solution)/shard_map/ppermute | solution.py:378
  153.7 14.4 %collective-permute-start.9 = (bf16[128,1024]{1,0:T(8,128)(2,1)}, bf16[128,1024]{1,0:T(8,128)(2,1)S(1)}, u32[]{:S(2)}, u32[]{:S(2)}) collective-permute-start(bf16[128,1024]{1,0:T(8,128)(2,1)} %get-tuple-element.31), channel_id=1, source_target_pairs={{0,12},{4,0},{8,4},{12,8},{1,13},{5,1},{9,5},{13,9},{2,14},{6,2},{... | collective-permute-start | bytes 786440 | tf_op jit(solution)/shard_map/ppermute | solution.py:378
  168.8 2.0 %add_convert_fusion.1 = bf16[128,1024]{1,0:T(8,128)(2,1)} fusion(bf16[128,1024]{1,0:T(8,128)(2,1)} %collective-permute-done.5, bf16[128,1024]{1,0:T(8,128)(2,1)} %collective-permute-done.4, bf16[128,1024]{1,0:T(8,128)(2,1)} %collective-permute-done.3, bf16[128,1024]{1,0:T(8,128)(2,1)S(1)} %copy-done.6), kind=kLoop, calls=%fused_computation.9 | loop fusion | flops 1048576 | bytes 1310720 | tf_op jit(solution)/shard_map/convert_element_type | solution.py:434
  170.7 3.6 %collective-permute-done.10 = bf16[128,1024]{1,0:T(8,128)(2,1)S(1)} collective-permute-done((bf16[128,1024]{1,0:T(8,128)(2,1)}, bf16[128,1024]{1,0:T(8,128)(2,1)S(1)}, u32[]{:S(2)}, u32[]{:S(2)}) %collective-permute-start.10) | collective-permute-done | bytes 262176 | tf_op jit(solution)/shard_map/ppermute | solution.py:378
  174.4 2.7 %collective-permute-done.9 = bf16[128,1024]{1,0:T(8,128)(2,1)S(1)} collective-permute-done((bf16[128,1024]{1,0:T(8,128)(2,1)}, bf16[128,1024]{1,0:T(8,128)(2,1)S(1)}, u32[]{:S(2)}, u32[]{:S(2)}) %collective-permute-start.9) | collective-permute-done | bytes 262176 | tf_op jit(solution)/shard_map/ppermute | solution.py:378
  177.1 1.8 add_convert_fusion
  178.9 4.7 %shard_map.105 = f32[192,4,1024]{2,1,0:T(4,128)} custom-call(f32[4,192,1024]{2,1,0:T(8,128)} %get-tuple-element.41.own_ref, bf16[4,192,1024]{2,1,0:T(8,128)(2,1)} %collective-permute-done.24.share_ref), custom_call_target="tpu_custom_call" | custom-call | bytes 7864320 | tf_op jit(solution)/shard_map/pallas_call | solution.py:487
  183.6 1.6 copy-done
  185.2 7.0 %shard_map.104 = f32[256,4,1536]{2,1,0:T(4,128)} custom-call(f32[4,256,1536]{2,1,0:T(8,128)} %get-tuple-element.39.own_ref, bf16[4,256,1536]{2,1,0:T(8,128)(2,1)} %copy-done), custom_call_target="tpu_custom_call" | custom-call | bytes 15728640 | tf_op jit(solution)/shard_map/pallas_call | solution.py:487
  (74 shorter events, 8.5 us)
Async XLA Ops:
  0.6 12.8 %collective-permute-start.6 = (bf16[128,1024]{1,0:T(8,128)(2,1)}, bf16[128,1024]{1,0:T(8,128)(2,1)}, u32[]{:S(2)}, u32[]{:S(2)}) collective-permute-start(bf16[128,1024]{1,0:T(8,128)(2,1)} %refs_0_.1), channel_id=1, source_target_pairs={{0,4},{4,8},{8,12},{12,0},{1,5},{5,9},{9,13},{13,1},{2,6},{6,10},{... | collective-permute-start | bytes 786440 | tf_op jit(solution)/shard_map/ppermute | solution.py:378
  4.4 23.5 %slice-start = ((s8[6291456]{0:T(1024)(128)(4,1)}), s8[2097152]{0:T(1024)(128)(4,1)S(1)}, s32[]{:S(2)}) async-start(s8[6291456]{0:T(1024)(128)(4,1)} %bitcast.28), calls=%async_computation | async-start | bytes 4194304
  5.6 43.5 %copy-start.1 = (bf16[144,1024]{1,0:T(8,128)(2,1)}, bf16[144,1024]{1,0:T(8,128)(2,1)S(1)}, u32[]{:S(2)}) copy-start(bf16[144,1024]{1,0:T(8,128)(2,1)S(1)} %fusion.4.refs_0_.refs_4_) | copy-start | bytes 884740
  5.6 45.5 %collective-permute-start = (bf16[144,1024]{1,0:T(8,128)(2,1)S(1)}, bf16[144,1024]{1,0:T(8,128)(2,1)S(1)}, u32[]{:S(2)}, u32[]{:S(2)}) collective-permute-start(bf16[144,1024]{1,0:T(8,128)(2,1)S(1)} %fusion.4.refs_0_.refs_4_), channel_id=1, source_target_pairs={{0,4},{4,8},{8,12},{12,0},{1,5},{5,9},{9,13},{13,1},{2,6},{6,10},{... | collective-permute-start | bytes 884744 | tf_op jit(solution)/shard_map/ppermute | solution.py:378
  7.2 45.4 %collective-permute-start.1 = (bf16[144,1024]{1,0:T(8,128)(2,1)S(1)}, bf16[144,1024]{1,0:T(8,128)(2,1)S(1)}, u32[]{:S(2)}, u32[]{:S(2)}) collective-permute-start(bf16[144,1024]{1,0:T(8,128)(2,1)S(1)} %fusion.4.refs_0_.refs_4_), channel_id=1, source_target_pairs={{0,8},{4,12},{8,0},{12,4},{1,9},{5,13},{9,1},{13,5},{2,10},{6,14},... | collective-permute-start | bytes 884744 | tf_op jit(solution)/shard_map/ppermute | solution.py:378
  8.3 44.9 %collective-permute-start.2 = (bf16[144,1024]{1,0:T(8,128)(2,1)S(1)}, bf16[144,1024]{1,0:T(8,128)(2,1)S(1)}, u32[]{:S(2)}, u32[]{:S(2)}) collective-permute-start(bf16[144,1024]{1,0:T(8,128)(2,1)S(1)} %fusion.4.refs_0_.refs_4_), channel_id=1, source_target_pairs={{0,12},{4,0},{8,4},{12,8},{1,13},{5,1},{9,5},{13,9},{2,14},{6,2},{... | collective-permute-start | bytes 884744 | tf_op jit(solution)/shard_map/ppermute | solution.py:378
  11.1 37.9 %collective-permute-start.7 = (bf16[128,1024]{1,0:T(8,128)(2,1)}, bf16[128,1024]{1,0:T(8,128)(2,1)}, u32[]{:S(2)}, u32[]{:S(2)}) collective-permute-start(bf16[128,1024]{1,0:T(8,128)(2,1)} %refs_0_.1), channel_id=1, source_target_pairs={{0,8},{4,12},{8,0},{12,4},{1,9},{5,13},{9,1},{13,5},{2,10},{6,14},... | collective-permute-start | bytes 786440 | tf_op jit(solution)/shard_map/ppermute | solution.py:378
  13.4 37.1 %collective-permute-start.8 = (bf16[128,1024]{1,0:T(8,128)(2,1)}, bf16[128,1024]{1,0:T(8,128)(2,1)}, u32[]{:S(2)}, u32[]{:S(2)}) collective-permute-start(bf16[128,1024]{1,0:T(8,128)(2,1)} %refs_0_.1), channel_id=1, source_target_pairs={{0,12},{4,0},{8,4},{12,8},{1,13},{5,1},{9,5},{13,9},{2,14},{6,2},{... | collective-permute-start | bytes 786440 | tf_op jit(solution)/shard_map/ppermute | solution.py:378
  27.9 22.7 %copy-start.5 = (bf16[128,1024]{1,0:T(8,128)(2,1)S(1)}, bf16[128,1024]{1,0:T(8,128)(2,1)}, u32[]{:S(2)}) copy-start(bf16[128,1024]{1,0:T(8,128)(2,1)} %refs_0_.1) | copy-start | bytes 786436
  49.1 22.6 %collective-permute-start.15 = (bf16[144,1024]{1,0:T(8,128)(2,1)S(1)}, bf16[144,1024]{1,0:T(8,128)(2,1)S(1)}, u32[]{:S(2)}, u32[]{:S(2)}) collective-permute-start(bf16[144,1024]{1,0:T(8,128)(2,1)S(1)} %fusion.4.refs_0_.refs_4_), channel_id=1, source_target_pairs={{0,2},{1,3},{2,0},{3,1},{4,6},{5,7},{6,4},{7,5},{8,10},{9,11},{10,... | collective-permute-start | bytes 884744 | tf_op jit(solution)/shard_map/ppermute | solution.py:385
  50.6 20.4 %collective-permute-start.19 = (bf16[128,1024]{1,0:T(8,128)(2,1)S(1)}, bf16[128,1024]{1,0:T(8,128)(2,1)S(1)}, u32[]{:S(2)}, u32[]{:S(2)}) collective-permute-start(bf16[128,1024]{1,0:T(8,128)(2,1)S(1)} %copy-done.5), channel_id=1, source_target_pairs={{0,2},{1,3},{2,0},{3,1},{4,6},{5,7},{6,4},{7,5},{8,10},{9,11},{10,... | collective-permute-start | bytes 786440 | tf_op jit(solution)/shard_map/ppermute | solution.py:385
  51.1 21.9 %collective-permute-start.20 = (bf16[128,1024]{1,0:T(8,128)(2,1)}, bf16[128,1024]{1,0:T(8,128)(2,1)S(1)}, u32[]{:S(2)}, u32[]{:S(2)}) collective-permute-start(bf16[128,1024]{1,0:T(8,128)(2,1)} %collective-permute-done.6.refs_1_), channel_id=1, source_target_pairs={{0,2},{1,3},{2,0},{3,1},{4,6},{5,7},{6,4},{7,5},{8,10},{9,11},{10,... | collective-permute-start | bytes 786440 | tf_op jit(solution)/shard_map/ppermute | solution.py:385
  52.6 38.2 %collective-permute-start.21 = (bf16[128,1024]{1,0:T(8,128)(2,1)}, bf16[128,1024]{1,0:T(8,128)(2,1)S(1)}, u32[]{:S(2)}, u32[]{:S(2)}) collective-permute-start(bf16[128,1024]{1,0:T(8,128)(2,1)} %collective-permute-done.7.refs_2_), channel_id=1, source_target_pairs={{0,2},{1,3},{2,0},{3,1},{4,6},{5,7},{6,4},{7,5},{8,10},{9,11},{10,... | collective-permute-start | bytes 786440 | tf_op jit(solution)/shard_map/ppermute | solution.py:385
  53.2 37.7 %collective-permute-start.22 = (bf16[128,1024]{1,0:T(8,128)(2,1)}, bf16[128,1024]{1,0:T(8,128)(2,1)S(1)}, u32[]{:S(2)}, u32[]{:S(2)}) collective-permute-start(bf16[128,1024]{1,0:T(8,128)(2,1)} %collective-permute-done.8.refs_3_), channel_id=1, source_target_pairs={{0,2},{1,3},{2,0},{3,1},{4,6},{5,7},{6,4},{7,5},{8,10},{9,11},{10,... | collective-permute-start | bytes 786440 | tf_op jit(solution)/shard_map/ppermute | solution.py:385
  71.0 19.9 %copy-start.13 = (bf16[128,1024]{1,0:T(8,128)(2,1)}, bf16[128,1024]{1,0:T(8,128)(2,1)S(1)}, u32[]{:S(2)}) copy-start(bf16[128,1024]{1,0:T(8,128)(2,1)S(1)} %collective-permute-done.19.refs_8_) | copy-start | bytes 786436
  71.0 19.9 %collective-permute-start.16 = (bf16[144,1024]{1,0:T(8,128)(2,1)}, bf16[144,1024]{1,0:T(8,128)(2,1)S(1)}, u32[]{:S(2)}, u32[]{:S(2)}) collective-permute-start(bf16[144,1024]{1,0:T(8,128)(2,1)} %copy-done.2), channel_id=1, source_target_pairs={{0,2},{1,3},{2,0},{3,1},{4,6},{5,7},{6,4},{7,5},{8,10},{9,11},{10,... | collective-permute-start | bytes 884744 | tf_op jit(solution)/shard_map/ppermute | solution.py:385
  71.7 22.4 %collective-permute-start.17 = (bf16[144,1024]{1,0:T(8,128)(2,1)}, bf16[144,1024]{1,0:T(8,128)(2,1)S(1)}, u32[]{:S(2)}, u32[]{:S(2)}) collective-permute-start(bf16[144,1024]{1,0:T(8,128)(2,1)} %copy-done.3), channel_id=1, source_target_pairs={{0,2},{1,3},{2,0},{3,1},{4,6},{5,7},{6,4},{7,5},{8,10},{9,11},{10,... | collective-permute-start | bytes 884744 | tf_op jit(solution)/shard_map/ppermute | solution.py:385
  73.1 26.3 %collective-permute-start.18 = (bf16[144,1024]{1,0:T(8,128)(2,1)}, bf16[144,1024]{1,0:T(8,128)(2,1)S(1)}, u32[]{:S(2)}, u32[]{:S(2)}) collective-permute-start(bf16[144,1024]{1,0:T(8,128)(2,1)} %copy-done.4), channel_id=1, source_target_pairs={{0,2},{1,3},{2,0},{3,1},{4,6},{5,7},{6,4},{7,5},{8,10},{9,11},{10,... | collective-permute-start | bytes 884744 | tf_op jit(solution)/shard_map/ppermute | solution.py:385
  100.0 23.3 %copy-start.8 = (f32[4,4,128]{2,1,0:T(4,128)S(1)}, f32[4,4,128]{2,1,0:T(4,128)}, u32[]{:S(2)}) copy-start(f32[4,4,128]{2,1,0:T(4,128)} %get-tuple-element.34) | copy-start | bytes 24580
  100.1 35.4 %copy-start.7 = (s32[128,6]{0,1:T(8,128)S(1)}, s32[128,6]{0,1:T(8,128)}, u32[]{:S(2)}) copy-start(s32[128,6]{0,1:T(8,128)} %param.7) | copy-start | bytes 9220
  100.1 68.7 %copy-start.6 = (bf16[128,1024]{1,0:T(8,128)(2,1)S(1)}, bf16[128,1024]{1,0:T(8,128)(2,1)}, u32[]{:S(2)}) copy-start(bf16[128,1024]{1,0:T(8,128)(2,1)} %get-tuple-element.24) | copy-start | bytes 786436
  122.8 60.8 %collective-permute-start.23 = (bf16[4,256,1536]{2,1,0:T(8,128)(2,1)}, bf16[4,256,1536]{2,1,0:T(8,128)(2,1)S(1)}, u32[]{:S(2)}, u32[]{:S(2)}) collective-permute-start(bf16[4,256,1536]{2,1,0:T(8,128)(2,1)} %get-tuple-element.40), channel_id=1, source_target_pairs={{0,1},{1,0},{2,3},{3,2},{4,5},{5,4},{6,7},{7,6},{8,9},{9,8},{10,11... | collective-permute-start | bytes 9437192 | tf_op jit(solution)/shard_map/ppermute | solution.py:484
  122.9 56.0 %collective-permute-start.24 = (bf16[4,192,1024]{2,1,0:T(8,128)(2,1)}, bf16[4,192,1024]{2,1,0:T(8,128)(2,1)}, u32[]{:S(2)}, u32[]{:S(2)}) collective-permute-start(bf16[4,192,1024]{2,1,0:T(8,128)(2,1)} %get-tuple-element.42), channel_id=1, source_target_pairs={{0,1},{1,0},{2,3},{3,2},{4,5},{5,4},{6,7},{7,6},{8,9},{9,8},{10,11... | collective-permute-start | bytes 4718600 | tf_op jit(solution)/shard_map/ppermute | solution.py:484
  123.4 7.4 %collective-permute-start.12 = (f32[4,128]{1,0:T(4,128)S(1)}, f32[4,128]{1,0:T(4,128)S(1)}, u32[]{:S(2)}, u32[]{:S(2)}) collective-permute-start(f32[4,128]{1,0:T(4,128)S(1)} %get-tuple-element.50), channel_id=1, source_target_pairs={{0,12},{4,0},{8,4},{12,8},{1,13},{5,1},{9,5},{13,9},{2,14},{6,2},{... | collective-permute-start | bytes 6152 | tf_op jit(solution)/shard_map/ppermute | solution.py:378
  129.5 4.5 %collective-permute-start.13 = (f32[4,128]{1,0:T(4,128)S(1)}, f32[4,128]{1,0:T(4,128)S(1)}, u32[]{:S(2)}, u32[]{:S(2)}) collective-permute-start(f32[4,128]{1,0:T(4,128)S(1)} %get-tuple-element.49), channel_id=1, source_target_pairs={{0,8},{4,12},{8,0},{12,4},{1,9},{5,13},{9,1},{13,5},{2,10},{6,14},... | collective-permute-start | bytes 6152 | tf_op jit(solution)/shard_map/ppermute | solution.py:378
  129.5 6.0 %collective-permute-start.14 = (f32[4,128]{1,0:T(4,128)S(1)}, f32[4,128]{1,0:T(4,128)S(1)}, u32[]{:S(2)}, u32[]{:S(2)}) collective-permute-start(f32[4,128]{1,0:T(4,128)S(1)} %get-tuple-element.48), channel_id=1, source_target_pairs={{0,4},{4,8},{8,12},{12,0},{1,5},{5,9},{9,13},{13,1},{2,6},{6,10},{... | collective-permute-start | bytes 6152 | tf_op jit(solution)/shard_map/ppermute | solution.py:378
  130.8 11.7 %collective-permute-start.5 = (bf16[128,1024]{1,0:T(8,128)(2,1)}, bf16[128,1024]{1,0:T(8,128)(2,1)}, u32[]{:S(2)}, u32[]{:S(2)}) collective-permute-start(bf16[128,1024]{1,0:T(8,128)(2,1)} %get-tuple-element.27), channel_id=1, source_target_pairs={{0,4},{4,8},{8,12},{12,0},{1,5},{5,9},{9,13},{13,1},{2,6},{6,10},{... | collective-permute-start | bytes 786440 | tf_op jit(solution)/shard_map/ppermute | solution.py:378
  134.0 19.8 %collective-permute-start.4 = (bf16[128,1024]{1,0:T(8,128)(2,1)}, bf16[128,1024]{1,0:T(8,128)(2,1)}, u32[]{:S(2)}, u32[]{:S(2)}) collective-permute-start(bf16[128,1024]{1,0:T(8,128)(2,1)} %get-tuple-element.26), channel_id=1, source_target_pairs={{0,8},{4,12},{8,0},{12,4},{1,9},{5,13},{9,1},{13,5},{2,10},{6,14},... | collective-permute-start | bytes 786440 | tf_op jit(solution)/shard_map/ppermute | solution.py:378
  135.5 18.3 %collective-permute-start.3 = (bf16[128,1024]{1,0:T(8,128)(2,1)}, bf16[128,1024]{1,0:T(8,128)(2,1)}, u32[]{:S(2)}, u32[]{:S(2)}) collective-permute-start(bf16[128,1024]{1,0:T(8,128)(2,1)} %get-tuple-element.25), channel_id=1, source_target_pairs={{0,12},{4,0},{8,4},{12,8},{1,13},{5,1},{9,5},{13,9},{2,14},{6,2},{... | collective-permute-start | bytes 786440 | tf_op jit(solution)/shard_map/ppermute | solution.py:378
  142.5 28.3 %collective-permute-start.11 = (bf16[128,1024]{1,0:T(8,128)(2,1)}, bf16[128,1024]{1,0:T(8,128)(2,1)S(1)}, u32[]{:S(2)}, u32[]{:S(2)}) collective-permute-start(bf16[128,1024]{1,0:T(8,128)(2,1)} %get-tuple-element.33), channel_id=1, source_target_pairs={{0,4},{4,8},{8,12},{12,0},{1,5},{5,9},{9,13},{13,1},{2,6},{6,10},{... | collective-permute-start | bytes 786440 | tf_op jit(solution)/shard_map/ppermute | solution.py:378
  153.7 20.7 %collective-permute-start.10 = (bf16[128,1024]{1,0:T(8,128)(2,1)}, bf16[128,1024]{1,0:T(8,128)(2,1)S(1)}, u32[]{:S(2)}, u32[]{:S(2)}) collective-permute-start(bf16[128,1024]{1,0:T(8,128)(2,1)} %get-tuple-element.32), channel_id=1, source_target_pairs={{0,8},{4,12},{8,0},{12,4},{1,9},{5,13},{9,1},{13,5},{2,10},{6,14},... | collective-permute-start | bytes 786440 | tf_op jit(solution)/shard_map/ppermute | solution.py:378
  153.7 23.3 %collective-permute-start.9 = (bf16[128,1024]{1,0:T(8,128)(2,1)}, bf16[128,1024]{1,0:T(8,128)(2,1)S(1)}, u32[]{:S(2)}, u32[]{:S(2)}) collective-permute-start(bf16[128,1024]{1,0:T(8,128)(2,1)} %get-tuple-element.31), channel_id=1, source_target_pairs={{0,12},{4,0},{8,4},{12,8},{1,13},{5,1},{9,5},{13,9},{2,14},{6,2},{... | collective-permute-start | bytes 786440 | tf_op jit(solution)/shard_map/ppermute | solution.py:378
  (12 other events, 89.7 us)

commit v2 on v1

--- a/solution.py
+++ b/solution.py
@@ -168,17 +168,17 @@
     return (combined, token_gradient, prob_gradient, gate_up_gradient, down_gradient)
 
 
-NOTES = 16
 HALF = 8
+FWD, BWD, FAR, JOIN = 16, 16, 24, 8
 
 
 def routing_tile(note_refs, expert, count, cap):
     members, weights = [], []
     for ref in note_refs:
         tile = ref[...].astype(F32)
-        named = tile[:HALF].astype(jnp.int32) == expert
+        named = tile[:, :count].astype(jnp.int32) == expert
         members.append(jnp.max(jnp.where(named, 1.0, 0.0), axis=0, keepdims=True))
-        weights.append(jnp.sum(jnp.where(named, tile[HALF:], 0.0), axis=0, keepdims=True))
+        weights.append(jnp.sum(jnp.where(named, tile[:, count:], 0.0), axis=0, keepdims=True))
     member = jnp.concatenate(members, axis=0)
     ahead = (
         lax.broadcasted_iota(jnp.int32, (count, count), 0) < lax.broadcasted_iota(jnp.int32, (count, count), 1)
@@ -347,14 +347,14 @@
     return pl.BlockSpec((1,) + shape, lambda e, info: (e,) + (0,) * len(shape))
 
 
-def kernel_call(body, grid, in_specs, out_specs, out_shape, scratch, flops, moved):
+def kernel_call(body, grid, in_specs, out_specs, out_shape, scratch, flops, moved, grant):
     return pl.pallas_call(
         body,
         grid_spec=pltpu.PrefetchScalarGridSpec(
             num_scalar_prefetch=1, grid=(grid,), in_specs=in_specs, out_specs=out_specs, scratch_shapes=scratch
         ),
         out_shape=out_shape,
-        compiler_params=pltpu.CompilerParams(vmem_limit_bytes=56 << 20),
+        compiler_params=pltpu.CompilerParams(vmem_limit_bytes=grant << 20),
         cost_estimate=pl.CostEstimate(flops=flops, bytes_accessed=moved, transcendentals=0),
     )
 
@@ -384,10 +384,11 @@
         ]
         return lax.ppermute(values, "replica", step)
 
-    fill = ((0, HALF - top), (0, width - count))
-    packed = jnp.concatenate(
-        [tokens, jnp.pad(expert_ids.T.astype(BF), fill, constant_values=-1), jnp.pad(gate_probs.T, fill)], axis=0
-    )
+    fill = ((0, HALF - top), (0, 0))
+    notes = jnp.concatenate(
+        [jnp.pad(expert_ids.T.astype(BF), fill, constant_values=-1), jnp.pad(gate_probs.T, fill)], axis=1
+    )
+    packed = jnp.concatenate([tokens, jnp.pad(notes, ((0, 0), (0, width - 2 * count)))], axis=0)
 
     def gathered(values):
         far = [to_chip(values)]
@@ -405,7 +406,7 @@
     )
 
     block_specs = [whole(count, width)] * sources
-    note_specs = [pl.BlockSpec((NOTES, count), lambda e, info: (count // NOTES, 0))] * sources
+    note_specs = [pl.BlockSpec((HALF, 2 * count), lambda e, info: (count // HALF, 0))] * sources
     weight_specs = [each(width, pre_width), each(hidden_width, width)]
     block_shape = jax.ShapeDtypeStruct((count, width), BF)
     gathered_rows = pltpu.VMEM((sources * count, width), BF)
@@ -425,6 +426,7 @@
         [gathered_rows, part_total],
         4 * product,
         2 * weight_bytes,
+        FWD,
     )(info, *near_packed, *near_packed, gate_rows, down_rows)
 
     def returned(parts):
@@ -446,6 +448,7 @@
         [gathered_rows, part_total],
         4 * product,
         2 * weight_bytes,
+        BWD,
     )(info, *near_cots, *near_packed, gate_rows, down_rows, pre_act, outputs)
     prob_arrived = [to_source(prob_part[s], -s) for s in range(sources)]
     grad_arrived = returned(grad_parts)
@@ -473,6 +476,7 @@
         ],
         6 * product,
         3 * weight_bytes,
+        FAR,
     )(
         info, *far_packed, *far_packed, *far_cots, gate_rows, down_rows,
         inputs, hidden, out_grad, pre_grad,
@@ -490,7 +494,7 @@
             in_specs=[pl.BlockSpec((local, cut, size), lambda i: (0, i, 0))] * 2,
             out_specs=pl.BlockSpec((cut, local, size), lambda i: (i, 0, 0)),
             out_shape=jax.ShapeDtypeStruct((rows, local, size), F32),
-            compiler_params=pltpu.CompilerParams(vmem_limit_bytes=56 << 20),
+            compiler_params=pltpu.CompilerParams(vmem_limit_bytes=JOIN << 20),
             cost_estimate=pl.CostEstimate(flops=0, bytes_accessed=10 * own.size, transcendentals=0),
         )(own, theirs)
 
@@ -509,7 +513,7 @@
 def on_device(*args, sources, replicas):
     count, top, local = args[0].shape[0], args[1].shape[1], args[4].shape[1]
     small = sources * min(CAP, count) * local <= 1024 and sources <= 4
-    plain = replicas == 2 * CORES and small and count % 128 == 0 and top <= HALF
+    plain = replicas == 2 * CORES and small and count % 128 == 0 and top <= HALF and 2 * count <= args[0].shape[1]
     return (two_chips if plain else general)(*args, sources=sources, replicas=replicas)
 
 

time: 193 us -> 186 us (0.964)
  Pallas kernels: 67.8 us -> 50.7 us
  local copies, waits for them, and re-layouts: 19.9 us -> 32 us
    unnamed x40 -> x30, local copies, waits for them, and re-layouts: 19.9 us -> 32 us
    pallas_call x1, Pallas kernels: 16.3 us -> 9.48 us  [two_chips(): kernel_call(functools.partial(own_forward, sources, cap), local, block_sp...]
    pallas_call x1, Pallas kernels: 17.1 us -> 11.1 us  [two_chips(): kernel_call(functools.partial(own_backward, sources, cap), local, block_s...]
    pallas_call x1, Pallas kernels: 22.7 us -> 19.7 us  [two_chips(): kernel_call(functools.partial(far_gradients, sources, cap), local, block_...]
  transfers between devices with their start and end apart: 25 -> 25, of which waited for: 10 -> 10; matrix products, arithmetic and copies ran while one was open for 13% -> 13% of each run, Pallas kernels for 20% -> 14%
where the time goes in v2:
time: 186 us; the launch traced here: 185 us
  Pallas kernels  50.7 us (27%)
  waiting for transfers between devices  50.6 us (27%)
  starting transfers between devices  44.2 us (24%)
  local copies, waits for them, and re-layouts  32 us (17%)
  other arithmetic  6.93 us (4%)
    ppermute x15, waiting for transfers between devices, to_source(): return lax.ppermute(values, 'expert', step) if shift else values  42.1 us
    ppermute x15, starting transfers between devices, to_source(): return lax.ppermute(values, 'expert', step) if shift else values  35.6 us
    unnamed x30, local copies, waits for them, and re-layouts  32 us
    pallas_call x1, Pallas kernels, two_chips(): kernel_call(functools.partial(far_gradients, sources, cap), local, block_...  19.7 us
    pallas_call x1, Pallas kernels, two_chips(): kernel_call(functools.partial(own_backward, sources, cap), local, block_s...  11.1 us
    pallas_call x2, Pallas kernels, final(): pl.pallas_call(functools.partial(joined, local), grid=(rows // cut,), in_...  10.4 us
    pallas_call x1, Pallas kernels, two_chips(): kernel_call(functools.partial(own_forward, sources, cap), local, block_sp...  9.48 us
    ppermute x8, waiting for transfers between devices, to_chip(): return lax.ppermute(values, 'replica', step)  8.49 us
  transfers between devices with their start and end apart: 25, of which 10 were waited for; matrix products, arithmetic and copies ran while one was open for 13% of the time, Pallas kernels for 14%

profile of v2, /device:TPU:0, one launch (start us, length us, event | category | flops | bytes accessed | tf_op | source)
XLA Modules:
  0.0 185.2 jit_solution(2613309358834781023)
XLA Ops:
  0.6 3.1 %collective-permute-start.6 = (bf16[128,1024]{1,0:T(8,128)(2,1)}, bf16[128,1024]{1,0:T(8,128)(2,1)S(1)}, u32[]{:S(2)}, u32[]{:S(2)}) collective-permute-start(bf16[128,1024]{1,0:T(8,128)(2,1)} %refs_0_.1), channel_id=1, source_target_pairs={{0,4},{4,8},{8,12},{12,0},{1,5},{5,9},{9,13},{13,1},{2,6},{6,10},{... | collective-permute-start | bytes 786440 | tf_op jit(solution)/shard_map/ppermute | solution.py:378
  6.1 1.6 collective-permute-start
  8.8 2.8 %collective-permute-start.2 = (bf16[136,1024]{1,0:T(8,128)(2,1)S(1)}, bf16[136,1024]{1,0:T(8,128)(2,1)S(1)}, u32[]{:S(2)}, u32[]{:S(2)}) collective-permute-start(bf16[136,1024]{1,0:T(8,128)(2,1)S(1)} %fusion.1.refs_0_.refs_4_), channel_id=1, source_target_pairs={{0,12},{4,0},{8,4},{12,8},{1,13},{5,1},{9,5},{13,9},{2,14},{6,2},{... | collective-permute-start | bytes 835592 | tf_op jit(solution)/shard_map/ppermute | solution.py:378
  12.0 1.3 collective-permute-done.6.refs_1_
  13.3 1.8 collective-permute-start.8
  15.1 12.9 %copy.17 = bf16[1024,4,1536]{2,0,1:T(8,128)(2,1)} copy(bf16[1024,4,1536]{2,1,0:T(4,128)(2,1)} %param.10) | data formatting | bytes 25165824 | tf_op args[4]
  28.1 4.8 %copy.18 = bf16[768,4,1024]{2,0,1:T(8,128)(2,1)} copy(bf16[768,4,1024]{2,1,0:T(4,128)(2,1)S(1)} %copy-done.12) | data formatting | bytes 12582912 | tf_op args[5]
  33.0 14.6 %collective-permute-done.7.refs_2_ = bf16[128,1024]{1,0:T(8,128)(2,1)S(1)} collective-permute-done((bf16[128,1024]{1,0:T(8,128)(2,1)}, bf16[128,1024]{1,0:T(8,128)(2,1)S(1)}, u32[]{:S(2)}, u32[]{:S(2)}) %collective-permute-start.7) | collective-permute-done | bytes 262176 | tf_op jit(solution)/shard_map/ppermute | solution.py:378
  47.6 1.5 collective-permute-start.15
  49.6 1.5 collective-permute-start.20
  51.6 1.5 collective-permute-start.22
  53.1 4.6 %copy-done = bf16[1024,4,1536]{2,0,1:T(8,128)(2,1)S(1)} copy-done((bf16[1024,4,1536]{2,0,1:T(8,128)(2,1)S(1)}, bf16[1024,4,1536]{2,0,1:T(8,128)(2,1)}, u32[]{:S(2)}) %copy-start) | copy-done | bytes 12582936
  57.7 2.8 %copy-done.1 = bf16[768,4,1024]{2,0,1:T(8,128)(2,1)S(1)} copy-done((bf16[768,4,1024]{2,0,1:T(8,128)(2,1)S(1)}, bf16[768,4,1024]{2,0,1:T(8,128)(2,1)}, u32[]{:S(2)}) %copy-start.1) | copy-done | bytes 6291480
  60.5 9.5 %shard_map.101 = (bf16[128,1024]{1,0:T(8,128)(2,1)S(1)}, bf16[128,1024]{1,0:T(8,128)(2,1)S(1)}, bf16[128,1024]{1,0:T(8,128)(2,1)S(1)}, bf16[128,1024]{1,0:T(8,12...) custom-call(s32[3]{0:T(128)S(1)} %pad_add_fusion.info, ...), custom_call_target="tpu_custom_call" | custom-call | flops 6442450944 | bytes 37748736 | tf_op jit(solution)/shard_map/pallas_call | solution.py:420
  72.6 1.5 collective-permute-start.17
  74.7 11.1 %shard_map.102 = (bf16[128,1024]{1,0:T(8,128)(2,1)S(1)}, bf16[128,1024]{1,0:T(8,128)(2,1)S(1)}, bf16[128,1024]{1,0:T(8,128)(2,1)S(1)}, bf16[128,1024]{1,0:T(8,12...) custom-call(s32[3]{0:T(128)S(1)} %pad_add_fusion.info, ...), custom_call_target="tpu_custom_call" | custom-call | flops 6442450944 | bytes 37748736 | tf_op jit(solution)/shard_map/pallas_call | solution.py:440
  88.0 3.5 %collective-permute-done.17.refs_2_.refs_6_ = bf16[136,1024]{1,0:T(8,128)(2,1)S(1)} collective-permute-done((bf16[136,1024]{1,0:T(8,128)(2,1)S(1)}, bf16[136,1024]{1,0:T(8,128)(2,1)S(1)}, u32[]{:S(2)}, u32[]{:S(2)}) %collective-permute-start.17) | collective-permute-done | bytes 278560 | tf_op jit(solution)/shard_map/ppermute | solution.py:385
  91.5 4.9 %collective-permute-done.18.refs_3_.refs_7_ = bf16[136,1024]{1,0:T(8,128)(2,1)S(1)} collective-permute-done((bf16[136,1024]{1,0:T(8,128)(2,1)S(1)}, bf16[136,1024]{1,0:T(8,128)(2,1)S(1)}, u32[]{:S(2)}, u32[]{:S(2)}) %collective-permute-start.18) | collective-permute-done | bytes 278560 | tf_op jit(solution)/shard_map/ppermute | solution.py:385
  96.4 19.7 %shard_map.103 = (f32[4,256,1536]{2,1,0:T(8,128)S(1)}, bf16[4,256,1536]{2,1,0:T(8,128)(2,1)}, f32[4,192,1024]{2,1,0:T(8,128)S(1)}, bf16[4,192,1024]{2,1,0:T(8,128)(2,1)}) custom-call(s32[3]{0:T(128)S(1)} %pad_add_fusion.info, bf16[136,1024]{1,0:T(8,128)(2,1)S(1)} %collective-permute-done.15.refs_0_.refs_4_, ...), custom_call_target="tpu_custom_call" | custom-call | flops 9663676416 | bytes 56623104 | tf_op jit(solution)/shard_map/pallas_call | solution.py:457
  116.2 2.7 %copy-done.2 = f32[4,256,1536]{2,1,0:T(8,128)} copy-done((f32[4,256,1536]{2,1,0:T(8,128)}, f32[4,256,1536]{2,1,0:T(8,128)S(1)}, u32[]{:S(2)}) %copy-start.2) | copy-done | bytes 6291480
  119.4 6.1 %collective-permute-start.12 = (f32[4,128]{1,0:T(4,128)S(1)}, f32[4,128]{1,0:T(4,128)S(1)}, u32[]{:S(2)}, u32[]{:S(2)}) collective-permute-start(f32[4,128]{1,0:T(4,128)S(1)} %get-tuple-element.50), channel_id=1, source_target_pairs={{0,12},{4,0},{8,4},{12,8},{1,13},{5,1},{9,5},{13,9},{2,14},{6,2},{... | collective-permute-start | bytes 6152 | tf_op jit(solution)/shard_map/ppermute | solution.py:378
  126.8 2.2 %collective-permute-start.5 = (bf16[128,1024]{1,0:T(8,128)(2,1)}, bf16[128,1024]{1,0:T(8,128)(2,1)}, u32[]{:S(2)}, u32[]{:S(2)}) collective-permute-start(bf16[128,1024]{1,0:T(8,128)(2,1)} %copy-done.11), channel_id=1, source_target_pairs={{0,4},{4,8},{8,12},{12,0},{1,5},{5,9},{9,13},{13,1},{2,6},{6,10},{... | collective-permute-start | bytes 786440 | tf_op jit(solution)/shard_map/ppermute | solution.py:378
  130.0 1.5 collective-permute-start.4
  131.6 6.9 %collective-permute-done.5 = bf16[128,1024]{1,0:T(8,128)(2,1)} collective-permute-done((bf16[128,1024]{1,0:T(8,128)(2,1)}, bf16[128,1024]{1,0:T(8,128)(2,1)}, u32[]{:S(2)}, u32[]{:S(2)}) %collective-permute-start.5) | collective-permute-done | bytes 262176 | tf_op jit(solution)/shard_map/ppermute | solution.py:378
  138.5 11.2 %collective-permute-done.4 = bf16[128,1024]{1,0:T(8,128)(2,1)} collective-permute-done((bf16[128,1024]{1,0:T(8,128)(2,1)}, bf16[128,1024]{1,0:T(8,128)(2,1)}, u32[]{:S(2)}, u32[]{:S(2)}) %collective-permute-start.4) | collective-permute-done | bytes 262176 | tf_op jit(solution)/shard_map/ppermute | solution.py:378
  149.7 14.4 %collective-permute-start.9 = (bf16[128,1024]{1,0:T(8,128)(2,1)}, bf16[128,1024]{1,0:T(8,128)(2,1)S(1)}, u32[]{:S(2)}, u32[]{:S(2)}) collective-permute-start(bf16[128,1024]{1,0:T(8,128)(2,1)} %copy-done.7), channel_id=1, source_target_pairs={{0,12},{4,0},{8,4},{12,8},{1,13},{5,1},{9,5},{13,9},{2,14},{6,2},{... | collective-permute-start | bytes 786440 | tf_op jit(solution)/shard_map/ppermute | solution.py:378
  164.7 2.0 %add_convert_fusion.1 = bf16[128,1024]{1,0:T(8,128)(2,1)} fusion(bf16[128,1024]{1,0:T(8,128)(2,1)} %collective-permute-done.5, bf16[128,1024]{1,0:T(8,128)(2,1)} %collective-permute-done.4, bf16[128,1024]{1,0:T(8,128)(2,1)} %collective-permute-done.3, bf16[128,1024]{1,0:T(8,128)(2,1)S(1)} %get-tuple-element.24), kind=kLoop, calls=%fused_computation.5 | loop fusion | flops 1048576 | bytes 1310720 | tf_op jit(solution)/shard_map/convert_element_type | solution.py:436
  166.7 3.6 %collective-permute-done.10 = bf16[128,1024]{1,0:T(8,128)(2,1)S(1)} collective-permute-done((bf16[128,1024]{1,0:T(8,128)(2,1)}, bf16[128,1024]{1,0:T(8,128)(2,1)S(1)}, u32[]{:S(2)}, u32[]{:S(2)}) %collective-permute-start.10) | collective-permute-done | bytes 262176 | tf_op jit(solution)/shard_map/ppermute | solution.py:378
  170.3 2.7 %collective-permute-done.9 = bf16[128,1024]{1,0:T(8,128)(2,1)S(1)} collective-permute-done((bf16[128,1024]{1,0:T(8,128)(2,1)}, bf16[128,1024]{1,0:T(8,128)(2,1)S(1)}, u32[]{:S(2)}, u32[]{:S(2)}) %collective-permute-start.9) | collective-permute-done | bytes 262176 | tf_op jit(solution)/shard_map/ppermute | solution.py:378
  173.0 1.8 add_convert_fusion
  174.8 4.7 %shard_map.105 = f32[192,4,1024]{2,1,0:T(4,128)} custom-call(f32[4,192,1024]{2,1,0:T(8,128)S(1)} %get-tuple-element.41.own_ref, bf16[4,192,1024]{2,1,0:T(8,128)(2,1)} %collective-permute-done.24.share_ref), custom_call_target="tpu_custom_call" | custom-call | bytes 7864320 | tf_op jit(solution)/shard_map/pallas_call | solution.py:491
  179.5 5.7 %shard_map.104 = f32[256,4,1536]{2,1,0:T(4,128)} custom-call(f32[4,256,1536]{2,1,0:T(8,128)S(1)} %copy-done.3, bf16[4,256,1536]{2,1,0:T(8,128)(2,1)} %collective-permute-done.23.share_ref), custom_call_target="tpu_custom_call" | custom-call | bytes 15728640 | tf_op jit(solution)/shard_map/pallas_call | solution.py:491
  (64 shorter events, 13.8 us)
Async XLA Ops:
  0.6 12.7 %collective-permute-start.6 = (bf16[128,1024]{1,0:T(8,128)(2,1)}, bf16[128,1024]{1,0:T(8,128)(2,1)S(1)}, u32[]{:S(2)}, u32[]{:S(2)}) collective-permute-start(bf16[128,1024]{1,0:T(8,128)(2,1)} %refs_0_.1), channel_id=1, source_target_pairs={{0,4},{4,8},{8,12},{12,0},{1,5},{5,9},{9,13},{13,1},{2,6},{6,10},{... | collective-permute-start | bytes 786440 | tf_op jit(solution)/shard_map/ppermute | solution.py:378
  6.1 43.5 %collective-permute-start = (bf16[136,1024]{1,0:T(8,128)(2,1)S(1)}, bf16[136,1024]{1,0:T(8,128)(2,1)S(1)}, u32[]{:S(2)}, u32[]{:S(2)}) collective-permute-start(bf16[136,1024]{1,0:T(8,128)(2,1)S(1)} %fusion.1.refs_0_.refs_4_), channel_id=1, source_target_pairs={{0,4},{4,8},{8,12},{12,0},{1,5},{5,9},{9,13},{13,1},{2,6},{6,10},{... | collective-permute-start | bytes 835592 | tf_op jit(solution)/shard_map/ppermute | solution.py:378
  7.7 43.4 %collective-permute-start.1 = (bf16[136,1024]{1,0:T(8,128)(2,1)S(1)}, bf16[136,1024]{1,0:T(8,128)(2,1)S(1)}, u32[]{:S(2)}, u32[]{:S(2)}) collective-permute-start(bf16[136,1024]{1,0:T(8,128)(2,1)S(1)} %fusion.1.refs_0_.refs_4_), channel_id=1, source_target_pairs={{0,8},{4,12},{8,0},{12,4},{1,9},{5,13},{9,1},{13,5},{2,10},{6,14},... | collective-permute-start | bytes 835592 | tf_op jit(solution)/shard_map/ppermute | solution.py:378
  8.8 42.8 %collective-permute-start.2 = (bf16[136,1024]{1,0:T(8,128)(2,1)S(1)}, bf16[136,1024]{1,0:T(8,128)(2,1)S(1)}, u32[]{:S(2)}, u32[]{:S(2)}) collective-permute-start(bf16[136,1024]{1,0:T(8,128)(2,1)S(1)} %fusion.1.refs_0_.refs_4_), channel_id=1, source_target_pairs={{0,12},{4,0},{8,4},{12,8},{1,13},{5,1},{9,5},{13,9},{2,14},{6,2},{... | collective-permute-start | bytes 835592 | tf_op jit(solution)/shard_map/ppermute | solution.py:378
  11.7 35.9 %collective-permute-start.7 = (bf16[128,1024]{1,0:T(8,128)(2,1)}, bf16[128,1024]{1,0:T(8,128)(2,1)S(1)}, u32[]{:S(2)}, u32[]{:S(2)}) collective-permute-start(bf16[128,1024]{1,0:T(8,128)(2,1)} %refs_0_.1), channel_id=1, source_target_pairs={{0,8},{4,12},{8,0},{12,4},{1,9},{5,13},{9,1},{13,5},{2,10},{6,14},... | collective-permute-start | bytes 786440 | tf_op jit(solution)/shard_map/ppermute | solution.py:378
  13.3 35.7 %collective-permute-start.8 = (bf16[128,1024]{1,0:T(8,128)(2,1)}, bf16[128,1024]{1,0:T(8,128)(2,1)S(1)}, u32[]{:S(2)}, u32[]{:S(2)}) collective-permute-start(bf16[128,1024]{1,0:T(8,128)(2,1)} %refs_0_.1), channel_id=1, source_target_pairs={{0,12},{4,0},{8,4},{12,8},{1,13},{5,1},{9,5},{13,9},{2,14},{6,2},{... | collective-permute-start | bytes 786440 | tf_op jit(solution)/shard_map/ppermute | solution.py:378
  15.1 12.9 %copy-start.12 = (bf16[768,4,1024]{2,1,0:T(4,128)(2,1)S(1)}, bf16[768,4,1024]{2,1,0:T(4,128)(2,1)}, u32[]{:S(2)}) copy-start(bf16[768,4,1024]{2,1,0:T(4,128)(2,1)} %param.11) | copy-start | bytes 18874372
  28.1 21.0 %copy-start.4 = (bf16[128,1024]{1,0:T(8,128)(2,1)S(1)}, bf16[128,1024]{1,0:T(8,128)(2,1)}, u32[]{:S(2)}) copy-start(bf16[128,1024]{1,0:T(8,128)(2,1)} %refs_0_.1) | copy-start | bytes 786436
  47.6 25.1 %collective-permute-start.15 = (bf16[136,1024]{1,0:T(8,128)(2,1)S(1)}, bf16[136,1024]{1,0:T(8,128)(2,1)S(1)}, u32[]{:S(2)}, u32[]{:S(2)}) collective-permute-start(bf16[136,1024]{1,0:T(8,128)(2,1)S(1)} %fusion.1.refs_0_.refs_4_), channel_id=1, source_target_pairs={{0,2},{1,3},{2,0},{3,1},{4,6},{5,7},{6,4},{7,5},{8,10},{9,11},{10,... | collective-permute-start | bytes 835592 | tf_op jit(solution)/shard_map/ppermute | solution.py:385
  49.1 23.0 %collective-permute-start.19 = (bf16[128,1024]{1,0:T(8,128)(2,1)S(1)}, bf16[128,1024]{1,0:T(8,128)(2,1)S(1)}, u32[]{:S(2)}, u32[]{:S(2)}) collective-permute-start(bf16[128,1024]{1,0:T(8,128)(2,1)S(1)} %copy-done.4), channel_id=1, source_target_pairs={{0,2},{1,3},{2,0},{3,1},{4,6},{5,7},{6,4},{7,5},{8,10},{9,11},{10,... | collective-permute-start | bytes 786440 | tf_op jit(solution)/shard_map/ppermute | solution.py:385
  49.6 24.5 %collective-permute-start.20 = (bf16[128,1024]{1,0:T(8,128)(2,1)S(1)}, bf16[128,1024]{1,0:T(8,128)(2,1)S(1)}, u32[]{:S(2)}, u32[]{:S(2)}) collective-permute-start(bf16[128,1024]{1,0:T(8,128)(2,1)S(1)} %collective-permute-done.6.refs_1_), channel_id=1, source_target_pairs={{0,2},{1,3},{2,0},{3,1},{4,6},{5,7},{6,4},{7,5},{8,10},{9,11},{10,... | collective-permute-start | bytes 786440 | tf_op jit(solution)/shard_map/ppermute | solution.py:385
  51.1 36.8 %collective-permute-start.21 = (bf16[128,1024]{1,0:T(8,128)(2,1)S(1)}, bf16[128,1024]{1,0:T(8,128)(2,1)S(1)}, u32[]{:S(2)}, u32[]{:S(2)}) collective-permute-start(bf16[128,1024]{1,0:T(8,128)(2,1)S(1)} %collective-permute-done.7.refs_2_), channel_id=1, source_target_pairs={{0,2},{1,3},{2,0},{3,1},{4,6},{5,7},{6,4},{7,5},{8,10},{9,11},{10,... | collective-permute-start | bytes 786440 | tf_op jit(solution)/shard_map/ppermute | solution.py:385
  51.6 36.3 %collective-permute-start.22 = (bf16[128,1024]{1,0:T(8,128)(2,1)S(1)}, bf16[128,1024]{1,0:T(8,128)(2,1)S(1)}, u32[]{:S(2)}, u32[]{:S(2)}) collective-permute-start(bf16[128,1024]{1,0:T(8,128)(2,1)S(1)} %collective-permute-done.8.refs_3_), channel_id=1, source_target_pairs={{0,2},{1,3},{2,0},{3,1},{4,6},{5,7},{6,4},{7,5},{8,10},{9,11},{10,... | collective-permute-start | bytes 786440 | tf_op jit(solution)/shard_map/ppermute | solution.py:385
  53.1 4.6 %copy-start = (bf16[1024,4,1536]{2,0,1:T(8,128)(2,1)S(1)}, bf16[1024,4,1536]{2,0,1:T(8,128)(2,1)}, u32[]{:S(2)}) copy-start(bf16[1024,4,1536]{2,0,1:T(8,128)(2,1)} %copy.17) | copy-start | bytes 37748740
  57.7 2.8 %copy-start.1 = (bf16[768,4,1024]{2,0,1:T(8,128)(2,1)S(1)}, bf16[768,4,1024]{2,0,1:T(8,128)(2,1)}, u32[]{:S(2)}) copy-start(bf16[768,4,1024]{2,0,1:T(8,128)(2,1)} %copy.18) | copy-start | bytes 18874372
  72.1 15.9 %collective-permute-start.16 = (bf16[136,1024]{1,0:T(8,128)(2,1)S(1)}, bf16[136,1024]{1,0:T(8,128)(2,1)S(1)}, u32[]{:S(2)}, u32[]{:S(2)}) collective-permute-start(bf16[136,1024]{1,0:T(8,128)(2,1)S(1)} %collective-permute-done.refs_1_.refs_5_), channel_id=1, source_target_pairs={{0,2},{1,3},{2,0},{3,1},{4,6},{5,7},{6,4},{7,5},{8,10},{9,11},{10,... | collective-permute-start | bytes 835592 | tf_op jit(solution)/shard_map/ppermute | solution.py:385
  72.6 18.9 %collective-permute-start.17 = (bf16[136,1024]{1,0:T(8,128)(2,1)S(1)}, bf16[136,1024]{1,0:T(8,128)(2,1)S(1)}, u32[]{:S(2)}, u32[]{:S(2)}) collective-permute-start(bf16[136,1024]{1,0:T(8,128)(2,1)S(1)} %collective-permute-done.1.refs_2_.refs_6_), channel_id=1, source_target_pairs={{0,2},{1,3},{2,0},{3,1},{4,6},{5,7},{6,4},{7,5},{8,10},{9,11},{10,... | collective-permute-start | bytes 835592 | tf_op jit(solution)/shard_map/ppermute | solution.py:385
  74.1 22.3 %collective-permute-start.18 = (bf16[136,1024]{1,0:T(8,128)(2,1)S(1)}, bf16[136,1024]{1,0:T(8,128)(2,1)S(1)}, u32[]{:S(2)}, u32[]{:S(2)}) collective-permute-start(bf16[136,1024]{1,0:T(8,128)(2,1)S(1)} %collective-permute-done.2.refs_3_.refs_7_), channel_id=1, source_target_pairs={{0,2},{1,3},{2,0},{3,1},{4,6},{5,7},{6,4},{7,5},{8,10},{9,11},{10,... | collective-permute-start | bytes 835592 | tf_op jit(solution)/shard_map/ppermute | solution.py:385
  87.9 28.2 %copy-start.5 = (bf16[128,1024]{1,0:T(8,128)(2,1)}, bf16[128,1024]{1,0:T(8,128)(2,1)S(1)}, u32[]{:S(2)}) copy-start(bf16[128,1024]{1,0:T(8,128)(2,1)S(1)} %get-tuple-element.30) | copy-start | bytes 786436
  96.4 35.0 %copy-start.13 = (s32[128,6]{0,1:T(8,128)S(1)}, s32[128,6]{0,1:T(8,128)}, u32[]{:S(2)}) copy-start(s32[128,6]{0,1:T(8,128)} %param.7) | copy-start | bytes 9220
  118.9 60.6 %collective-permute-start.23 = (bf16[4,256,1536]{2,1,0:T(8,128)(2,1)}, bf16[4,256,1536]{2,1,0:T(8,128)(2,1)}, u32[]{:S(2)}, u32[]{:S(2)}) collective-permute-start(bf16[4,256,1536]{2,1,0:T(8,128)(2,1)} %get-tuple-element.40), channel_id=1, source_target_pairs={{0,1},{1,0},{2,3},{3,2},{4,5},{5,4},{6,7},{7,6},{8,9},{9,8},{10,11... | collective-permute-start | bytes 9437192 | tf_op jit(solution)/shard_map/ppermute | solution.py:488
  118.9 56.0 %collective-permute-start.24 = (bf16[4,192,1024]{2,1,0:T(8,128)(2,1)}, bf16[4,192,1024]{2,1,0:T(8,128)(2,1)}, u32[]{:S(2)}, u32[]{:S(2)}) collective-permute-start(bf16[4,192,1024]{2,1,0:T(8,128)(2,1)} %get-tuple-element.42), channel_id=1, source_target_pairs={{0,1},{1,0},{2,3},{3,2},{4,5},{5,4},{6,7},{7,6},{8,9},{9,8},{10,11... | collective-permute-start | bytes 4718600 | tf_op jit(solution)/shard_map/ppermute | solution.py:488
  119.4 7.4 %collective-permute-start.12 = (f32[4,128]{1,0:T(4,128)S(1)}, f32[4,128]{1,0:T(4,128)S(1)}, u32[]{:S(2)}, u32[]{:S(2)}) collective-permute-start(f32[4,128]{1,0:T(4,128)S(1)} %get-tuple-element.50), channel_id=1, source_target_pairs={{0,12},{4,0},{8,4},{12,8},{1,13},{5,1},{9,5},{13,9},{2,14},{6,2},{... | collective-permute-start | bytes 6152 | tf_op jit(solution)/shard_map/ppermute | solution.py:378
  125.5 4.5 %collective-permute-start.13 = (f32[4,128]{1,0:T(4,128)S(1)}, f32[4,128]{1,0:T(4,128)S(1)}, u32[]{:S(2)}, u32[]{:S(2)}) collective-permute-start(f32[4,128]{1,0:T(4,128)S(1)} %get-tuple-element.49), channel_id=1, source_target_pairs={{0,8},{4,12},{8,0},{12,4},{1,9},{5,13},{9,1},{13,5},{2,10},{6,14},... | collective-permute-start | bytes 6152 | tf_op jit(solution)/shard_map/ppermute | solution.py:378
  125.5 6.0 %collective-permute-start.14 = (f32[4,128]{1,0:T(4,128)S(1)}, f32[4,128]{1,0:T(4,128)S(1)}, u32[]{:S(2)}, u32[]{:S(2)}) collective-permute-start(f32[4,128]{1,0:T(4,128)S(1)} %get-tuple-element.48), channel_id=1, source_target_pairs={{0,4},{4,8},{8,12},{12,0},{1,5},{5,9},{9,13},{13,1},{2,6},{6,10},{... | collective-permute-start | bytes 6152 | tf_op jit(solution)/shard_map/ppermute | solution.py:378
  126.8 11.7 %collective-permute-start.5 = (bf16[128,1024]{1,0:T(8,128)(2,1)}, bf16[128,1024]{1,0:T(8,128)(2,1)}, u32[]{:S(2)}, u32[]{:S(2)}) collective-permute-start(bf16[128,1024]{1,0:T(8,128)(2,1)} %copy-done.11), channel_id=1, source_target_pairs={{0,4},{4,8},{8,12},{12,0},{1,5},{5,9},{9,13},{13,1},{2,6},{6,10},{... | collective-permute-start | bytes 786440 | tf_op jit(solution)/shard_map/ppermute | solution.py:378
  130.0 19.8 %collective-permute-start.4 = (bf16[128,1024]{1,0:T(8,128)(2,1)}, bf16[128,1024]{1,0:T(8,128)(2,1)}, u32[]{:S(2)}, u32[]{:S(2)}) collective-permute-start(bf16[128,1024]{1,0:T(8,128)(2,1)} %copy-done.9), channel_id=1, source_target_pairs={{0,8},{4,12},{8,0},{12,4},{1,9},{5,13},{9,1},{13,5},{2,10},{6,14},... | collective-permute-start | bytes 786440 | tf_op jit(solution)/shard_map/ppermute | solution.py:378
  131.4 18.3 %collective-permute-start.3 = (bf16[128,1024]{1,0:T(8,128)(2,1)}, bf16[128,1024]{1,0:T(8,128)(2,1)}, u32[]{:S(2)}, u32[]{:S(2)}) collective-permute-start(bf16[128,1024]{1,0:T(8,128)(2,1)} %copy-done.6), channel_id=1, source_target_pairs={{0,12},{4,0},{8,4},{12,8},{1,13},{5,1},{9,5},{13,9},{2,14},{6,2},{... | collective-permute-start | bytes 786440 | tf_op jit(solution)/shard_map/ppermute | solution.py:378
  138.5 28.2 %collective-permute-start.11 = (bf16[128,1024]{1,0:T(8,128)(2,1)}, bf16[128,1024]{1,0:T(8,128)(2,1)S(1)}, u32[]{:S(2)}, u32[]{:S(2)}) collective-permute-start(bf16[128,1024]{1,0:T(8,128)(2,1)} %copy-done.10), channel_id=1, source_target_pairs={{0,4},{4,8},{8,12},{12,0},{1,5},{5,9},{9,13},{13,1},{2,6},{6,10},{... | collective-permute-start | bytes 786440 | tf_op jit(solution)/shard_map/ppermute | solution.py:378
  149.7 20.6 %collective-permute-start.10 = (bf16[128,1024]{1,0:T(8,128)(2,1)}, bf16[128,1024]{1,0:T(8,128)(2,1)S(1)}, u32[]{:S(2)}, u32[]{:S(2)}) collective-permute-start(bf16[128,1024]{1,0:T(8,128)(2,1)} %copy-done.8), channel_id=1, source_target_pairs={{0,8},{4,12},{8,0},{12,4},{1,9},{5,13},{9,1},{13,5},{2,10},{6,14},... | collective-permute-start | bytes 786440 | tf_op jit(solution)/shard_map/ppermute | solution.py:378
  149.7 23.3 %collective-permute-start.9 = (bf16[128,1024]{1,0:T(8,128)(2,1)}, bf16[128,1024]{1,0:T(8,128)(2,1)S(1)}, u32[]{:S(2)}, u32[]{:S(2)}) collective-permute-start(bf16[128,1024]{1,0:T(8,128)(2,1)} %copy-done.7), channel_id=1, source_target_pairs={{0,12},{4,0},{8,4},{12,8},{1,13},{5,1},{9,5},{13,9},{2,14},{6,2},{... | collective-permute-start | bytes 786440 | tf_op jit(solution)/shard_map/ppermute | solution.py:378
  174.8 4.7 %copy-start.3 = (f32[4,256,1536]{2,1,0:T(8,128)S(1)}, f32[4,256,1536]{2,1,0:T(8,128)}, u32[]{:S(2)}) copy-start(f32[4,256,1536]{2,1,0:T(8,128)} %copy-done.2) | copy-start | bytes 18874372
  (7 other events, 6.9 us)

commit v3 on v2

--- a/solution.py
+++ b/solution.py
@@ -169,7 +169,7 @@
 
 
 HALF = 8
-FWD, BWD, FAR, JOIN = 16, 16, 24, 8
+FWD, BWD, FAR, JOIN = 24, 24, 28, 8
 
 
 def routing_tile(note_refs, expert, count, cap):
@@ -298,7 +298,7 @@
     cots, refs = refs[:sources], refs[sources:]
     gate_ref, down_ref, input_ref, hidden_ref, out_grad_ref, pre_grad_ref = refs[:6]
     gate_own, gate_share, down_own, down_share = refs[6:10]
-    tok, cot, all_inputs, all_hidden, all_grads, all_pre, gate_sum, down_sum = refs[10:]
+    tok, cot, all_inputs, all_hidden, all_grads, all_pre, down_sum = refs[10:]
     e = pl.program_id(0)
     count = tok.shape[0] // sources
     slots = sources * cap
@@ -323,20 +323,31 @@
         scratch[slots:, :] = far
 
     place, core = info[1], info[2]
-    for left, right, total, own, share in (
-        (all_hidden, all_grads, down_sum, down_own, down_share),
-        (all_inputs, all_pre, gate_sum, gate_own, gate_share),
-    ):
-        size, block = total.shape[0], own.shape[1]
-        columns = pl.ds(pl.multiple_of(place * size, size), size)
-        total[...] = across(left[:, columns], right[...])
-        own[0] = total[pl.ds(pl.multiple_of(core * block, block), block), :]
-        share[0] = total[pl.ds(pl.multiple_of((1 - core) * block, block), block), :].astype(BF)
-
-
-def joined(local, own_ref, share_ref, out_ref):
-    for e in range(local):
-        out_ref[:, e, :] = own_ref[e] + share_ref[e].astype(F32)
+
+    def block(index, size):
+        return pl.ds(pl.multiple_of(index * size, size), size)
+
+    size = gate_own.shape[1]
+    gate_own[0] = across(all_inputs[:, block(place * CORES + core, size)], all_pre[...])
+    gate_share[0] = across(all_inputs[:, block(place * CORES + 1 - core, size)], all_pre[...]).astype(BF)
+    size = down_own.shape[1]
+    down_sum[...] = across(all_hidden[:, block(place, CORES * size)], all_grads[...])
+    down_own[0] = down_sum[block(core, size), :]
+    down_share[0] = down_sum[block(1 - core, size), :].astype(BF)
+
+
+def joined(local, gate_own, gate_share, down_own, down_share, gate_out, down_out):
+    for own, share, out in ((gate_own, gate_share, gate_out), (down_own, down_share, down_out)):
+        for e in range(local):
+            out[:, e, :] = own[e] + share[e].astype(F32)
+
+
+def summed(sources, *refs):
+    for first, out in ((0, refs[-2]), (sources, refs[-1])):
+        total = refs[first][...].astype(F32)
+        for ref in refs[first + 1:first + sources]:
+            total += ref[...].astype(F32)
+        out[...] = total.astype(BF)
 
 
 def whole(*shape):
@@ -373,9 +384,8 @@
     slots = sources * cap
     info = jnp.stack([home * local, place, core]).astype(jnp.int32)
 
-    def to_source(values, shift):
-        step = [(i, (i + shift) % sources) for i in range(sources)]
-        return lax.ppermute(values, "expert", step) if shift else values
+    def to_mate(values, mask):
+        return lax.ppermute(values, "expert", [(i, i ^ mask) for i in range(sources)]) if mask else values
 
     def to_chip(values):
         step = [
@@ -390,20 +400,32 @@
     )
     packed = jnp.concatenate([tokens, jnp.pad(notes, ((0, 0), (0, width - 2 * count)))], axis=0)
 
+    far_own = to_chip(jnp.concatenate([packed, cotangent], axis=0))
+
     def gathered(values):
-        far = [to_chip(values)]
-        held = [to_source(values, s) for s in range(sources)]
-        far += [to_chip(h) for h in held[1:]]
+        held = [values] * sources
+        for mask in range(1, sources):
+            low = mask & -mask
+            held[mask] = to_mate(held[mask - low], low)
+        far = [to_chip(h) for h in held[1:]]
         return held, far
 
     near_packed, far_packed = gathered(packed)
     near_cots, far_cots = gathered(cotangent)
-    gate_rows = lax.optimization_barrier(
-        with_layout_constraint(gate_up.swapaxes(0, 1), Layout((0, 1, 2)))
-    )
-    down_rows = lax.optimization_barrier(
-        with_layout_constraint(down_weights.swapaxes(0, 1), Layout((0, 1, 2)))
-    )
+    far_packed = [far_own[:packed.shape[0]]] + far_packed
+    far_cots = [far_own[packed.shape[0]:]] + far_cots
+
+    always = lax.optimization_barrier(jnp.ones((), jnp.bool_))
+
+    def in_hbm(values):
+        return pltpu.with_memory_space_constraint(values, pltpu.HBM)
+
+    def by_expert(weights):
+        moved = with_layout_constraint(weights.swapaxes(0, 1), Layout((0, 1, 2)))
+        return in_hbm(lax.optimization_barrier(moved))
+
+    down_rows = by_expert(down_weights)
+    gate_rows = by_expert(jnp.where(always, gate_up, jnp.zeros((), BF)))
 
     block_specs = [whole(count, width)] * sources
     note_specs = [pl.BlockSpec((HALF, 2 * count), lambda e, info: (count // HALF, 0))] * sources
@@ -430,10 +452,7 @@
     )(info, *near_packed, *near_packed, gate_rows, down_rows)
 
     def returned(parts):
-        return [to_source(parts[s], -s) for s in range(sources)]
-
-    def added(arrived):
-        return sum([a.astype(F32) for a in arrived[1:]], arrived[0].astype(F32)).astype(BF)
+        return [to_mate(parts[s], s) for s in range(sources)]
 
     out_arrived = returned(out_parts)
 
@@ -450,7 +469,7 @@
         2 * weight_bytes,
         BWD,
     )(info, *near_cots, *near_packed, gate_rows, down_rows, pre_act, outputs)
-    prob_arrived = [to_source(prob_part[s], -s) for s in range(sources)]
+    prob_arrived = [to_mate(prob_part[s], s) for s in range(sources)]
     grad_arrived = returned(grad_parts)
 
     gate_block, down_block = width // replicas, hidden_width // replicas
@@ -465,14 +484,14 @@
             each(down_block, width), each(down_block, width),
         ],
         [
-            array(pre_width, F32, gate_block), array(pre_width, BF, gate_block),
-            array(width, F32, down_block), array(width, BF, down_block),
+            pltpu.HBM((local, gate_block, pre_width), F32), array(pre_width, BF, gate_block),
+            pltpu.HBM((local, down_block, width), F32), array(width, BF, down_block),
         ],
         [
             gathered_rows, gathered_rows,
             pltpu.VMEM((2 * slots, width), BF), pltpu.VMEM((2 * slots, hidden_width), BF),
             pltpu.VMEM((2 * slots, width), BF), pltpu.VMEM((2 * slots, pre_width), BF),
-            pltpu.VMEM((CORES * gate_block, pre_width), F32), pltpu.VMEM((CORES * down_block, width), F32),
+            pltpu.VMEM((CORES * down_block, width), F32),
         ],
         6 * product,
         3 * weight_bytes,
@@ -483,37 +502,55 @@
     )
 
     pair = [(i, i ^ 1) for i in range(replicas)]
-
-    def final(own, share):
-        theirs = lax.ppermute(share, "replica", pair)
-        rows, size = own.shape[1], own.shape[2]
-        cut = rows // 4
-        return pl.pallas_call(
-            functools.partial(joined, local),
-            grid=(rows // cut,),
-            in_specs=[pl.BlockSpec((local, cut, size), lambda i: (0, i, 0))] * 2,
-            out_specs=pl.BlockSpec((cut, local, size), lambda i: (i, 0, 0)),
-            out_shape=jax.ShapeDtypeStruct((rows, local, size), F32),
-            compiler_params=pltpu.CompilerParams(vmem_limit_bytes=JOIN << 20),
-            cost_estimate=pl.CostEstimate(flops=0, bytes_accessed=10 * own.size, transcendentals=0),
-        )(own, theirs)
-
-    gate_up_gradient = final(gate_own, gate_share)
-    down_gradient = final(down_own, down_share)
+    down_theirs, gate_theirs = lax.ppermute(down_share, "replica", pair), lax.ppermute(gate_share, "replica", pair)
+
+    combined, token_gradient = pl.pallas_call(
+        functools.partial(summed, sources),
+        name="summed",
+        grid=(2,),
+        in_specs=[pl.BlockSpec((count // 2, width), lambda i: (i, 0))] * (2 * sources),
+        out_specs=[pl.BlockSpec((count // 2, width), lambda i: (i, 0))] * 2,
+        out_shape=[block_shape] * 2,
+        compiler_params=pltpu.CompilerParams(vmem_limit_bytes=JOIN << 20),
+        cost_estimate=pl.CostEstimate(flops=0, bytes_accessed=20 * count * width, transcendentals=0),
+    )(*out_arrived, *grad_arrived)
+
+    cuts = 8
+    gate_cut, down_cut = gate_block // cuts, down_block // cuts
+
+    def near_spec(cut, size):
+        return pl.BlockSpec((local, cut, size), lambda i: (0, i, 0))
+
+    def out_spec(cut, size):
+        return pl.BlockSpec((cut, local, size), lambda i: (i, 0, 0))
+
+    gate_up_gradient, down_gradient = pl.pallas_call(
+        functools.partial(joined, local),
+        name="joined",
+        grid=(cuts,),
+        in_specs=[near_spec(gate_cut, pre_width)] * 2 + [near_spec(down_cut, width)] * 2,
+        out_specs=[out_spec(gate_cut, pre_width), out_spec(down_cut, width)],
+        out_shape=[
+            jax.ShapeDtypeStruct((gate_block, local, pre_width), F32),
+            jax.ShapeDtypeStruct((down_block, local, width), F32),
+        ],
+        compiler_params=pltpu.CompilerParams(vmem_limit_bytes=JOIN << 20),
+        cost_estimate=pl.CostEstimate(flops=0, bytes_accessed=10 * gate_own.size, transcendentals=0),
+    )(in_hbm(gate_own), gate_theirs, in_hbm(down_own), down_theirs)
 
     choice = expert_ids.T
     prob_gradient = jnp.zeros((top, count), F32)
     for s in range(sources):
-        block = lax.rem(home + s, sources) * local
+        block = jnp.bitwise_xor(home, s) * local
         hit = choice[:, None, :] == (block + jnp.arange(local, dtype=jnp.int32))[None, :, None]
         prob_gradient = prob_gradient + jnp.sum(jnp.where(hit, prob_arrived[s][None], 0.0), axis=1)
-    return (added(out_arrived), added(grad_arrived), prob_gradient.T, gate_up_gradient, down_gradient)
+    return (combined, token_gradient, prob_gradient.T, gate_up_gradient, down_gradient)
 
 
 def on_device(*args, sources, replicas):
     count, top, local = args[0].shape[0], args[1].shape[1], args[4].shape[1]
     small = sources * min(CAP, count) * local <= 1024 and sources <= 4
-    plain = replicas == 2 * CORES and small and count % 128 == 0 and top <= HALF and 2 * count <= args[0].shape[1]
+    plain = replicas == 2 * CORES and small and sources & (sources - 1) == 0 and args[0].shape[1] % (128 * replicas) == 0 and count % 128 == 0 and top <= HALF and 2 * count <= args[0].shape[1]
     return (two_chips if plain else general)(*args, sources=sources, replicas=replicas)
 
 

time: 186 us -> 177 us (0.952)
  local copies, waits for them, and re-layouts: 32 us -> 10.8 us
  starting transfers between devices: 44.2 us -> 27.9 us
  other arithmetic: 6.93 us -> 18.2 us
  waiting for transfers between devices: 50.6 us -> 58.9 us
  Pallas kernels: 50.7 us -> 58 us
    unnamed x30 -> x15, local copies, waits for them, and re-layouts: 32 us -> 10.7 us
    ppermute x17, starting transfers between devices: 36.1 us -> 19.9 us  [the longest x15 19.4 us: to_mate(): lax.ppermute(values, 'expert', [(i, i ^ mask) for i in range(sources)])]
    ppermute x17, waiting for transfers between devices: 42.1 us -> 57.7 us  [the longest x15 57.7 us: to_mate(): lax.ppermute(values, 'expert', [(i, i ^ mask) for i in range(sources)])]
    transpose x0 -> x1, other arithmetic: none -> 14 us  [by_expert(): moved = with_layout_constraint(weights.swapaxes(0, 1), Layout((0, 1, 2)))]
    ppermute x8 -> x7, waiting for transfers between devices: 8.49 us -> 1.25 us  [to_chip(): return lax.ppermute(values, 'replica', step)]
    convert_element_type x2 -> x0, other arithmetic: 3.8 us -> none  [added(): sum([a.astype(F32) for a in arrived[1:]], arrived[0].astype(F32)).astype(BF)]
    pallas_call x1, Pallas kernels: 9.48 us -> 12.9 us  [two_chips(): kernel_call(functools.partial(own_forward, sources, cap), local, block_sp...]
    pallas_call x1, Pallas kernels: 11.1 us -> 13.4 us  [two_chips(): kernel_call(functools.partial(own_backward, sources, cap), local, block_s...]
  transfers between devices with their start and end apart: 25 -> 24, of which waited for: 10 -> 8; matrix products, arithmetic and copies ran while one was open for 13% -> 13% of each run, Pallas kernels for 14% -> 16%
where the time goes in v3:
time: 177 us; the launch traced here: 175 us
  waiting for transfers between devices  58.9 us (33%)
  Pallas kernels  58 us (33%)
  starting transfers between devices  27.9 us (16%)
  other arithmetic  18.2 us (10%)
  local copies, waits for them, and re-layouts  10.8 us (6%)
    ppermute x15, waiting for transfers between devices, to_mate(): lax.ppermute(values, 'expert', [(i, i ^ mask) for i in range(sources)])  57.7 us
    pallas_call x1, Pallas kernels, two_chips(): kernel_call(functools.partial(far_gradients, sources, cap), local, block_...  19.6 us
    ppermute x15, starting transfers between devices, to_mate(): lax.ppermute(values, 'expert', [(i, i ^ mask) for i in range(sources)])  19.4 us
    transpose x1, other arithmetic, by_expert(): moved = with_layout_constraint(weights.swapaxes(0, 1), Layout((0, 1, 2)))  14 us
    pallas_call x1, Pallas kernels, two_chips(): kernel_call(functools.partial(own_backward, sources, cap), local, block_s...  13.4 us
    pallas_call x1, Pallas kernels, two_chips(): kernel_call(functools.partial(own_forward, sources, cap), local, block_sp...  12.9 us
    unnamed x15, local copies, waits for them, and re-layouts  10.7 us
    pallas_call x1, Pallas kernels, two_chips(): pl.pallas_call(functools.partial(joined, local), name='joined', grid=(cut...  10.1 us
  transfers between devices with their start and end apart: 24, of which 8 were waited for; matrix products, arithmetic and copies ran while one was open for 13% of the time, Pallas kernels for 16%

profile of v3, /device:TPU:0, one launch (start us, length us, event | category | flops | bytes accessed | tf_op | source)
XLA Modules:
  0.0 174.5 jit_solution(5670658679468748645)
XLA Ops:
  2.0 1.0 pad_maximum_fusion.1.refs_0_.refs_4_
  3.0 4.1 %collective-permute-start.1 = (bf16[136,1024]{1,0:T(8,128)(2,1)S(1)}, bf16[136,1024]{1,0:T(8,128)(2,1)S(1)}, u32[]{:S(2)}, u32[]{:S(2)}) collective-permute-start(bf16[136,1024]{1,0:T(8,128)(2,1)S(1)} %pad_maximum_fusion.1.refs_0_.refs_4_), channel_id=1, source_target_pairs={{0,8},{4,12},{8,0},{12,4},{1,9},{5,13},{9,1},{13,5},{2,10},{6,14},... | collective-permute-start | bytes 835592 | tf_op jit(solution)/shard_map/ppermute | solution.py:388
  7.2 1.8 %collective-permute-start = (bf16[136,1024]{1,0:T(8,128)(2,1)S(1)}, bf16[136,1024]{1,0:T(8,128)(2,1)S(1)}, u32[]{:S(2)}, u32[]{:S(2)}) collective-permute-start(bf16[136,1024]{1,0:T(8,128)(2,1)S(1)} %pad_maximum_fusion.1.refs_0_.refs_4_), channel_id=1, source_target_pairs={{0,4},{4,0},{8,12},{12,8},{1,5},{5,1},{9,13},{13,9},{2,6},{6,2},{1... | collective-permute-start | bytes 835592 | tf_op jit(solution)/shard_map/ppermute | solution.py:388
  9.2 1.1 pad_maximum_fusion
  10.3 1.8 %collective-permute-start.15 = (bf16[264,1024]{1,0:T(8,128)(2,1)S(1)}, bf16[264,1024]{1,0:T(8,128)(2,1)S(1)}, u32[]{:S(2)}, u32[]{:S(2)}) collective-permute-start(bf16[264,1024]{1,0:T(8,128)(2,1)S(1)} %pad_maximum_fusion), channel_id=1, source_target_pairs={{0,2},{1,3},{2,0},{3,1},{4,6},{5,7},{6,4},{7,5},{8,10},{9,11},{10,... | collective-permute-start | bytes 1622024 | tf_op jit(solution)/shard_map/ppermute | solution.py:395
  12.1 19.0 %collective-permute-done.7.refs_2_ = bf16[128,1024]{1,0:T(8,128)(2,1)S(1)} collective-permute-done((bf16[128,1024]{1,0:T(8,128)(2,1)}, bf16[128,1024]{1,0:T(8,128)(2,1)S(1)}, u32[]{:S(2)}, u32[]{:S(2)}) %collective-permute-start.7) | collective-permute-done | bytes 262176 | tf_op jit(solution)/shard_map/ppermute | solution.py:388
  31.1 0.8 collective-permute-start.8
  31.9 1.3 collective-permute-start.2
  33.1 14.0 %fusion.refs_8_.refs_12_ = bf16[4,1024,1536]{2,1,0:T(8,128)(2,1)} fusion(bf16[1024,4,1536]{2,1,0:T(4,128)(2,1)} %param.10, pred[]{:T(512)} %constant.27.clone.1), kind=kLoop, calls=%fused_computation.1 | loop fusion | flops 6291456 | bytes 25165824 | tf_op jit(solution)/shard_map/transpose | solution.py:424
  47.2 7.6 %copy.19 = bf16[768,4,1024]{2,0,1:T(8,128)(2,1)} copy(bf16[768,4,1024]{2,1,0:T(4,128)(2,1)} %param.11) | data formatting | bytes 12582912 | tf_op args[5]
  54.8 1.5 collective-permute-start.20
  56.9 1.6 collective-permute-start.17
  59.0 1.5 collective-permute-start.21
  60.6 12.9 %shard_map.101 = (bf16[128,1024]{1,0:T(8,128)(2,1)S(1)}, bf16[128,1024]{1,0:T(8,128)(2,1)}, bf16[128,1024]{1,0:T(8,128)(2,1)}, bf16[128,1024]{1,0:T(8,128)(2,1)}...) custom-call(s32[3]{0:T(128)S(1)} %pad_add_fusion.info, ...), custom_call_target="tpu_custom_call" | custom-call | flops 6442450944 | bytes 37748736 | tf_op jit(solution)/shard_map/pallas_call | solution.py:442
  74.0 13.4 %shard_map.102 = (bf16[128,1024]{1,0:T(8,128)(2,1)S(1)}, bf16[128,1024]{1,0:T(8,128)(2,1)S(1)}, bf16[128,1024]{1,0:T(8,128)(2,1)S(1)}, bf16[128,1024]{1,0:T(8,12...) custom-call(s32[3]{0:T(128)S(1)} %pad_add_fusion.info, ...), custom_call_target="tpu_custom_call" | custom-call | flops 6442450944 | bytes 37748736 | tf_op jit(solution)/shard_map/pallas_call | solution.py:459
  87.4 0.7 copy-done.3
  88.1 0.7 copy-done.4
  88.8 0.7 copy-done.5
  89.6 1.2 collective-permute-done.18.refs_3_.refs_7_
  90.8 19.6 %shard_map.103 = (f32[4,256,1536]{2,1,0:T(8,128)}, bf16[4,256,1536]{2,1,0:T(8,128)(2,1)}, f32[4,192,1024]{2,1,0:T(8,128)}, bf16[4,192,1024]{2,1,0:T(8,128)(2,1)}) custom-call(s32[3]{0:T(128)S(1)} %pad_add_fusion.info, bf16[136,1024]{1,0:T(8,128)(2,1)S(1)} %slice.24.refs_0_.refs_4_, bf16[136,1024]{1,0:T(8,128)(2,1)S(1)} %collective-permute-done.16.refs_1_.refs_5_, ...), custom_call_target="tpu_custom_call" | custom-call | flops 9663676416 | bytes 56623104 | tf_op jit(solution)/shard_map/pallas_call | solution.py:476
  111.0 1.6 collective-permute-start.12
  112.6 3.3 %collective-permute-start.13 = (f32[4,128]{1,0:T(4,128)S(1)}, f32[4,128]{1,0:T(4,128)S(1)}, u32[]{:S(2)}, u32[]{:S(2)}) collective-permute-start(f32[4,128]{1,0:T(4,128)S(1)} %get-tuple-element.57), channel_id=1, source_target_pairs={{0,8},{4,12},{8,0},{12,4},{1,9},{5,13},{9,1},{13,5},{2,10},{6,14},... | collective-permute-start | bytes 6152 | tf_op jit(solution)/shard_map/ppermute | solution.py:388
  116.5 1.0 collective-permute-done.13
  117.5 2.9 %collective-permute-start.4 = (bf16[128,1024]{1,0:T(8,128)(2,1)}, bf16[128,1024]{1,0:T(8,128)(2,1)}, u32[]{:S(2)}, u32[]{:S(2)}) collective-permute-start(bf16[128,1024]{1,0:T(8,128)(2,1)} %get-tuple-element.30), channel_id=1, source_target_pairs={{0,8},{4,12},{8,0},{12,4},{1,9},{5,13},{9,1},{13,5},{2,10},{6,14},... | collective-permute-start | bytes 786440 | tf_op jit(solution)/shard_map/ppermute | solution.py:388
  120.4 0.9 collective-permute-done.14
  121.3 7.3 %collective-permute-done.3.refs_1_ = bf16[128,1024]{1,0:T(8,128)(2,1)} collective-permute-done((bf16[128,1024]{1,0:T(8,128)(2,1)}, bf16[128,1024]{1,0:T(8,128)(2,1)}, u32[]{:S(2)}, u32[]{:S(2)}) %collective-permute-start.3) | collective-permute-done | bytes 262176 | tf_op jit(solution)/shard_map/ppermute | solution.py:388
  128.6 10.5 %collective-permute-done.4.refs_2_ = bf16[128,1024]{1,0:T(8,128)(2,1)} collective-permute-done((bf16[128,1024]{1,0:T(8,128)(2,1)}, bf16[128,1024]{1,0:T(8,128)(2,1)}, u32[]{:S(2)}, u32[]{:S(2)}) %collective-permute-start.4) | collective-permute-done | bytes 262176 | tf_op jit(solution)/shard_map/ppermute | solution.py:388
  139.2 2.7 %collective-permute-start.11 = (bf16[128,1024]{1,0:T(8,128)(2,1)}, bf16[128,1024]{1,0:T(8,128)(2,1)S(1)}, u32[]{:S(2)}, u32[]{:S(2)}) collective-permute-start(bf16[128,1024]{1,0:T(8,128)(2,1)} %copy-done.3), channel_id=1, source_target_pairs={{0,12},{4,8},{8,4},{12,0},{1,13},{5,9},{9,5},{13,1},{2,14},{6,10},... | collective-permute-start | bytes 786440 | tf_op jit(solution)/shard_map/ppermute | solution.py:388
  142.7 18.9 %collective-permute-done.10.refs_6_ = bf16[128,1024]{1,0:T(8,128)(2,1)S(1)} collective-permute-done((bf16[128,1024]{1,0:T(8,128)(2,1)}, bf16[128,1024]{1,0:T(8,128)(2,1)S(1)}, u32[]{:S(2)}, u32[]{:S(2)}) %collective-permute-start.10) | collective-permute-done | bytes 262176 | tf_op jit(solution)/shard_map/ppermute | solution.py:388
  161.5 0.9 copy-done.2
  162.5 2.0 %summed.1 = (bf16[128,1024]{1,0:T(8,128)(2,1)}, bf16[128,1024]{1,0:T(8,128)(2,1)}) custom-call(bf16[128,1024]{1,0:T(8,128)(2,1)S(1)} %get-tuple-element.28.refs_0_, bf16[128,1024]{1,0:T(8,128)(2,1)} %collective-permute-done.3.refs_1_, bf16[128,1024]{1,0:T(8,128)(2,1)} %collective-permute-done.4.refs_2_, bf16[128,1024]{1,0:T(8,128)(2,1)} %collective-permute-done.5.refs_3_, ...), custom_call_target="tpu_custom_call" | custom-call | bytes 2621440 | tf_op jit(solution)/shard_map/summed/pallas_call | solution.py:507
  164.5 10.1 %joined.1 = (f32[256,4,1536]{2,1,0:T(4,128)}, f32[192,4,1024]{2,1,0:T(4,128)}) custom-call(f32[4,256,1536]{2,1,0:T(8,128)} %get-tuple-element.45.gate_own, bf16[4,256,1536]{2,1,0:T(8,128)(2,1)S(1)} %collective-permute-done.22.gate_share, f32[4,192,1024]{2,1,0:T(8,128)} %get-tuple-element.47.down_own, bf16[4,192,1024]{2,1,0:T(8,128)(2,1)} %collective-permute-done.23.down_share), custom_call_target="tpu_custom_call" | custom-call | bytes 15728640 | tf_op jit(solution)/shard_map/joined/pallas_call | solution.py:527
  (50 shorter events, 5.3 us)
Async XLA Ops:
  3.0 28.9 %collective-permute-start.1 = (bf16[136,1024]{1,0:T(8,128)(2,1)S(1)}, bf16[136,1024]{1,0:T(8,128)(2,1)S(1)}, u32[]{:S(2)}, u32[]{:S(2)}) collective-permute-start(bf16[136,1024]{1,0:T(8,128)(2,1)S(1)} %pad_maximum_fusion.1.refs_0_.refs_4_), channel_id=1, source_target_pairs={{0,8},{4,12},{8,0},{12,4},{1,9},{5,13},{9,1},{13,5},{2,10},{6,14},... | collective-permute-start | bytes 835592 | tf_op jit(solution)/shard_map/ppermute | solution.py:388
  7.1 24.0 %collective-permute-start.7 = (bf16[128,1024]{1,0:T(8,128)(2,1)}, bf16[128,1024]{1,0:T(8,128)(2,1)S(1)}, u32[]{:S(2)}, u32[]{:S(2)}) collective-permute-start(bf16[128,1024]{1,0:T(8,128)(2,1)} %refs_0_.1), channel_id=1, source_target_pairs={{0,8},{4,12},{8,0},{12,4},{1,9},{5,13},{9,1},{13,5},{2,10},{6,14},... | collective-permute-start | bytes 786440 | tf_op jit(solution)/shard_map/ppermute | solution.py:388
  7.2 49.7 %collective-permute-start = (bf16[136,1024]{1,0:T(8,128)(2,1)S(1)}, bf16[136,1024]{1,0:T(8,128)(2,1)S(1)}, u32[]{:S(2)}, u32[]{:S(2)}) collective-permute-start(bf16[136,1024]{1,0:T(8,128)(2,1)S(1)} %pad_maximum_fusion.1.refs_0_.refs_4_), channel_id=1, source_target_pairs={{0,4},{4,0},{8,12},{12,8},{1,5},{5,1},{9,13},{13,9},{2,6},{6,2},{1... | collective-permute-start | bytes 835592 | tf_op jit(solution)/shard_map/ppermute | solution.py:388
  9.0 45.8 %collective-permute-start.6 = (bf16[128,1024]{1,0:T(8,128)(2,1)}, bf16[128,1024]{1,0:T(8,128)(2,1)S(1)}, u32[]{:S(2)}, u32[]{:S(2)}) collective-permute-start(bf16[128,1024]{1,0:T(8,128)(2,1)} %refs_0_.1), channel_id=1, source_target_pairs={{0,4},{4,0},{8,12},{12,8},{1,5},{5,1},{9,13},{13,9},{2,6},{6,2},{1... | collective-permute-start | bytes 786440 | tf_op jit(solution)/shard_map/ppermute | solution.py:388
  10.3 46.1 %collective-permute-start.15 = (bf16[264,1024]{1,0:T(8,128)(2,1)S(1)}, bf16[264,1024]{1,0:T(8,128)(2,1)S(1)}, u32[]{:S(2)}, u32[]{:S(2)}) collective-permute-start(bf16[264,1024]{1,0:T(8,128)(2,1)S(1)} %pad_maximum_fusion), channel_id=1, source_target_pairs={{0,2},{1,3},{2,0},{3,1},{4,6},{5,7},{6,4},{7,5},{8,10},{9,11},{10,... | collective-permute-start | bytes 1622024 | tf_op jit(solution)/shard_map/ppermute | solution.py:395
  31.1 27.5 %collective-permute-start.8 = (bf16[128,1024]{1,0:T(8,128)(2,1)S(1)}, bf16[128,1024]{1,0:T(8,128)(2,1)S(1)}, u32[]{:S(2)}, u32[]{:S(2)}) collective-permute-start(bf16[128,1024]{1,0:T(8,128)(2,1)S(1)} %collective-permute-done.7.refs_2_), channel_id=1, source_target_pairs={{0,4},{4,0},{8,12},{12,8},{1,5},{5,1},{9,13},{13,9},{2,6},{6,2},{1... | collective-permute-start | bytes 786440 | tf_op jit(solution)/shard_map/ppermute | solution.py:388
  31.9 27.2 %collective-permute-start.2 = (bf16[136,1024]{1,0:T(8,128)(2,1)S(1)}, bf16[136,1024]{1,0:T(8,128)(2,1)S(1)}, u32[]{:S(2)}, u32[]{:S(2)}) collective-permute-start(bf16[136,1024]{1,0:T(8,128)(2,1)S(1)} %collective-permute-done.1.refs_2_.refs_6_), channel_id=1, source_target_pairs={{0,4},{4,0},{8,12},{12,8},{1,5},{5,1},{9,13},{13,9},{2,6},{6,2},{1... | collective-permute-start | bytes 835592 | tf_op jit(solution)/shard_map/ppermute | solution.py:388
  54.8 34.7 %collective-permute-start.20 = (bf16[128,1024]{1,0:T(8,128)(2,1)S(1)}, bf16[128,1024]{1,0:T(8,128)(2,1)S(1)}, u32[]{:S(2)}, u32[]{:S(2)}) collective-permute-start(bf16[128,1024]{1,0:T(8,128)(2,1)S(1)} %collective-permute-done.7.refs_2_), channel_id=1, source_target_pairs={{0,2},{1,3},{2,0},{3,1},{4,6},{5,7},{6,4},{7,5},{8,10},{9,11},{10,... | collective-permute-start | bytes 786440 | tf_op jit(solution)/shard_map/ppermute | solution.py:395
  56.4 17.1 %collective-permute-start.19 = (bf16[128,1024]{1,0:T(8,128)(2,1)S(1)}, bf16[128,1024]{1,0:T(8,128)(2,1)S(1)}, u32[]{:S(2)}, u32[]{:S(2)}) collective-permute-start(bf16[128,1024]{1,0:T(8,128)(2,1)S(1)} %collective-permute-done.6.refs_1_), channel_id=1, source_target_pairs={{0,2},{1,3},{2,0},{3,1},{4,6},{5,7},{6,4},{7,5},{8,10},{9,11},{10,... | collective-permute-start | bytes 786440 | tf_op jit(solution)/shard_map/ppermute | solution.py:395
  56.9 17.0 %copy-start = (bf16[128,1024]{1,0:T(8,128)(2,1)S(1)}, bf16[128,1024]{1,0:T(8,128)(2,1)}, u32[]{:S(2)}) copy-start(bf16[128,1024]{1,0:T(8,128)(2,1)} %refs_0_.1) | copy-start | bytes 786436
  56.9 32.6 %collective-permute-start.17 = (bf16[136,1024]{1,0:T(8,128)(2,1)S(1)}, bf16[136,1024]{1,0:T(8,128)(2,1)S(1)}, u32[]{:S(2)}, u32[]{:S(2)}) collective-permute-start(bf16[136,1024]{1,0:T(8,128)(2,1)S(1)} %collective-permute-done.1.refs_2_.refs_6_), channel_id=1, source_target_pairs={{0,2},{1,3},{2,0},{3,1},{4,6},{5,7},{6,4},{7,5},{8,10},{9,11},{10,... | collective-permute-start | bytes 835592 | tf_op jit(solution)/shard_map/ppermute | solution.py:395
  58.5 31.0 %collective-permute-start.16 = (bf16[136,1024]{1,0:T(8,128)(2,1)S(1)}, bf16[136,1024]{1,0:T(8,128)(2,1)S(1)}, u32[]{:S(2)}, u32[]{:S(2)}) collective-permute-start(bf16[136,1024]{1,0:T(8,128)(2,1)S(1)} %collective-permute-done.refs_1_.refs_5_), channel_id=1, source_target_pairs={{0,2},{1,3},{2,0},{3,1},{4,6},{5,7},{6,4},{7,5},{8,10},{9,11},{10,... | collective-permute-start | bytes 835592 | tf_op jit(solution)/shard_map/ppermute | solution.py:395
  59.0 30.6 %collective-permute-start.21 = (bf16[128,1024]{1,0:T(8,128)(2,1)S(1)}, bf16[128,1024]{1,0:T(8,128)(2,1)S(1)}, u32[]{:S(2)}, u32[]{:S(2)}) collective-permute-start(bf16[128,1024]{1,0:T(8,128)(2,1)S(1)} %collective-permute-done.8.refs_3_), channel_id=1, source_target_pairs={{0,2},{1,3},{2,0},{3,1},{4,6},{5,7},{6,4},{7,5},{8,10},{9,11},{10,... | collective-permute-start | bytes 786440 | tf_op jit(solution)/shard_map/ppermute | solution.py:395
  73.5 17.4 %collective-permute-start.18 = (bf16[136,1024]{1,0:T(8,128)(2,1)S(1)}, bf16[136,1024]{1,0:T(8,128)(2,1)S(1)}, u32[]{:S(2)}, u32[]{:S(2)}) collective-permute-start(bf16[136,1024]{1,0:T(8,128)(2,1)S(1)} %collective-permute-done.2.refs_3_.refs_7_), channel_id=1, source_target_pairs={{0,2},{1,3},{2,0},{3,1},{4,6},{5,7},{6,4},{7,5},{8,10},{9,11},{10,... | collective-permute-start | bytes 835592 | tf_op jit(solution)/shard_map/ppermute | solution.py:395
  87.4 0.7 copy-start.3
  88.1 0.7 copy-start.4
  88.8 0.7 copy-start.5
  89.6 20.9 %copy-start.1 = (bf16[128,1024]{1,0:T(8,128)(2,1)}, bf16[128,1024]{1,0:T(8,128)(2,1)S(1)}, u32[]{:S(2)}) copy-start(bf16[128,1024]{1,0:T(8,128)(2,1)S(1)} %get-tuple-element.34.refs_4_) | copy-start | bytes 786436
  90.8 51.0 %copy-start.6 = (s32[128,6]{0,1:T(8,128)S(1)}, s32[128,6]{0,1:T(8,128)}, u32[]{:S(2)}) copy-start(s32[128,6]{0,1:T(8,128)} %param.7) | copy-start | bytes 9220
  110.5 54.0 %collective-permute-start.22 = (bf16[4,256,1536]{2,1,0:T(8,128)(2,1)}, bf16[4,256,1536]{2,1,0:T(8,128)(2,1)S(1)}, u32[]{:S(2)}, u32[]{:S(2)}) collective-permute-start(bf16[4,256,1536]{2,1,0:T(8,128)(2,1)} %get-tuple-element.46), channel_id=1, source_target_pairs={{0,1},{1,0},{2,3},{3,2},{4,5},{5,4},{6,7},{7,6},{8,9},{9,8},{10,11... | collective-permute-start | bytes 9437192 | tf_op jit(solution)/shard_map/ppermute | solution.py:505
  110.5 54.0 %collective-permute-start.23 = (bf16[4,192,1024]{2,1,0:T(8,128)(2,1)}, bf16[4,192,1024]{2,1,0:T(8,128)(2,1)}, u32[]{:S(2)}, u32[]{:S(2)}) collective-permute-start(bf16[4,192,1024]{2,1,0:T(8,128)(2,1)} %get-tuple-element.48), channel_id=1, source_target_pairs={{0,1},{1,0},{2,3},{3,2},{4,5},{5,4},{6,7},{7,6},{8,9},{9,8},{10,11... | collective-permute-start | bytes 4718600 | tf_op jit(solution)/shard_map/ppermute | solution.py:505
  111.0 4.9 %collective-permute-start.12 = (f32[4,128]{1,0:T(4,128)S(1)}, f32[4,128]{1,0:T(4,128)S(1)}, u32[]{:S(2)}, u32[]{:S(2)}) collective-permute-start(f32[4,128]{1,0:T(4,128)S(1)} %get-tuple-element.58), channel_id=1, source_target_pairs={{0,4},{4,0},{8,12},{12,8},{1,5},{5,1},{9,13},{13,9},{2,6},{6,2},{1... | collective-permute-start | bytes 6152 | tf_op jit(solution)/shard_map/ppermute | solution.py:388
  112.6 4.8 %collective-permute-start.13 = (f32[4,128]{1,0:T(4,128)S(1)}, f32[4,128]{1,0:T(4,128)S(1)}, u32[]{:S(2)}, u32[]{:S(2)}) collective-permute-start(f32[4,128]{1,0:T(4,128)S(1)} %get-tuple-element.57), channel_id=1, source_target_pairs={{0,8},{4,12},{8,0},{12,4},{1,9},{5,13},{9,1},{13,5},{2,10},{6,14},... | collective-permute-start | bytes 6152 | tf_op jit(solution)/shard_map/ppermute | solution.py:388
  115.9 5.4 %collective-permute-start.14 = (f32[4,128]{1,0:T(4,128)S(1)}, f32[4,128]{1,0:T(4,128)S(1)}, u32[]{:S(2)}, u32[]{:S(2)}) collective-permute-start(f32[4,128]{1,0:T(4,128)S(1)} %get-tuple-element.56), channel_id=1, source_target_pairs={{0,12},{4,8},{8,4},{12,0},{1,13},{5,9},{9,5},{13,1},{2,14},{6,10},... | collective-permute-start | bytes 6152 | tf_op jit(solution)/shard_map/ppermute | solution.py:388
  115.9 12.7 %collective-permute-start.3 = (bf16[128,1024]{1,0:T(8,128)(2,1)}, bf16[128,1024]{1,0:T(8,128)(2,1)}, u32[]{:S(2)}, u32[]{:S(2)}) collective-permute-start(bf16[128,1024]{1,0:T(8,128)(2,1)} %get-tuple-element.29), channel_id=1, source_target_pairs={{0,4},{4,0},{8,12},{12,8},{1,5},{5,1},{9,13},{13,9},{2,6},{6,2},{1... | collective-permute-start | bytes 786440 | tf_op jit(solution)/shard_map/ppermute | solution.py:388
  117.5 21.7 %collective-permute-start.4 = (bf16[128,1024]{1,0:T(8,128)(2,1)}, bf16[128,1024]{1,0:T(8,128)(2,1)}, u32[]{:S(2)}, u32[]{:S(2)}) collective-permute-start(bf16[128,1024]{1,0:T(8,128)(2,1)} %get-tuple-element.30), channel_id=1, source_target_pairs={{0,8},{4,12},{8,0},{12,4},{1,9},{5,13},{9,1},{13,5},{2,10},{6,14},... | collective-permute-start | bytes 786440 | tf_op jit(solution)/shard_map/ppermute | solution.py:388
  121.3 17.9 %collective-permute-start.5 = (bf16[128,1024]{1,0:T(8,128)(2,1)}, bf16[128,1024]{1,0:T(8,128)(2,1)}, u32[]{:S(2)}, u32[]{:S(2)}) collective-permute-start(bf16[128,1024]{1,0:T(8,128)(2,1)} %get-tuple-element.31), channel_id=1, source_target_pairs={{0,12},{4,8},{8,4},{12,0},{1,13},{5,9},{9,5},{13,1},{2,14},{6,10},... | collective-permute-start | bytes 786440 | tf_op jit(solution)/shard_map/ppermute | solution.py:388
  128.6 14.0 %collective-permute-start.9 = (bf16[128,1024]{1,0:T(8,128)(2,1)}, bf16[128,1024]{1,0:T(8,128)(2,1)S(1)}, u32[]{:S(2)}, u32[]{:S(2)}) collective-permute-start(bf16[128,1024]{1,0:T(8,128)(2,1)} %copy-done.5), channel_id=1, source_target_pairs={{0,4},{4,0},{8,12},{12,8},{1,5},{5,1},{9,13},{13,9},{2,6},{6,2},{1... | collective-permute-start | bytes 786440 | tf_op jit(solution)/shard_map/ppermute | solution.py:388
  139.1 22.4 %collective-permute-start.10 = (bf16[128,1024]{1,0:T(8,128)(2,1)}, bf16[128,1024]{1,0:T(8,128)(2,1)S(1)}, u32[]{:S(2)}, u32[]{:S(2)}) collective-permute-start(bf16[128,1024]{1,0:T(8,128)(2,1)} %copy-done.4), channel_id=1, source_target_pairs={{0,8},{4,12},{8,0},{12,4},{1,9},{5,13},{9,1},{13,5},{2,10},{6,14},... | collective-permute-start | bytes 786440 | tf_op jit(solution)/shard_map/ppermute | solution.py:388
  139.2 22.4 %collective-permute-start.11 = (bf16[128,1024]{1,0:T(8,128)(2,1)}, bf16[128,1024]{1,0:T(8,128)(2,1)S(1)}, u32[]{:S(2)}, u32[]{:S(2)}) collective-permute-start(bf16[128,1024]{1,0:T(8,128)(2,1)} %copy-done.3), channel_id=1, source_target_pairs={{0,12},{4,8},{8,4},{12,0},{1,13},{5,9},{9,5},{13,1},{2,14},{6,10},... | collective-permute-start | bytes 786440 | tf_op jit(solution)/shard_map/ppermute | solution.py:388
  161.5 1.0 copy-start.2

commit v4 on v3

--- a/solution.py
+++ b/solution.py
@@ -169,6 +169,7 @@
 
 
 HALF = 8
+SPLIT = 3
 FWD, BWD, FAR, JOIN = 24, 24, 28, 8
 
 
@@ -263,7 +264,7 @@
     note_refs, refs = refs[:sources], refs[sources:]
     gate_ref, down_ref, pre_ref, output_ref, refs = refs[0], refs[1], refs[2], refs[3], refs[4:]
     part_refs, refs = refs[:sources], refs[sources:]
-    prob_ref, out_grad_ref, pre_grad_ref, cot, total = refs
+    out_grad_ref, pre_grad_ref, cot, total, prob = refs
     e = pl.program_id(0)
     count = cot.shape[0] // sources
 
@@ -272,6 +273,7 @@
         for s in range(sources):
             cot[s * count:(s + 1) * count, :] = cots[s][...]
         total[...] = jnp.zeros_like(total)
+        prob[...] = jnp.zeros_like(prob)
 
     picks, weights = routing_tile(note_refs, info[0] + e, count, cap)
     pick = selected(picks, [1.0] * sources).astype(BF)
@@ -282,14 +284,20 @@
     pre_grad_ref[0] = pre_grad
     slot_prob = jnp.sum(raw_cot * output_ref[0].astype(F32), axis=1, keepdims=True)
     for s in range(sources):
-        prob_ref[s, pl.ds(e, 1), :] = jnp.sum(jnp.where(picks[s], slot_prob, 0.0), axis=0, keepdims=True)
+        prob[s, pl.ds(e, 1), :] = jnp.sum(jnp.where(picks[s], slot_prob, 0.0), axis=0, keepdims=True)
     input_grad = against(pre_grad, gate_ref[0]).astype(BF)
     total[...] += across(pick, input_grad)
 
     @pl.when(e == pl.num_programs(0) - 1)
     def _():
         for s in range(sources):
-            part_refs[s][...] = total[s * count:(s + 1) * count, :].astype(BF)
+            part_refs[s][:count, :] = total[s * count:(s + 1) * count, :].astype(BF)
+            part_refs[s][count:, :] = jnp.zeros((HALF, total.shape[1]), BF)
+            left = prob[s]
+            for i in range(SPLIT):
+                piece = left.astype(BF)
+                part_refs[s][count:, i * count:(i + 1) * count] = piece
+                left = left - piece.astype(F32)
 
 
 def far_gradients(sources, cap, info, *refs):
@@ -343,7 +351,12 @@
 
 
 def summed(sources, *refs):
-    for first, out in ((0, refs[-2]), (sources, refs[-1])):
+    prob_out = refs[-1]
+    for s in range(sources):
+        tile = refs[2 * sources + s][...].astype(F32)
+        count = prob_out.shape[2]
+        prob_out[s] = sum(tile[:, i * count:(i + 1) * count] for i in range(SPLIT))
+    for first, out in ((0, refs[-3]), (sources, refs[-2])):
         total = refs[first][...].astype(F32)
         for ref in refs[first + 1:first + sources]:
             total += ref[...].astype(F32)
@@ -422,7 +435,7 @@
 
     def by_expert(weights):
         moved = with_layout_constraint(weights.swapaxes(0, 1), Layout((0, 1, 2)))
-        return in_hbm(lax.optimization_barrier(moved))
+        return lax.optimization_barrier(moved)
 
     down_rows = by_expert(down_weights)
     gate_rows = by_expert(jnp.where(always, gate_up, jnp.zeros((), BF)))
@@ -449,27 +462,24 @@
         4 * product,
         2 * weight_bytes,
         FWD,
-    )(info, *near_packed, *near_packed, gate_rows, down_rows)
+    )(info, *near_packed, *near_packed, in_hbm(gate_rows), in_hbm(down_rows))
 
     def returned(parts):
         return [to_mate(parts[s], s) for s in range(sources)]
 
     out_arrived = returned(out_parts)
 
-    *grad_parts, prob_part, out_grad, pre_grad = kernel_call(
+    *grad_parts, out_grad, pre_grad = kernel_call(
         functools.partial(own_backward, sources, cap),
         local,
         block_specs + note_specs + weight_specs + [each(slots, pre_width), each(slots, width)],
-        block_specs + [whole(sources, local, count), each(slots, width), each(slots, pre_width)],
-        [block_shape] * sources + [
-            jax.ShapeDtypeStruct((sources, local, count), F32), array(width, BF), array(pre_width, BF)
-        ],
-        [gathered_rows, part_total],
+        [whole(count + HALF, width)] * sources + [each(slots, width), each(slots, pre_width)],
+        [jax.ShapeDtypeStruct((count + HALF, width), BF)] * sources + [array(width, BF), array(pre_width, BF)],
+        [gathered_rows, part_total, pltpu.VMEM((sources, HALF, count), F32)],
         4 * product,
         2 * weight_bytes,
         BWD,
     )(info, *near_cots, *near_packed, gate_rows, down_rows, pre_act, outputs)
-    prob_arrived = [to_mate(prob_part[s], s) for s in range(sources)]
     grad_arrived = returned(grad_parts)
 
     gate_block, down_block = width // replicas, hidden_width // replicas
@@ -485,7 +495,7 @@
         ],
         [
             pltpu.HBM((local, gate_block, pre_width), F32), array(pre_width, BF, gate_block),
-            pltpu.HBM((local, down_block, width), F32), array(width, BF, down_block),
+            array(width, F32, down_block), array(width, BF, down_block),
         ],
         [
             gathered_rows, gathered_rows,
@@ -497,23 +507,25 @@
         3 * weight_bytes,
         FAR,
     )(
-        info, *far_packed, *far_packed, *far_cots, gate_rows, down_rows,
+        info, *far_packed, *far_packed, *far_cots, in_hbm(gate_rows), in_hbm(down_rows),
         inputs, hidden, out_grad, pre_grad,
     )
 
     pair = [(i, i ^ 1) for i in range(replicas)]
     down_theirs, gate_theirs = lax.ppermute(down_share, "replica", pair), lax.ppermute(gate_share, "replica", pair)
 
-    combined, token_gradient = pl.pallas_call(
+    combined, token_gradient, prob_theirs = pl.pallas_call(
         functools.partial(summed, sources),
         name="summed",
         grid=(2,),
-        in_specs=[pl.BlockSpec((count // 2, width), lambda i: (i, 0))] * (2 * sources),
-        out_specs=[pl.BlockSpec((count // 2, width), lambda i: (i, 0))] * 2,
-        out_shape=[block_shape] * 2,
+        in_specs=[pl.BlockSpec((count // 2, width), lambda i: (i, 0))] * (2 * sources)
+        + [pl.BlockSpec((HALF, width), lambda i: (count // HALF, 0))] * sources,
+        out_specs=[pl.BlockSpec((count // 2, width), lambda i: (i, 0))] * 2
+        + [pl.BlockSpec((sources, HALF, count), lambda i: (0, 0, 0))],
+        out_shape=[block_shape] * 2 + [jax.ShapeDtypeStruct((sources, HALF, count), F32)],
         compiler_params=pltpu.CompilerParams(vmem_limit_bytes=JOIN << 20),
         cost_estimate=pl.CostEstimate(flops=0, bytes_accessed=20 * count * width, transcendentals=0),
-    )(*out_arrived, *grad_arrived)
+    )(*out_arrived, *grad_arrived, *grad_arrived)
 
     cuts = 8
     gate_cut, down_cut = gate_block // cuts, down_block // cuts
@@ -536,21 +548,22 @@
         ],
         compiler_params=pltpu.CompilerParams(vmem_limit_bytes=JOIN << 20),
         cost_estimate=pl.CostEstimate(flops=0, bytes_accessed=10 * gate_own.size, transcendentals=0),
-    )(in_hbm(gate_own), gate_theirs, in_hbm(down_own), down_theirs)
+    )(in_hbm(gate_own), gate_theirs, down_own, down_theirs)
 
     choice = expert_ids.T
     prob_gradient = jnp.zeros((top, count), F32)
     for s in range(sources):
         block = jnp.bitwise_xor(home, s) * local
         hit = choice[:, None, :] == (block + jnp.arange(local, dtype=jnp.int32))[None, :, None]
-        prob_gradient = prob_gradient + jnp.sum(jnp.where(hit, prob_arrived[s][None], 0.0), axis=1)
+        theirs = prob_theirs[s, :local]
+        prob_gradient = prob_gradient + jnp.sum(jnp.where(hit, theirs[None], 0.0), axis=1)
     return (combined, token_gradient, prob_gradient.T, gate_up_gradient, down_gradient)
 
 
 def on_device(*args, sources, replicas):
     count, top, local = args[0].shape[0], args[1].shape[1], args[4].shape[1]
     small = sources * min(CAP, count) * local <= 1024 and sources <= 4
-    plain = replicas == 2 * CORES and small and sources & (sources - 1) == 0 and args[0].shape[1] % (128 * replicas) == 0 and count % 128 == 0 and top <= HALF and 2 * count <= args[0].shape[1]
+    plain = replicas == 2 * CORES and small and sources & (sources - 1) == 0 and local <= HALF and SPLIT * count <= args[0].shape[1] and args[0].shape[1] % (128 * replicas) == 0 and count % 128 == 0 and top <= HALF and 2 * count <= args[0].shape[1]
     return (two_chips if plain else general)(*args, sources=sources, replicas=replicas)
 
 

time: 177 us -> 178 us (level)
  starting transfers between devices: 27.9 us -> 24.3 us
  local copies, waits for them, and re-layouts: 10.8 us -> 13.6 us
    ppermute x15 -> x12, starting transfers between devices: 19.4 us -> 15.7 us  [to_mate(): lax.ppermute(values, 'expert', [(i, i ^ mask) for i in range(sources)])]
    unnamed x15 -> x25, local copies, waits for them, and re-layouts: 10.7 us -> 13.5 us
    ppermute x7, waiting for transfers between devices: 1.25 us -> 3.56 us  [to_chip(): return lax.ppermute(values, 'replica', step)]
    ppermute x15 -> x12, waiting for transfers between devices: 57.7 us -> 56.4 us  [to_mate(): lax.ppermute(values, 'expert', [(i, i ^ mask) for i in range(sources)])]
  transfers between devices with their start and end apart: 24 -> 21, of which waited for: 8 -> 6; matrix products, arithmetic and copies ran while one was open for 13% -> 14% of each run, Pallas kernels for 16% -> 16%
where the time goes in v4:
time: 178 us; the launch traced here: 174 us
  waiting for transfers between devices  59.9 us (34%)
  Pallas kernels  57.5 us (32%)
  starting transfers between devices  24.3 us (14%)
  other arithmetic  18.3 us (10%)
  local copies, waits for them, and re-layouts  13.6 us (8%)
    ppermute x12, waiting for transfers between devices, to_mate(): lax.ppermute(values, 'expert', [(i, i ^ mask) for i in range(sources)])  56.4 us
    pallas_call x1, Pallas kernels, two_chips(): kernel_call(functools.partial(far_gradients, sources, cap), local, block_...  19.3 us
    ppermute x12, starting transfers between devices, to_mate(): lax.ppermute(values, 'expert', [(i, i ^ mask) for i in range(sources)])  15.7 us
    transpose x1, other arithmetic, by_expert(): moved = with_layout_constraint(weights.swapaxes(0, 1), Layout((0, 1, 2)))  14.1 us
    pallas_call x1, Pallas kernels, two_chips(): kernel_call(functools.partial(own_backward, sources, cap), local, block_s...  14 us
    unnamed x25, local copies, waits for them, and re-layouts  13.5 us
    pallas_call x1, Pallas kernels, two_chips(): kernel_call(functools.partial(own_forward, sources, cap), local, block_sp...  12 us
    pallas_call x1, Pallas kernels, two_chips(): pl.pallas_call(functools.partial(joined, local), name='joined', grid=(cut...  10.1 us
  transfers between devices with their start and end apart: 21, of which 6 were waited for; matrix products, arithmetic and copies ran while one was open for 14% of the time, Pallas kernels for 16%

profile of v4, /device:TPU:0, one launch (start us, length us, event | category | flops | bytes accessed | tf_op | source)
XLA Modules:
  0.0 174.3 jit_solution(12838172999800041714)
XLA Ops:
  2.0 1.0 pad_maximum_fusion.1.refs_0_.refs_4_
  3.0 4.1 %collective-permute-start.1 = (bf16[136,1024]{1,0:T(8,128)(2,1)S(1)}, bf16[136,1024]{1,0:T(8,128)(2,1)S(1)}, u32[]{:S(2)}, u32[]{:S(2)}) collective-permute-start(bf16[136,1024]{1,0:T(8,128)(2,1)S(1)} %pad_maximum_fusion.1.refs_0_.refs_4_), channel_id=1, source_target_pairs={{0,8},{4,12},{8,0},{12,4},{1,9},{5,13},{9,1},{13,5},{2,10},{6,14},... | collective-permute-start | bytes 835592 | tf_op jit(solution)/shard_map/ppermute | solution.py:401
  7.2 1.8 %collective-permute-start = (bf16[136,1024]{1,0:T(8,128)(2,1)S(1)}, bf16[136,1024]{1,0:T(8,128)(2,1)S(1)}, u32[]{:S(2)}, u32[]{:S(2)}) collective-permute-start(bf16[136,1024]{1,0:T(8,128)(2,1)S(1)} %pad_maximum_fusion.1.refs_0_.refs_4_), channel_id=1, source_target_pairs={{0,4},{4,0},{8,12},{12,8},{1,5},{5,1},{9,13},{13,9},{2,6},{6,2},{1... | collective-permute-start | bytes 835592 | tf_op jit(solution)/shard_map/ppermute | solution.py:401
  9.2 1.1 pad_maximum_fusion
  10.3 1.8 %collective-permute-start.12 = (bf16[264,1024]{1,0:T(8,128)(2,1)S(1)}, bf16[264,1024]{1,0:T(8,128)(2,1)S(1)}, u32[]{:S(2)}, u32[]{:S(2)}) collective-permute-start(bf16[264,1024]{1,0:T(8,128)(2,1)S(1)} %pad_maximum_fusion), channel_id=1, source_target_pairs={{0,2},{1,3},{2,0},{3,1},{4,6},{5,7},{6,4},{7,5},{8,10},{9,11},{10,... | collective-permute-start | bytes 1622024 | tf_op jit(solution)/shard_map/ppermute | solution.py:408
  12.1 19.0 %collective-permute-done.7.refs_2_ = bf16[128,1024]{1,0:T(8,128)(2,1)S(1)} collective-permute-done((bf16[128,1024]{1,0:T(8,128)(2,1)}, bf16[128,1024]{1,0:T(8,128)(2,1)S(1)}, u32[]{:S(2)}, u32[]{:S(2)}) %collective-permute-start.7) | collective-permute-done | bytes 262176 | tf_op jit(solution)/shard_map/ppermute | solution.py:401
  31.1 0.8 collective-permute-start.8
  31.9 1.3 collective-permute-start.2
  33.1 14.1 %fusion.refs_8_.refs_12_ = bf16[4,1024,1536]{2,1,0:T(8,128)(2,1)} fusion(bf16[1024,4,1536]{2,1,0:T(4,128)(2,1)} %param.10, pred[]{:T(512)} %constant.27.clone.1), kind=kLoop, calls=%fused_computation.1 | loop fusion | flops 6291456 | bytes 25165824 | tf_op jit(solution)/shard_map/transpose | solution.py:437
  47.2 7.6 %copy.19 = bf16[768,4,1024]{2,0,1:T(8,128)(2,1)} copy(bf16[768,4,1024]{2,1,0:T(4,128)(2,1)} %param.11) | data formatting | bytes 12582912 | tf_op args[5]
  54.9 1.5 collective-permute-start.17
  57.0 1.6 collective-permute-start.14
  59.1 1.5 collective-permute-start.18
  60.6 12.0 %shard_map.101 = (bf16[128,1024]{1,0:T(8,128)(2,1)S(1)}, bf16[128,1024]{1,0:T(8,128)(2,1)S(1)}, bf16[128,1024]{1,0:T(8,128)(2,1)S(1)}, bf16[128,1024]{1,0:T(8,12...) custom-call(s32[3]{0:T(128)S(1)} %pad_add_fusion.info, ...), custom_call_target="tpu_custom_call" | custom-call | flops 6442450944 | bytes 37748736 | tf_op jit(solution)/shard_map/pallas_call | solution.py:455
  73.3 14.0 %shard_map.102 = (bf16[136,1024]{1,0:T(8,128)(2,1)S(1)}, bf16[136,1024]{1,0:T(8,128)(2,1)}, bf16[136,1024]{1,0:T(8,128)(2,1)}, bf16[136,1024]{1,0:T(8,128)(2,1)}...) custom-call(s32[3]{0:T(128)S(1)} %pad_add_fusion.info, bf16[128,1024]{1,0:T(8,128)(2,1)S(1)} %copy-done, ...), custom_call_target="tpu_custom_call" | custom-call | flops 6442450944 | bytes 37748736 | tf_op jit(solution)/shard_map/pallas_call | solution.py:472
  87.3 3.5 %collective-permute-done.15.refs_3_.refs_7_ = bf16[136,1024]{1,0:T(8,128)(2,1)S(1)} collective-permute-done((bf16[136,1024]{1,0:T(8,128)(2,1)S(1)}, bf16[136,1024]{1,0:T(8,128)(2,1)S(1)}, u32[]{:S(2)}, u32[]{:S(2)}) %collective-permute-start.15) | collective-permute-done | bytes 278560 | tf_op jit(solution)/shard_map/ppermute | solution.py:408
  90.9 19.3 %shard_map.103 = (f32[4,256,1536]{2,1,0:T(8,128)}, bf16[4,256,1536]{2,1,0:T(8,128)(2,1)}, f32[4,192,1024]{2,1,0:T(8,128)S(1)}, bf16[4,192,1024]{2,1,0:T(8,128)(2,1)}) custom-call(s32[3]{0:T(128)S(1)} %pad_add_fusion.info, bf16[136,1024]{1,0:T(8,128)(2,1)S(1)} %slice.24.refs_0_.refs_4_, bf16[136,1024]{1,0:T(8,128)(2,1)S(1)} %collective-permute-done.13.refs_1_.refs_5_, ...), custom_call_target="tpu_custom_call" | custom-call | flops 9663676416 | bytes 56623104 | tf_op jit(solution)/shard_map/pallas_call | solution.py:486
  110.7 1.6 collective-permute-start.3
  112.3 3.3 %collective-permute-start.4 = (bf16[128,1024]{1,0:T(8,128)(2,1)S(1)}, bf16[128,1024]{1,0:T(8,128)(2,1)S(1)}, u32[]{:S(2)}, u32[]{:S(2)}) collective-permute-start(bf16[128,1024]{1,0:T(8,128)(2,1)S(1)} %get-tuple-element.30), channel_id=1, source_target_pairs={{0,8},{4,12},{8,0},{12,4},{1,9},{5,13},{9,1},{13,5},{2,10},{6,14},... | collective-permute-start | bytes 786440 | tf_op jit(solution)/shard_map/ppermute | solution.py:401
  115.6 8.5 %collective-permute-done.3.refs_1_ = bf16[128,1024]{1,0:T(8,128)(2,1)S(1)} collective-permute-done((bf16[128,1024]{1,0:T(8,128)(2,1)S(1)}, bf16[128,1024]{1,0:T(8,128)(2,1)S(1)}, u32[]{:S(2)}, u32[]{:S(2)}) %collective-permute-start.3) | collective-permute-done | bytes 262176 | tf_op jit(solution)/shard_map/ppermute | solution.py:401
  124.1 0.7 copy-done.3
  124.8 9.3 %collective-permute-done.4.refs_2_ = bf16[128,1024]{1,0:T(8,128)(2,1)S(1)} collective-permute-done((bf16[128,1024]{1,0:T(8,128)(2,1)S(1)}, bf16[128,1024]{1,0:T(8,128)(2,1)S(1)}, u32[]{:S(2)}, u32[]{:S(2)}) %collective-permute-start.4) | collective-permute-done | bytes 262176 | tf_op jit(solution)/shard_map/ppermute | solution.py:401
  134.0 0.7 copy-done.5
  135.4 2.6 %collective-permute-start.11 = (bf16[136,1024]{1,0:T(8,128)(2,1)}, bf16[136,1024]{1,0:T(8,128)(2,1)}, u32[]{:S(2)}, u32[]{:S(2)}) collective-permute-start(bf16[136,1024]{1,0:T(8,128)(2,1)} %get-tuple-element.37), channel_id=1, source_target_pairs={{0,12},{4,8},{8,4},{12,0},{1,13},{5,9},{9,5},{13,1},{2,14},{6,10},... | collective-permute-start | bytes 835592 | tf_op jit(solution)/shard_map/ppermute | solution.py:401
  138.1 1.1 collective-permute-done.9.refs_5_.refs_9_
  139.1 18.5 %collective-permute-done.10.refs_6_.refs_10_ = bf16[136,1024]{1,0:T(8,128)(2,1)} collective-permute-done((bf16[136,1024]{1,0:T(8,128)(2,1)}, bf16[136,1024]{1,0:T(8,128)(2,1)}, u32[]{:S(2)}, u32[]{:S(2)}) %collective-permute-start.10) | collective-permute-done | bytes 278560 | tf_op jit(solution)/shard_map/ppermute | solution.py:401
  157.7 0.9 copy-done.2
  158.6 0.9 copy-done.4
  159.6 0.9 copy-done.6
  160.5 0.9 copy-done.8
  161.5 2.1 %summed.1 = (bf16[128,1024]{1,0:T(8,128)(2,1)}, bf16[128,1024]{1,0:T(8,128)(2,1)}, f32[4,8,128]{2,1,0:T(8,128)S(1)}) custom-call(bf16[128,1024]{1,0:T(8,128)(2,1)S(1)} %copy-done.2, bf16[128,1024]{1,0:T(8,128)(2,1)S(1)} %copy-done.4, bf16[128,1024]{1,0:T(8,128)(2,1)S(1)} %copy-done.6, bf16[128,1024]{1,0:T(8,128)(2,1)S(1)} %copy-done.8, ...), custom_call_target="tpu_custom_call" | custom-call | bytes 2621440 | tf_op jit(solution)/shard_map/summed/pallas_call | solution.py:517
  164.3 10.1 %joined.1 = (f32[256,4,1536]{2,1,0:T(4,128)}, f32[192,4,1024]{2,1,0:T(4,128)}) custom-call(f32[4,256,1536]{2,1,0:T(8,128)} %get-tuple-element.45.gate_own, bf16[4,256,1536]{2,1,0:T(8,128)(2,1)} %collective-permute-done.19.gate_share, f32[4,192,1024]{2,1,0:T(8,128)S(1)} %get-tuple-element.47.down_own, bf16[4,192,1024]{2,1,0:T(8,128)(2,1)} %collective-permute-done.20.down_share), custom_call_target="tpu_custom_call" | custom-call | bytes 15728640 | tf_op jit(solution)/shard_map/joined/pallas_call | solution.py:539
  (55 shorter events, 5.3 us)
Async XLA Ops:
  3.0 28.9 %collective-permute-start.1 = (bf16[136,1024]{1,0:T(8,128)(2,1)S(1)}, bf16[136,1024]{1,0:T(8,128)(2,1)S(1)}, u32[]{:S(2)}, u32[]{:S(2)}) collective-permute-start(bf16[136,1024]{1,0:T(8,128)(2,1)S(1)} %pad_maximum_fusion.1.refs_0_.refs_4_), channel_id=1, source_target_pairs={{0,8},{4,12},{8,0},{12,4},{1,9},{5,13},{9,1},{13,5},{2,10},{6,14},... | collective-permute-start | bytes 835592 | tf_op jit(solution)/shard_map/ppermute | solution.py:401
  7.1 24.0 %collective-permute-start.7 = (bf16[128,1024]{1,0:T(8,128)(2,1)}, bf16[128,1024]{1,0:T(8,128)(2,1)S(1)}, u32[]{:S(2)}, u32[]{:S(2)}) collective-permute-start(bf16[128,1024]{1,0:T(8,128)(2,1)} %refs_0_.1), channel_id=1, source_target_pairs={{0,8},{4,12},{8,0},{12,4},{1,9},{5,13},{9,1},{13,5},{2,10},{6,14},... | collective-permute-start | bytes 786440 | tf_op jit(solution)/shard_map/ppermute | solution.py:401
  7.2 49.8 %collective-permute-start = (bf16[136,1024]{1,0:T(8,128)(2,1)S(1)}, bf16[136,1024]{1,0:T(8,128)(2,1)S(1)}, u32[]{:S(2)}, u32[]{:S(2)}) collective-permute-start(bf16[136,1024]{1,0:T(8,128)(2,1)S(1)} %pad_maximum_fusion.1.refs_0_.refs_4_), channel_id=1, source_target_pairs={{0,4},{4,0},{8,12},{12,8},{1,5},{5,1},{9,13},{13,9},{2,6},{6,2},{1... | collective-permute-start | bytes 835592 | tf_op jit(solution)/shard_map/ppermute | solution.py:401
  9.0 45.8 %collective-permute-start.6 = (bf16[128,1024]{1,0:T(8,128)(2,1)}, bf16[128,1024]{1,0:T(8,128)(2,1)S(1)}, u32[]{:S(2)}, u32[]{:S(2)}) collective-permute-start(bf16[128,1024]{1,0:T(8,128)(2,1)} %refs_0_.1), channel_id=1, source_target_pairs={{0,4},{4,0},{8,12},{12,8},{1,5},{5,1},{9,13},{13,9},{2,6},{6,2},{1... | collective-permute-start | bytes 786440 | tf_op jit(solution)/shard_map/ppermute | solution.py:401
  10.3 46.1 %collective-permute-start.12 = (bf16[264,1024]{1,0:T(8,128)(2,1)S(1)}, bf16[264,1024]{1,0:T(8,128)(2,1)S(1)}, u32[]{:S(2)}, u32[]{:S(2)}) collective-permute-start(bf16[264,1024]{1,0:T(8,128)(2,1)S(1)} %pad_maximum_fusion), channel_id=1, source_target_pairs={{0,2},{1,3},{2,0},{3,1},{4,6},{5,7},{6,4},{7,5},{8,10},{9,11},{10,... | collective-permute-start | bytes 1622024 | tf_op jit(solution)/shard_map/ppermute | solution.py:408
  31.1 27.5 %collective-permute-start.8 = (bf16[128,1024]{1,0:T(8,128)(2,1)S(1)}, bf16[128,1024]{1,0:T(8,128)(2,1)S(1)}, u32[]{:S(2)}, u32[]{:S(2)}) collective-permute-start(bf16[128,1024]{1,0:T(8,128)(2,1)S(1)} %collective-permute-done.7.refs_2_), channel_id=1, source_target_pairs={{0,4},{4,0},{8,12},{12,8},{1,5},{5,1},{9,13},{13,9},{2,6},{6,2},{1... | collective-permute-start | bytes 786440 | tf_op jit(solution)/shard_map/ppermute | solution.py:401
  31.9 27.2 %collective-permute-start.2 = (bf16[136,1024]{1,0:T(8,128)(2,1)S(1)}, bf16[136,1024]{1,0:T(8,128)(2,1)S(1)}, u32[]{:S(2)}, u32[]{:S(2)}) collective-permute-start(bf16[136,1024]{1,0:T(8,128)(2,1)S(1)} %collective-permute-done.1.refs_2_.refs_6_), channel_id=1, source_target_pairs={{0,4},{4,0},{8,12},{12,8},{1,5},{5,1},{9,13},{13,9},{2,6},{6,2},{1... | collective-permute-start | bytes 835592 | tf_op jit(solution)/shard_map/ppermute | solution.py:401
  54.9 32.4 %collective-permute-start.17 = (bf16[128,1024]{1,0:T(8,128)(2,1)S(1)}, bf16[128,1024]{1,0:T(8,128)(2,1)S(1)}, u32[]{:S(2)}, u32[]{:S(2)}) collective-permute-start(bf16[128,1024]{1,0:T(8,128)(2,1)S(1)} %collective-permute-done.7.refs_2_), channel_id=1, source_target_pairs={{0,2},{1,3},{2,0},{3,1},{4,6},{5,7},{6,4},{7,5},{8,10},{9,11},{10,... | collective-permute-start | bytes 786440 | tf_op jit(solution)/shard_map/ppermute | solution.py:408
  56.4 16.3 %collective-permute-start.16 = (bf16[128,1024]{1,0:T(8,128)(2,1)S(1)}, bf16[128,1024]{1,0:T(8,128)(2,1)S(1)}, u32[]{:S(2)}, u32[]{:S(2)}) collective-permute-start(bf16[128,1024]{1,0:T(8,128)(2,1)S(1)} %collective-permute-done.6.refs_1_), channel_id=1, source_target_pairs={{0,2},{1,3},{2,0},{3,1},{4,6},{5,7},{6,4},{7,5},{8,10},{9,11},{10,... | collective-permute-start | bytes 786440 | tf_op jit(solution)/shard_map/ppermute | solution.py:408
  56.9 16.3 %slice-start = ((s8[6291456]{0:T(1024)(128)(4,1)}), s8[4194304]{0:T(1024)(128)(4,1)S(1)}, s32[]{:S(2)}) async-start(s8[6291456]{0:T(1024)(128)(4,1)} %bitcast.23), calls=%async_computation | async-start | bytes 8388608
  57.0 16.3 %slice-start.1 = ((s8[6291456]{0:T(1024)(128)(4,1)}), s8[2097152]{0:T(1024)(128)(4,1)S(1)}, s32[]{:S(2)}) async-start(s8[6291456]{0:T(1024)(128)(4,1)} %bitcast.23), calls=%async_computation.1 | async-start | bytes 4194304
  57.0 16.3 %copy-start = (bf16[128,1024]{1,0:T(8,128)(2,1)S(1)}, bf16[128,1024]{1,0:T(8,128)(2,1)}, u32[]{:S(2)}) copy-start(bf16[128,1024]{1,0:T(8,128)(2,1)} %refs_0_.1) | copy-start | bytes 786436
  57.0 30.3 %collective-permute-start.14 = (bf16[136,1024]{1,0:T(8,128)(2,1)S(1)}, bf16[136,1024]{1,0:T(8,128)(2,1)S(1)}, u32[]{:S(2)}, u32[]{:S(2)}) collective-permute-start(bf16[136,1024]{1,0:T(8,128)(2,1)S(1)} %collective-permute-done.1.refs_2_.refs_6_), channel_id=1, source_target_pairs={{0,2},{1,3},{2,0},{3,1},{4,6},{5,7},{6,4},{7,5},{8,10},{9,11},{10,... | collective-permute-start | bytes 835592 | tf_op jit(solution)/shard_map/ppermute | solution.py:408
  58.6 28.7 %collective-permute-start.13 = (bf16[136,1024]{1,0:T(8,128)(2,1)S(1)}, bf16[136,1024]{1,0:T(8,128)(2,1)S(1)}, u32[]{:S(2)}, u32[]{:S(2)}) collective-permute-start(bf16[136,1024]{1,0:T(8,128)(2,1)S(1)} %collective-permute-done.refs_1_.refs_5_), channel_id=1, source_target_pairs={{0,2},{1,3},{2,0},{3,1},{4,6},{5,7},{6,4},{7,5},{8,10},{9,11},{10,... | collective-permute-start | bytes 835592 | tf_op jit(solution)/shard_map/ppermute | solution.py:408
  59.1 28.2 %collective-permute-start.18 = (bf16[128,1024]{1,0:T(8,128)(2,1)S(1)}, bf16[128,1024]{1,0:T(8,128)(2,1)S(1)}, u32[]{:S(2)}, u32[]{:S(2)}) collective-permute-start(bf16[128,1024]{1,0:T(8,128)(2,1)S(1)} %collective-permute-done.8.refs_3_), channel_id=1, source_target_pairs={{0,2},{1,3},{2,0},{3,1},{4,6},{5,7},{6,4},{7,5},{8,10},{9,11},{10,... | collective-permute-start | bytes 786440 | tf_op jit(solution)/shard_map/ppermute | solution.py:408
  72.7 14.6 %copy-start.1 = (bf16[128,1024]{1,0:T(8,128)(2,1)}, bf16[128,1024]{1,0:T(8,128)(2,1)S(1)}, u32[]{:S(2)}) copy-start(bf16[128,1024]{1,0:T(8,128)(2,1)S(1)} %get-tuple-element.28.refs_0_) | copy-start | bytes 786436
  72.7 18.2 %collective-permute-start.15 = (bf16[136,1024]{1,0:T(8,128)(2,1)S(1)}, bf16[136,1024]{1,0:T(8,128)(2,1)S(1)}, u32[]{:S(2)}, u32[]{:S(2)}) collective-permute-start(bf16[136,1024]{1,0:T(8,128)(2,1)S(1)} %collective-permute-done.2.refs_3_.refs_7_), channel_id=1, source_target_pairs={{0,2},{1,3},{2,0},{3,1},{4,6},{5,7},{6,4},{7,5},{8,10},{9,11},{10,... | collective-permute-start | bytes 835592 | tf_op jit(solution)/shard_map/ppermute | solution.py:408
  110.2 53.3 %copy-start.9 = (s32[128,6]{0,1:T(8,128)S(1)}, s32[128,6]{0,1:T(8,128)}, u32[]{:S(2)}) copy-start(s32[128,6]{0,1:T(8,128)} %param.7) | copy-start | bytes 9220
  110.2 54.1 %collective-permute-start.19 = (bf16[4,256,1536]{2,1,0:T(8,128)(2,1)}, bf16[4,256,1536]{2,1,0:T(8,128)(2,1)}, u32[]{:S(2)}, u32[]{:S(2)}) collective-permute-start(bf16[4,256,1536]{2,1,0:T(8,128)(2,1)} %get-tuple-element.46), channel_id=1, source_target_pairs={{0,1},{1,0},{2,3},{3,2},{4,5},{5,4},{6,7},{7,6},{8,9},{9,8},{10,11... | collective-permute-start | bytes 9437192 | tf_op jit(solution)/shard_map/ppermute | solution.py:515
  110.2 54.0 %collective-permute-start.20 = (bf16[4,192,1024]{2,1,0:T(8,128)(2,1)}, bf16[4,192,1024]{2,1,0:T(8,128)(2,1)}, u32[]{:S(2)}, u32[]{:S(2)}) collective-permute-start(bf16[4,192,1024]{2,1,0:T(8,128)(2,1)} %get-tuple-element.48), channel_id=1, source_target_pairs={{0,1},{1,0},{2,3},{3,2},{4,5},{5,4},{6,7},{7,6},{8,9},{9,8},{10,11... | collective-permute-start | bytes 4718600 | tf_op jit(solution)/shard_map/ppermute | solution.py:515
  110.7 13.3 %collective-permute-start.3 = (bf16[128,1024]{1,0:T(8,128)(2,1)S(1)}, bf16[128,1024]{1,0:T(8,128)(2,1)S(1)}, u32[]{:S(2)}, u32[]{:S(2)}) collective-permute-start(bf16[128,1024]{1,0:T(8,128)(2,1)S(1)} %get-tuple-element.29), channel_id=1, source_target_pairs={{0,4},{4,0},{8,12},{12,8},{1,5},{5,1},{9,13},{13,9},{2,6},{6,2},{1... | collective-permute-start | bytes 786440 | tf_op jit(solution)/shard_map/ppermute | solution.py:401
  112.3 21.7 %collective-permute-start.4 = (bf16[128,1024]{1,0:T(8,128)(2,1)S(1)}, bf16[128,1024]{1,0:T(8,128)(2,1)S(1)}, u32[]{:S(2)}, u32[]{:S(2)}) collective-permute-start(bf16[128,1024]{1,0:T(8,128)(2,1)S(1)} %get-tuple-element.30), channel_id=1, source_target_pairs={{0,8},{4,12},{8,0},{12,4},{1,9},{5,13},{9,1},{13,5},{2,10},{6,14},... | collective-permute-start | bytes 786440 | tf_op jit(solution)/shard_map/ppermute | solution.py:401
  115.6 19.2 %collective-permute-start.5 = (bf16[128,1024]{1,0:T(8,128)(2,1)S(1)}, bf16[128,1024]{1,0:T(8,128)(2,1)S(1)}, u32[]{:S(2)}, u32[]{:S(2)}) collective-permute-start(bf16[128,1024]{1,0:T(8,128)(2,1)S(1)} %get-tuple-element.31), channel_id=1, source_target_pairs={{0,12},{4,8},{8,4},{12,0},{1,13},{5,9},{9,5},{13,1},{2,14},{6,10},... | collective-permute-start | bytes 786440 | tf_op jit(solution)/shard_map/ppermute | solution.py:401
  124.1 0.7 copy-start.3
  124.8 14.4 %collective-permute-start.9 = (bf16[136,1024]{1,0:T(8,128)(2,1)}, bf16[136,1024]{1,0:T(8,128)(2,1)}, u32[]{:S(2)}, u32[]{:S(2)}) collective-permute-start(bf16[136,1024]{1,0:T(8,128)(2,1)} %get-tuple-element.35), channel_id=1, source_target_pairs={{0,4},{4,0},{8,12},{12,8},{1,5},{5,1},{9,13},{13,9},{2,6},{6,2},{1... | collective-permute-start | bytes 835592 | tf_op jit(solution)/shard_map/ppermute | solution.py:401
  134.0 0.7 copy-start.5
  134.7 22.9 %collective-permute-start.10 = (bf16[136,1024]{1,0:T(8,128)(2,1)}, bf16[136,1024]{1,0:T(8,128)(2,1)}, u32[]{:S(2)}, u32[]{:S(2)}) collective-permute-start(bf16[136,1024]{1,0:T(8,128)(2,1)} %get-tuple-element.36), channel_id=1, source_target_pairs={{0,8},{4,12},{8,0},{12,4},{1,9},{5,13},{9,1},{13,5},{2,10},{6,14},... | collective-permute-start | bytes 835592 | tf_op jit(solution)/shard_map/ppermute | solution.py:401
  135.4 22.2 %collective-permute-start.11 = (bf16[136,1024]{1,0:T(8,128)(2,1)}, bf16[136,1024]{1,0:T(8,128)(2,1)}, u32[]{:S(2)}, u32[]{:S(2)}) collective-permute-start(bf16[136,1024]{1,0:T(8,128)(2,1)} %get-tuple-element.37), channel_id=1, source_target_pairs={{0,12},{4,8},{8,4},{12,0},{1,13},{5,9},{9,5},{13,1},{2,14},{6,10},... | collective-permute-start | bytes 835592 | tf_op jit(solution)/shard_map/ppermute | solution.py:401
  157.7 1.0 copy-start.2
  158.6 0.9 copy-start.4
  159.6 0.9 copy-start.6
  160.5 0.9 copy-start.8
  (1 other events, 0.7 us)
